TPU v7x, 32 devices: a whole 2x2x4 slice. The times are simulated.
32 devices in a mesh: wide: 8 (over z, y), narrow: 4 (over x, core).
Axes of the slice: x: 2, y: 2, z: 4, core: 2. Of those that a mesh axis runs over, the one named last changes fastest.
Arguments:
- layer_input: bfloat16 [16384, 768], P(('wide', 'narrow')), may hold values from -9 to 9
- layer_cotangent: bfloat16 [16384, 768], P(('wide', 'narrow')), may hold values from -13 to 13
- attend_weight: float32 [3, 768, 768], P(None, 'wide', 'narrow'), may hold values from -0.21875 to 0.21875
- attend_first: float32 [3, 768, 768], P(None, 'wide', 'narrow'), may hold values from -16 to 16
- attend_second: float32 [3, 768, 768], P(None, 'wide', 'narrow'), may hold values from 7.86432 to 31.1296
- output_weight: float32 [768, 768], P('narrow', 'wide'), may hold values from -1.75 to 1.75
- output_first: float32 [768, 768], P('narrow', 'wide'), may hold values from -6 to 6
- output_second: float32 [768, 768], P('narrow', 'wide'), may hold values from 0.147456 to 0.589824
- gated_weight: float32 [2, 768, 2048], P(None, 'wide', 'narrow'), may hold values from -0.21875 to 0.21875
- gated_first: float32 [2, 768, 2048], P(None, 'wide', 'narrow'), may hold values from -6 to 6
- gated_second: float32 [2, 768, 2048], P(None, 'wide', 'narrow'), may hold values from 4.194304 to 16.384
- down_weight: float32 [2048, 768], P('narrow', 'wide'), may hold values from -0.125 to 0.125
- down_first: float32 [2048, 768], P('narrow', 'wide'), may hold values from -16 to 16
- down_second: float32 [2048, 768], P('narrow', 'wide'), may hold values from 7.86432 to 31.1296
- norm_gains: float32 [2, 768], P(None, 'wide'), may hold values from 0.5 to 1.5
- gains_first: float32 [2, 768], P(None, 'wide'), may hold values from -48 to 48
- gains_second: float32 [2, 768], P(None, 'wide'), may hold values from 58.9824 to 235.9296
Outputs:
- layer_output: bfloat16 [16384, 768], P(('wide', 'narrow'))
- input_grad: float32 [16384, 768], P(('wide', 'narrow'))
- grad_norm: float32 [], replicated
- new_attend: float32 [3, 768, 768], P(None, 'wide', 'narrow')
- new_attend_first: float32 [3, 768, 768], P(None, 'wide', 'narrow')
- new_attend_second: float32 [3, 768, 768], P(None, 'wide', 'narrow')
- new_output: float32 [768, 768], P('narrow', 'wide')
- new_output_first: float32 [768, 768], P('narrow', 'wide')
- new_output_second: float32 [768, 768], P('narrow', 'wide')
- new_gated: float32 [2, 768, 2048], P(None, 'wide', 'narrow')
- new_gated_first: float32 [2, 768, 2048], P(None, 'wide', 'narrow')
- new_gated_second: float32 [2, 768, 2048], P(None, 'wide', 'narrow')
- new_down: float32 [2048, 768], P('narrow', 'wide')
- new_down_first: float32 [2048, 768], P('narrow', 'wide')
- new_down_second: float32 [2048, 768], P('narrow', 'wide')
- new_gains: float32 [2, 768], P(None, 'wide')
- new_gains_first: float32 [2, 768], P(None, 'wide')
- new_gains_second: float32 [2, 768], P(None, 'wide')
All inputs are finite; a program needn't handle non-finite values.
Results may differ from a plain program's by a relative error of at most 0.012.
The roundings to bfloat16 on the way count: a program that leaves them out, or rounds other values in their place, can miss the bound.
Values may be sent and summed in bfloat16 or wider, within the bound.
No kernel may reach another device: no remote copies, remote signals or barrier semaphores. Data moves between devices by JAX's collectives and lax.ppermute only.
A program may use at most 128 MiB of HBM per device.

v0:
```python
import functools
import math

import jax
import jax.numpy as jnp
from jax import lax
from jax.experimental import layout
from jax.experimental import pallas as pl
from jax.experimental.pallas import tpu as pltpu
from jax.sharding import PartitionSpec as P

D = 768
HD = 64
FF = 2048
L = 1024
ADAM_STEP = 5

EPSILON = 1e-05
WEIGHT_DECAY = 0.1
AVERAGING = 0.5

LOW = jnp.bfloat16
FULL = jnp.float32
QB = 256
MASKED = -1e30
SMALL = pl.CostEstimate(flops=10**6, bytes_accessed=10**4, transcendentals=0)


def swap(value, axis, bit):
    size = lax.axis_size(axis)
    return lax.ppermute(value, axis, [(i, i ^ bit) for i in range(size)])


def wide_bits():
    top = lax.axis_size("wide").bit_length() - 1
    return [1 << b for b in range(top - 1, -1, -1)]


def block_masks():
    masks = [0]
    for bit in wide_bits():
        masks = masks + [m ^ bit for m in masks]
    return masks


def after(value, *done):
    return lax.optimization_barrier((value, done))[0]


def widen(held, bits):
    for bit in bits:
        held = jnp.concatenate([held, swap(held, "wide", bit)], axis=0)
    return held


def add(kept, received):
    return kept.astype(FULL) + received.astype(FULL)


def narrow_down(held, bits):
    for bit in bits:
        half = held.shape[0] // 2
        held = add(held[:half], swap(held[half:].astype(LOW), "wide", bit))
    return held


def turn(value, cosine, sine, sign):
    width = value.shape[1]
    lane = lax.broadcasted_iota(jnp.int32, value.shape, 1) % HD
    other = jnp.where(
        lane < HD // 2,
        pltpu.roll(value, width - HD // 2, 1),
        pltpu.roll(value, HD // 2, 1),
    )
    reps = width // 128
    return value * jnp.concatenate([cosine] * reps, axis=1) + sign * other * jnp.concatenate(
        [sine] * reps, axis=1
    )


def nn(a, b):
    return lax.dot_general(a, b, (((1,), (0,)), ((), ())), preferred_element_type=FULL)


def nt(a, b):
    return lax.dot_general(a, b, (((1,), (1,)), ((), ())), preferred_element_type=FULL)


def diagonal(scores):
    key = lax.broadcasted_iota(jnp.int32, scores.shape, 0)
    query = lax.broadcasted_iota(jnp.int32, scores.shape, 1)
    return jnp.where(key <= query, scores, MASKED)


def flip(value):
    return value.astype(FULL).T


def attend_kernel(
    rows_ref, qka_ref, qkb_ref, voa_ref, vob_ref, cos_ref, sin_ref,
    q_ref, k_ref, v_ref, ctx_ref, lse_ref, hold,
):
    heads = q_ref.shape[0]
    width = heads * HD
    half = qka_ref.shape[0]

    def project(i, carry):
        rows = pl.ds(pl.multiple_of(i * QB, QB), QB)
        first, second = rows_ref[rows, :half], rows_ref[rows, half:]
        pair = nn(first, qka_ref[...]) + nn(second, qkb_ref[...])
        pair = turn(pair, cos_ref[rows, :], sin_ref[rows, :], 1.0)
        value = nn(first, voa_ref[:, :width]) + nn(second, vob_ref[:, :width])
        for h in range(heads):
            q_ref[h, rows, :] = (pair[:, h * HD : (h + 1) * HD] * (HD**-0.5)).astype(LOW)
            k_ref[h, rows, :] = pair[:, width + h * HD : width + (h + 1) * HD].astype(LOW)
            v_ref[h, rows, :] = value[:, h * HD : (h + 1) * HD].astype(LOW)
        return carry

    lax.fori_loop(0, L // QB, project, 0)

    def head(h, carry):
        turned = flip(v_ref[h]).astype(LOW)
        for i in range(L // QB):
            lo, hi = i * QB, (i + 1) * QB
            query = q_ref[h, lo:hi, :]
            diag = diagonal(nt(k_ref[h, lo:hi, :], query))
            peak = jnp.max(diag, axis=0, keepdims=True)
            if i:
                body = nt(k_ref[h, :lo, :], query)
                peak = jnp.maximum(peak, jnp.max(body, axis=0, keepdims=True))
            weight = jnp.exp(diag - peak)
            total = jnp.sum(weight, axis=0, keepdims=True)
            out = nn(turned[:, lo:hi], weight.astype(LOW))
            if i:
                weight = jnp.exp(body - peak)
                total = total + jnp.sum(weight, axis=0, keepdims=True)
                out = out + nn(turned[:, :lo], weight.astype(LOW))
            lse_ref[h, :, lo:hi] = peak + jnp.log(total)
            hold[h, lo:hi, :] = (out / total).T.astype(LOW)
        return carry

    lax.fori_loop(0, heads, head, 0)
    for h in range(heads):
        ctx_ref[:, h * HD : (h + 1) * HD] = hold[h]


def pinned(array):
    return pltpu.with_memory_space_constraint(array, pltpu.HBM)


def whole(array):
    zero = (0,) * len(array.shape)
    return pl.BlockSpec(array.shape, lambda *_: zero)


def by_head(shape):
    return pl.BlockSpec(shape, lambda h: (h, 0, 0))


def columns(piece, mode=None):
    array, width, j = piece if isinstance(piece, tuple) else (piece, piece.shape[-1], 0)
    lead = (0,) * (array.ndim - 1)
    shape = array.shape[:-1] + (width,)
    return array, pl.BlockSpec(shape, lambda *_: lead + (j,), pipeline_mode=mode)


def width_of(piece):
    return piece[1] if isinstance(piece, tuple) else piece.shape[1]


def attend_forward(rows, qk, vo, cosine, sine):
    heads = width_of(qk[0]) // 2 // HD
    headed = pltpu.HBM((heads, L, HD), LOW)
    outs = (
        headed, headed, headed,
        pltpu.HBM((L, heads * HD), LOW),
        pltpu.HBM((heads, 1, L), FULL),
    )
    args, specs = zip(*[columns(p) for p in (rows, *qk, *vo, cosine, sine)])
    return pl.pallas_call(
        attend_kernel,
        grid=(1,),
        in_specs=list(specs),
        out_specs=[whole(o) for o in outs],
        out_shape=outs,
        scratch_shapes=[pltpu.VMEM((heads, L, HD), LOW)],
        compiler_params=pltpu.CompilerParams(vmem_limit_bytes=24 << 20),
        cost_estimate=SMALL,
        name="attend_forward",
    )(*[pinned(a) for a in args])


def attend_back_kernel(
    q_ref, k_ref, v_ref, lse_ref, dctx_ref, cos_ref, sin_ref,
    dqk_ref, dv_ref, dctx, dqk, dk_sum, dv_sum,
):
    heads = dctx.shape[0]
    h = pl.program_id(0)

    @pl.when(h == 0)
    def _():
        for j in range(heads):
            dctx[j] = dctx_ref[:, j * HD : (j + 1) * HD]

    turned = flip(k_ref[0]).astype(LOW)
    for i in range(L // QB):
        lo, hi = i * QB, (i + 1) * QB
        query, back = q_ref[0, lo:hi, :], dctx[h, lo:hi, :]
        lse = lse_ref[0, :, lo:hi]
        prob = jnp.exp(diagonal(nt(k_ref[0, lo:hi, :], query)) - lse)
        grad = nt(v_ref[0, lo:hi, :], back)
        inner = jnp.sum(prob * grad, axis=0, keepdims=True)
        if i:
            prob_body = jnp.exp(nt(k_ref[0, :lo, :], query) - lse)
            grad_body = nt(v_ref[0, :lo, :], back)
            inner = inner + jnp.sum(prob_body * grad_body, axis=0, keepdims=True)
        score = (prob * (grad - inner)).astype(LOW)
        dv_sum[h, lo:hi, :] = nn(prob.astype(LOW), back)
        dk_sum[h, lo:hi, :] = nn(score, query)
        dquery = nn(turned[:, lo:hi], score)
        if i:
            score = (prob_body * (grad_body - inner)).astype(LOW)
            dv_sum[h, :lo, :] += nn(prob_body.astype(LOW), back)
            dk_sum[h, :lo, :] += nn(score, query)
            dquery = dquery + nn(turned[:, :lo], score)
        dqk[h, lo:hi, :] = (dquery * (HD**-0.5)).T

    def finish(i, carry):
        rows = pl.ds(pl.multiple_of(i * QB, QB), QB)
        pair = jnp.concatenate(
            [dqk[j, rows, :] for j in range(heads)] + [dk_sum[j, rows, :] for j in range(heads)],
            axis=1,
        )
        dqk_ref[rows, :] = turn(pair, cos_ref[rows, :], sin_ref[rows, :], -1.0).astype(LOW)
        dv_ref[rows, :] = jnp.concatenate(
            [dv_sum[j, rows, :] for j in range(heads)], axis=1
        ).astype(LOW)
        return carry

    @pl.when(h == heads - 1)
    def _():
        lax.fori_loop(0, L // QB, finish, 0)


def attend_backward(q, k, v, lse, dctx, cosine, sine):
    heads = q.shape[0]
    outs = (
        jax.ShapeDtypeStruct((L, 2 * heads * HD), LOW),
        jax.ShapeDtypeStruct((L, heads * HD), LOW),
    )
    return pl.pallas_call(
        attend_back_kernel,
        grid=(heads,),
        in_specs=[by_head((1, L, HD))] * 3
        + [by_head((1, 1, L)), whole(dctx), whole(cosine), whole(sine)],
        out_specs=[whole(o) for o in outs],
        out_shape=outs,
        scratch_shapes=[pltpu.VMEM((heads, L, HD), LOW)] + [pltpu.VMEM((heads, L, HD), FULL)] * 3,
        compiler_params=pltpu.CompilerParams(vmem_limit_bytes=24 << 20),
        cost_estimate=SMALL,
        name="attend_backward",
    )(pinned(q), pinned(k), pinned(v), pinned(lse), pinned(dctx), pinned(cosine), pinned(sine))


def held_once(array):
    zero = (0,) * array.ndim
    return pl.BlockSpec(array.shape, lambda *_: zero, pipeline_mode=pl.Buffered(1))


def in_top():
    return pl.program_id(0) < pl.num_programs(0) // 2


def halves(step, width):
    steps = L // step // 2
    return [
        pl.BlockSpec((step, width), lambda i: (jnp.minimum(i, steps - 1), 0)),
        pl.BlockSpec((step, width), lambda i: (jnp.maximum(i - steps, 0), 0)),
    ]


def by_rows(kernel, name, row_args, fixed, outs, sums=0, kept=(), scratch=(), loose=(), step=QB):
    specs, flat = [], []
    for r in row_args:
        if isinstance(r, tuple):
            specs += halves(step, r[0].shape[1])
            flat += r
        else:
            specs.append(pl.BlockSpec((step, r.shape[1]), lambda i: (i, 0)))
            flat.append(r)
    held, held_specs = zip(*[columns(f, pl.Buffered(1)) for f in fixed])
    shapes = [
        (pltpu.HBM if away else jax.ShapeDtypeStruct)((L, w), t) for w, t, away in outs
    ]
    out_specs = [pl.BlockSpec((step, w), lambda i: (i, 0)) for w, _, _ in outs]
    if not outs:
        shapes = [jax.ShapeDtypeStruct((L // 2, D), LOW)] * 2
        out_specs = halves(step, D)
    rows_out = len(shapes)
    shapes += [jax.ShapeDtypeStruct((1, D), FULL)] * sums
    shapes += [pltpu.HBM(shape, LOW) for shape in kept]
    out_specs += [whole(o) for o in shapes[rows_out:]]
    return pl.pallas_call(
        kernel,
        grid=(L // step,),
        in_specs=specs + list(held_specs),
        out_specs=out_specs,
        out_shape=shapes,
        scratch_shapes=list(scratch),
        compiler_params=pltpu.CompilerParams(vmem_limit_bytes=32 << 20),
        cost_estimate=SMALL,
        name=name,
    )(*flat, *[f if f.dtype == FULL or i in loose else pinned(f) for i, f in enumerate(held)])


def rms_scale(residual):
    return lax.rsqrt(jnp.mean(residual * residual, axis=1, keepdims=True) + EPSILON)


def norm_back(scaled, normed, inv):
    return inv * (scaled - normed * jnp.mean(scaled * normed, axis=1, keepdims=True))


def column_sum(sum_ref, value):
    @pl.when(pl.program_id(0) == 0)
    def _():
        sum_ref[...] = jnp.zeros_like(sum_ref)

    sum_ref[...] += jnp.sum(value, axis=0, keepdims=True)


def heads_out(held_ref, refs):
    att_ref, y_ref, x_ref, corner_ref = refs
    half, width = att_ref.shape[0], held_ref.shape[2]

    @pl.when(pl.program_id(0) == 0)
    def _():
        held_ref[0, :half] = att_ref[:, 3 * width :]
        held_ref[0, half:] = y_ref[:, 3 * width :]
        held_ref[1, :half] = x_ref[:, 3 * width :]
        held_ref[1, half:] = corner_ref[:, 3 * width :]


def project_kernel(one_ref, two_ref, att_ref, y_ref, x_ref, corner_ref, out_ref, held_ref):
    heads_out(held_ref, (att_ref, y_ref, x_ref, corner_ref))
    out_ref[...] = (nt(one_ref[...], held_ref[0]) + nt(two_ref[...], held_ref[1])).astype(LOW)


def gate_up(hidden, weights_ref, gate_ref, up_ref, act_ref):
    hid = gate_ref.shape[1]
    gate = nn(hidden, weights_ref[:, :hid])
    up = nn(hidden, weights_ref[:, hid:])
    gate_ref[...] = gate.astype(LOW)
    up_ref[...] = up.astype(LOW)
    act_ref[...] = (gate * jax.nn.sigmoid(gate) * up).astype(LOW)


def enter_kernel(
    rows_ref, mine_ref, theirs_ref, gain_ref, own_ref, y_ref,
    normed_ref, inv_ref, hidden_ref, gate_ref, up_ref, act_ref, weights_ref,
):
    half = own_ref.shape[0]

    @pl.when(pl.program_id(0) == 0)
    def _():
        weights_ref[:half] = own_ref[...]
        weights_ref[half:] = y_ref[...]

    residual = rows_ref[...].astype(FULL) + add(mine_ref[...], theirs_ref[...])
    inv = rms_scale(residual)
    normed = residual * inv
    hidden = (normed * gain_ref[0]).astype(LOW)
    normed_ref[...] = normed.astype(LOW)
    inv_ref[...] = inv
    hidden_ref[...] = hidden
    gate_up(hidden, weights_ref, gate_ref, up_ref, act_ref)


def rest_kernel(
    hidden_ref, act1_ref, x_ref, gate_corner_ref, up_corner_ref,
    low_own_ref, low_y_ref, low_x_ref, low_corner_ref, high_ref,
    gate_ref, up_ref, act_ref, out_ref, weights_ref, down_ref,
):
    half, hid = x_ref.shape[0], gate_ref.shape[1]
    cut = high_ref.shape[2]

    @pl.when(pl.program_id(0) == 0)
    def _():
        weights_ref[:half] = x_ref[...]
        weights_ref[half:, :hid] = gate_corner_ref[...]
        weights_ref[half:, hid:] = up_corner_ref[...]
        down_ref[0, :half, :cut] = low_own_ref[...]
        down_ref[0, half:, :cut] = low_y_ref[...]
        down_ref[1, :half, :cut] = low_x_ref[...]
        down_ref[1, half:, :cut] = low_corner_ref[...]
        down_ref[:, :, cut:] = high_ref[...]

    gate_up(hidden_ref[...], weights_ref, gate_ref, up_ref, act_ref)
    out_ref[...] = (nt(act1_ref[...], down_ref[0]) + nt(act_ref[...], down_ref[1])).astype(LOW)


def turn_kernel(
    normed_ref, mine_ref, theirs_ref, up_rows_ref, gains_ref,
    out_ref, low_ref, sum_ref,
):
    residual = normed_ref[...].astype(FULL) * gains_ref[0] + add(mine_ref[...], theirs_ref[...])
    inv = rms_scale(residual)
    normed = residual * inv
    gain = gains_ref[1]
    out_ref[...] = (normed * gain).astype(LOW)
    upstream = up_rows_ref[...].astype(FULL)
    column_sum(sum_ref, upstream * normed)
    low_ref[...] = norm_back(upstream * gain, normed, inv).astype(LOW)


def back_kernel(low_ref, gate1_ref, up1_ref, gate2_ref, up2_ref, down_ref, gg_ref, ug_ref):
    hid = gate1_ref.shape[1]
    low = low_ref[...]
    for x, gate_ref, up_ref in ((0, gate1_ref, up1_ref), (1, gate2_ref, up2_ref)):
        act_grad = nn(low, down_ref[x])
        gate, up = gate_ref[...].astype(FULL), up_ref[...].astype(FULL)
        sig = jax.nn.sigmoid(gate)
        gg = act_grad * up * (sig * (1.0 + gate * (1.0 - sig)))
        gg_ref[:, x * hid : (x + 1) * hid] = gg.astype(LOW)
        ug_ref[:, x * hid : (x + 1) * hid] = (act_grad * (gate * sig)).astype(LOW)


def mid_kernel(gg_ref, ug_ref, own_ref, other_ref, top_ref, bottom_ref):
    hid = gg_ref.shape[1] // 2
    total = 0.0
    for x, weights_ref in enumerate((own_ref, other_ref)):
        cols = slice(x * hid, (x + 1) * hid)
        total = total + nt(gg_ref[:, cols], weights_ref[:, :hid])
        total = total + nt(ug_ref[:, cols], weights_ref[:, hid:])
    low = total.astype(LOW)

    @pl.when(in_top())
    def _():
        top_ref[...] = low

    @pl.when(jnp.logical_not(in_top()))
    def _():
        bottom_ref[...] = low


def leave_kernel(
    grad_two_ref, mine_top_ref, mine_bottom_ref, theirs_top_ref, theirs_bottom_ref,
    normed_ref, inv_ref, gains_ref, att_ref, y_ref, x_ref, corner_ref,
    low_ref, ctx1_ref, ctx2_ref, sum_ref, held_ref,
):
    heads_out(held_ref, (att_ref, y_ref, x_ref, corner_ref))
    top = add(mine_top_ref[...], theirs_top_ref[...])
    bottom = add(mine_bottom_ref[...], theirs_bottom_ref[...])
    hidden_grad = grad_two_ref[...].astype(FULL) + jnp.where(in_top(), top, bottom)
    normed = normed_ref[...].astype(FULL)
    column_sum(sum_ref, hidden_grad * normed)
    low = norm_back(hidden_grad * gains_ref[0], normed, inv_ref[...]).astype(LOW)
    low_ref[...] = low
    ctx1_ref[...] = nn(low, held_ref[0]).astype(LOW)
    ctx2_ref[...] = nn(low, held_ref[1]).astype(LOW)


def input_kernel(
    qk1_ref, v1_ref, qk2_ref, v2_ref, att_ref, y_ref, x_ref, corner_ref,
    full_ref, low_ref, held_ref,
):
    half, width = att_ref.shape[0], v1_ref.shape[1]
    pair = 2 * width

    @pl.when(pl.program_id(0) == 0)
    def _():
        held_ref[0, :half] = att_ref[:, : pair + width]
        held_ref[0, half:] = y_ref[:, : pair + width]
        held_ref[1, :half] = x_ref[:, : pair + width]
        held_ref[1, half:] = corner_ref[:, : pair + width]

    total = 0.0
    for x, qk_ref, v_ref in ((0, qk1_ref, v1_ref), (1, qk2_ref, v2_ref)):
        total = total + nt(qk_ref[...], held_ref[x, :, :pair])
        total = total + nt(v_ref[...], held_ref[x, :, pair:])
    full_ref[...] = total
    low_ref[...] = total.astype(LOW)


def heads_grad_kernel(rows_ref, grad_ref, qk_ref, v_ref, ctx_ref, out_ref, vo_ref):
    width = v_ref.shape[1]
    rows = flip(rows_ref[...]).astype(LOW)
    out_ref[...] = nn(rows, qk_ref[...]).astype(LOW)
    vo_ref[:, :width] = nn(rows, v_ref[...]).astype(LOW)
    vo_ref[:, width:] = nn(flip(grad_ref[...]).astype(LOW), ctx_ref[...]).astype(LOW)


def heads_grad(rows, grad, dqk, dv, context):
    half, pair = D // 2, dqk.shape[1]
    split = pl.BlockSpec((L, 256), lambda i: (0, i))
    qk, vo = pl.pallas_call(
        heads_grad_kernel,
        grid=(D // 256,),
        in_specs=[split, split] + [held_once(g) for g in (dqk, dv, context)],
        out_specs=[pl.BlockSpec((256, pair), lambda i: (i, 0))] * 2,
        out_shape=[pltpu.HBM((D, pair), LOW)] * 2,
        compiler_params=pltpu.CompilerParams(vmem_limit_bytes=24 << 20),
        cost_estimate=SMALL,
        name="heads_grad",
    )(rows, grad, dqk, dv, context)
    return qk[:half], qk[half:], vo


def in_order(value, mover):
    total = 0.0
    for _ in range(2):
        part = value.astype(LOW)
        total = total + nt(part, mover)
        value = value - part.astype(FULL)
    return total


def finish_kernel(
    core_ref, one_ref, full_ref, out_ref, theirs_ref, mover_ref, *refs
):
    grad_ref, low_ref = refs[-2:]
    mover = mover_ref[...]
    grad = one_ref[...].astype(FULL) + full_ref[...] + theirs_ref[...].astype(FULL)
    grad_ref[...] = in_order(grad, mover)
    low_ref[...] = nt(out_ref[...], mover).astype(LOW)


def finish(part, done, core, grad_one, part_full, layer_output, theirs, mover):
    rows = theirs.shape[0]
    steps = rows // QB
    mine = pl.BlockSpec((QB, D), lambda i, c: (c[0] * steps + part, 0))
    plain = pl.BlockSpec((QB, D), lambda i, c: (part, 0))
    return pl.pallas_call(
        finish_kernel,
        grid_spec=pltpu.PrefetchScalarGridSpec(
            num_scalar_prefetch=1,
            grid=(1,),
            in_specs=[mine, mine, mine, plain, held_once(mover)]
            + [pl.BlockSpec(memory_space=pl.ANY)] * len(done),
            out_specs=[plain, plain],
        ),
        out_shape=[
            jax.ShapeDtypeStruct((rows, D), FULL), jax.ShapeDtypeStruct((rows, D), LOW)
        ],
        input_output_aliases={6 + i: i for i in range(len(done))},
        cost_estimate=pl.CostEstimate(
            flops=4 * 10**9, bytes_accessed=8 << 20, transcendentals=0
        ),
        name="finish",
    )(core, grad_one, pinned(part_full), pinned(layer_output), theirs, mover, *done)


def adam_kernel(clip, rates, *refs):
    me = refs[0][0]
    message = refs[1][...] + refs[2][...]
    att_ref, ffn_ref, down_ref = refs[3:6]
    ins, norm_ref, outs = refs[6:21], refs[21], refs[22:]
    block = ins[12].shape[1]
    gain_sum = message[:, : 2 * D]
    total = message[:, 2 * D : 2 * D + 1] + jnp.sum(gain_sum * gain_sum, axis=1, keepdims=True)
    norm = jnp.sqrt(total)
    norm_ref[...] = norm
    ratio = clip / jnp.maximum(norm, clip)

    def update(p, at, grad):
        rate, decay = rates[p]
        old = [ref[at] for ref in ins[3 * p : 3 * p + 3]]
        for ref, value in zip(
            outs[3 * p : 3 * p + 3], adam_update(*old, grad, ratio, rate, decay)
        ):
            ref[at] = value

    width, hid = att_ref.shape[1] // 4, ffn_ref.shape[1] // 2
    step = 32 if block % 32 == 0 else block

    def some(i, carry):
        rows = pl.ds(pl.multiple_of(i * step, step), step) if step < block else slice(None)
        for k in range(3):
            update(0, (k, rows), att_ref[rows, k * width : (k + 1) * width])
        for k in range(2):
            update(2, (k, rows), ffn_ref[rows, k * hid : (k + 1) * hid])
        update(3, rows, down_ref[rows, :])
        return carry

    if step < block:
        lax.fori_loop(0, block // step, some, 0)
    else:
        some(0, 0)
    update(1, ..., att_ref[:, 3 * width :].T)
    for k in range(2):
        mine = jnp.zeros((1, block), FULL)
        for j in range(D // block):
            start = k * D + j * block
            mine = jnp.where(me == j, gain_sum[:, start : start + block], mine)
        update(4, pl.ds(k, 1), mine)


def adam(me, clip, rates, grads, params):
    flat = [array for group in params for array in group]
    outs = [jax.ShapeDtypeStruct((1, 1), FULL)]
    outs += [jax.ShapeDtypeStruct(w.shape, FULL) for w in flat]
    vmem = pl.BlockSpec(memory_space=pltpu.VMEM)
    norm, *made = pl.pallas_call(
        functools.partial(adam_kernel, clip, rates),
        in_specs=[pl.BlockSpec(memory_space=pltpu.SMEM)] + [vmem] * (len(grads) + len(flat)),
        out_specs=[vmem] * len(outs),
        out_shape=outs,
        name="adam",
    )(me, *grads, *[pltpu.with_memory_space_constraint(f, pltpu.VMEM) for f in flat])
    return norm[0, 0], [made[i : i + 3] for i in range(0, len(made), 3)]


def rope_tables(place):
    half = HD // 2
    lane = jnp.arange(128) % HD
    freq = jnp.exp(-jnp.log(10000.0) * (lane % half).astype(FULL) / half)
    angle = place[:, None] * freq[None, :]
    return jnp.cos(angle), jnp.where(lane < half, -1.0, 1.0)[None, :] * jnp.sin(angle)


def adam_update(weight, first, second, grad, ratio, rate, decay):
    clipped = grad * ratio
    first_new = AVERAGING * first + (1.0 - AVERAGING) * clipped
    second_new = AVERAGING * second + (1.0 - AVERAGING) * clipped * clipped
    correction = 1.0 - AVERAGING**ADAM_STEP
    step = first_new / correction / (jnp.sqrt(second_new / correction) + 1e-08)
    return (weight - rate * (step + decay * weight), first_new, second_new)


def tn(rows, grads):
    out = lax.dot_general(rows, grads, (((0,), (0,)), ((), ())), preferred_element_type=FULL)
    return layout.with_layout_constraint(out.astype(LOW), layout.Layout((0, 1)))


def per_device(
    layer_input, layer_cotangent,
    attend_weight, attend_first, attend_second,
    output_weight, output_first, output_second,
    gated_weight, gated_first, gated_second,
    down_weight, down_first, down_second,
    norm_gains, gains_first, gains_second,
):
    rows = layer_input.shape[0]
    wide = lax.axis_size("wide")
    block = D // wide
    me = lax.axis_index("wide")
    narrow = lax.axis_index("narrow")
    core = narrow % 2
    cols = attend_weight.shape[2]

    bits = wide_bits()
    near = bits[:-1]
    half = D // 2
    hid = down_weight.shape[0]

    bits = wide_bits()
    near = bits[:-1]
    half = D // 2
    hid = down_weight.shape[0]
    pair = 2 * cols

    attend_low = attend_weight.astype(LOW)
    att = jnp.concatenate(
        [attend_low[0], attend_low[1], attend_low[2], output_weight.T.astype(LOW)], axis=1
    )
    cut = hid // 2
    down_t = down_weight.T
    ffn = jnp.concatenate([gated_weight[0], gated_weight[1], down_t[:, :cut]], axis=1).astype(LOW)
    down = down_t[:, cut:].astype(LOW)

    order = me ^ jnp.array(block_masks(), jnp.int32)
    source = (order[:, None] * block + jnp.arange(block)[None, :]).reshape(1, D)
    mover = (lax.broadcasted_iota(jnp.int32, (D, D), 0) == source).astype(LOW)
    mover = lax.optimization_barrier(mover)

    def both_halves(mine, theirs):
        first = core == 0
        return jnp.concatenate(
            [jnp.where(first, mine, theirs), jnp.where(first, theirs, mine)], axis=0
        )

    def own_rows(value):
        return lax.dynamic_slice_in_dim(value, core * rows, rows, axis=0)

    first = widen(att, near[:1])
    gains = widen(after(norm_gains, att).astype(LOW).astype(FULL)[None], bits[:1])
    first, down, gains = lax.optimization_barrier((first, down, gains))
    gains = widen(gains, bits[1:-1])
    att = widen(first, near[1:])
    down_y = swap(down, "wide", 1)
    down_x = swap(down, "narrow", 2)
    both = jnp.concatenate([layer_input, layer_cotangent], axis=0)
    moved = jnp.dot(both, mover, preferred_element_type=FULL).astype(LOW)
    place = jnp.arange(L, dtype=FULL)
    att, down_y, down_x, gains, moved, place = lax.optimization_barrier(
        (att, down_y, down_x, gains, moved, place)
    )
    att_y = swap(att, "wide", 1)
    att_x = swap(att, "narrow", 2)
    ffn = widen(after(ffn, att), near[:1])
    gains = widen(gains, bits[-1:])
    inputs = both_halves(moved[:rows], swap(moved[:rows], "narrow", 1))
    moved_up = moved[rows:]
    cosine, sine = rope_tables(place)
    inputs, att, att_y, att_x, ffn, gains, cosine, sine = lax.optimization_barrier(
        (inputs, att, att_y, att_x, ffn, gains, cosine, sine)
    )
    gains = gains.transpose(1, 0, 2).reshape(2, 1, D)
    down_corner = swap(down_y, "narrow", 2)
    qk_corner = swap(att_y[:, :pair], "narrow", 2)
    vo_corner = swap(att_x[:, pair:], "wide", 1)
    ffn = widen(ffn, near[1:])
    qk = [[(att, pair, 0), (att_y, pair, 0)], [(att_x, pair, 0), qk_corner]]
    vo = [[(att, pair, 1), (att_y, pair, 1)], [(att_x, pair, 1), vo_corner]]
    saved = [attend_forward(inputs, qk[0], vo[0], cosine, sine)]
    second_in, qk_corner, vo_corner, ffn, down_corner = lax.optimization_barrier(
        (after(inputs, saved[0][3]), qk_corner, vo_corner, ffn, down_corner)
    )
    other_up = swap(after(moved_up, second_in), "narrow", 1)
    down = jnp.stack([down, down_y, down_x, down_corner])[:, None]
    for bit in near[:1]:
        down = jnp.concatenate([down, swap(down, "wide", bit)], axis=1)
    corner = jnp.concatenate([qk_corner, vo_corner], axis=1)
    qk[1][1], vo[1][1] = (corner, pair, 0), (corner, pair, 1)
    ffn_y = swap(ffn, "wide", 1)
    ffn_x = swap(ffn, "narrow", 2)
    saved.append(attend_forward(second_in, qk[1], vo[1], cosine, sine))
    context = [s[3] for s in saved]
    att_out = [att, att_y, att_x, corner]
    held = [pltpu.VMEM((2, D, cols), LOW)]
    low_d, full_d = (D, LOW, False), (D, FULL, True)
    (attn_part,) = by_rows(
        project_kernel, "project", context, att_out, [low_d], scratch=held
    )
    ffn_y, ffn_x, attn_part, down = lax.optimization_barrier((ffn_y, ffn_x, attn_part, down))
    attn_other = swap(attn_part, "narrow", 1)
    down_far = [swap(down, "wide", bit) for bit in near[1:2]]
    gate_corner = swap(ffn_y[:, :hid], "narrow", 2)
    up_corner = swap(ffn_x[:, hid:], "wide", 1)
    flow = [(hid, LOW, True), (hid, LOW, True), (hid, LOW, False)]
    normed_one, inv_one, hidden_low, gate1, up1, act1, gu_own = by_rows(
        enter_kernel, "enter", [pinned(inputs), attn_part, attn_other],
        [gains, (ffn, 2 * hid, 0), (ffn_y, 2 * hid, 0)],
        [(D, LOW, True), (1, FULL, True), low_d] + flow, kept=[(D, 2 * hid)],
    )
    hidden_low, down, down_far = lax.optimization_barrier((hidden_low, down, down_far))
    moved_up, other_up, hidden_low = lax.optimization_barrier((moved_up, other_up, hidden_low))
    upstream = both_halves(moved_up, other_up)
    down = jnp.concatenate([down, *down_far], axis=1)
    for bit in near[2:]:
        down = jnp.concatenate([down, swap(down, "wide", bit)], axis=1)
    down = down.reshape(2, D, hid - cut)
    last_cols = 2 * hid // cut
    gate2, up2, act2, ffn_part, gu_other, down_all = by_rows(
        rest_kernel, "rest", [after(hidden_low, upstream), act1],
        [
            (ffn_x, 2 * hid, 0), gate_corner, (up_corner, hid, 0),
            (ffn, cut, last_cols), (ffn_y, cut, last_cols), (ffn_x, cut, last_cols),
            (up_corner, cut, hid // cut), down,
        ],
        flow + [low_d], kept=[(D, 2 * hid), (2, D, hid)], loose=(1, 2, 6),
    )
    ffn_other = swap(ffn_part, "narrow", 1)

    layer_output, grad_two_low, gain_two_grad = by_rows(
        turn_kernel, "turn", [pinned(normed_one), ffn_part, ffn_other, pinned(upstream)],
        [gains], [(D, LOW, True), low_d], sums=1,
    )
    down_send = tn(grad_two_low, act2)
    down_x = swap(down_send, "narrow", 2)
    wide_flow = (2 * hid, LOW, False)
    saves = [pinned(r) for r in (gate1, up1, gate2, up2)]
    gg, ug = by_rows(
        back_kernel, "back",
        [after(grad_two_low, down_send), *saves], [down_all], [wide_flow, wide_flow],
    )
    gate_send = tn(hidden_low[:, half:], gg)
    up_send = tn(hidden_low[:, half:], ug)
    gate_y = swap(gate_send, "wide", 1)
    up_y = swap(up_send, "wide", 1)
    mid_part = by_rows(
        mid_kernel, "mid", [after(gg, gate_send, up_send), ug], [gu_own, gu_other], []
    )
    mid_other = [swap(part, "narrow", 1) for part in mid_part]
    down_own = tn(grad_two_low, act1)
    gate_own = tn(hidden_low[:, :half], gg)
    up_own = tn(hidden_low[:, :half], ug)
    mid_part, mid_other, down_own, gate_own, up_own, down_x = lax.optimization_barrier(
        (mid_part, mid_other, down_own, gate_own, up_own, down_x)
    )
    grad_one_low, dctx1, dctx2, gain_one_grad = by_rows(
        leave_kernel, "leave",
        [grad_two_low, tuple(mid_part), tuple(mid_other), pinned(normed_one), pinned(inv_one)],
        [gains, *att_out], [low_d, (cols, LOW, True), (cols, LOW, True)],
        sums=1, scratch=held,
    )

    q, k, v, _, lse = saved[1]
    dqk2, dv2 = attend_backward(q, k, v, lse, dctx2, cosine, sine)
    down_x, gate_y, dqk2, dv2 = lax.optimization_barrier((down_x, gate_y, dqk2, dv2))
    down_sum, gate_sum = add(down_own, down_x), add(gate_own, gate_y)
    down_y = swap(down_sum[half:].astype(LOW), "wide", 1)
    gate_far = gate_sum[:, hid:].astype(LOW)
    gate_x = swap(gate_far, "narrow", 2)
    qk_near2, qk_send2, vo_send = heads_grad(inputs, grad_one_low, after(dqk2, gate_far), dv2, context[1])
    vo_x = swap(vo_send, "narrow", 2)
    qk_y2 = swap(qk_send2, "wide", 1)
    back = near[::-1]
    q, k, v, _, lse = saved[0]
    dqk1, dv1 = attend_backward(q, k, v, lse, after(dctx1, vo_send, qk_send2), cosine, sine)
    dqk1, dv1, up_y, down_y, qk_y2, gate_x = lax.optimization_barrier(
        (dqk1, dv1, up_y, down_y, qk_y2, gate_x)
    )
    early = narrow_down(add(down_sum[:half], down_y), back[:1])
    up_sum = add(up_own, up_y)
    up_x = swap(up_sum[:, hid:].astype(LOW), "narrow", 2)
    qk_near1, qk_send1, vo_own = heads_grad(inputs, grad_one_low, dqk1, dv1, context[0])
    qk_y1 = swap(qk_send1, "wide", 1)
    qk_far = add(qk_near2, qk_y2).astype(LOW)
    qk_x = swap(qk_far, "narrow", 2)
    vo_sum = add(vo_own, vo_x)
    vo_far = vo_sum[half:].astype(LOW)
    vo_y = swap(vo_far, "wide", 1)
    late = jnp.concatenate([add(gate_sum[:, :hid], gate_x), add(up_sum[:, :hid], up_x)], axis=1)
    early_red = narrow_down(early, back[1:])
    dqk1, vo_sum = lax.optimization_barrier((dqk1, vo_sum))
    part_full, part_low = by_rows(
        input_kernel, "inputs", [dqk1, dv1, dqk2, dv2],
        att_out, [full_d, low_d], step=128,
        scratch=[pltpu.VMEM((2, D, 3 * cols), LOW)],
    )
    late = narrow_down(late, back[:1])
    theirs = lax.dynamic_slice_in_dim(part_low, (1 - core) * rows, rows, axis=0)
    theirs = swap(theirs, "narrow", 1)
    qk_sum = add(qk_near1, qk_y1)
    last = jnp.concatenate([add(qk_sum, qk_x), add(vo_sum[:half], vo_y)], axis=1)
    gain_grads = jnp.concatenate([gain_one_grad, gain_two_grad], axis=0)
    gain_low = gain_grads.astype(LOW)
    gain_rest = (gain_grads - gain_low.astype(FULL)).astype(LOW)
    gain_grads = nt(jnp.concatenate([gain_low, gain_rest], axis=0), mover)
    gain_grads = gain_grads[:2] + gain_grads[2:]
    last, early_red, late, gain_grads, part_full = lax.optimization_barrier(
        (last, early_red, late, gain_grads, part_full)
    )
    last = narrow_down(last, back[:1])
    late_red = narrow_down(late, back[1:])
    early_square = jnp.sum(early_red * early_red) + jnp.sum(late_red * late_red)
    att_red = narrow_down(last, back[1:])

    square = jnp.full((1, 128), early_square + jnp.sum(att_red * att_red), FULL)
    square = square + swap(square, "narrow", 1)
    message = jnp.concatenate([gain_grads.reshape(1, 2 * D), square], axis=1)
    message = message + swap(message, "narrow", 2)
    which, done = jnp.full((1,), core, jnp.int32), ()
    theirs = after(theirs, message)
    for part in range(rows // QB):
        done = finish(part, done, which, grad_one_low, part_full, layer_output, theirs, mover)
    input_grad, layer_output = done
    for bit in bits[::-1][:-1]:
        message = message + swap(message, "wide", bit)
    received = swap(message, "wide", bits[0])
    all_tokens = rows * wide * lax.axis_size("narrow")
    clip = 0.02 * math.sqrt(all_tokens * (4 * D * D + 3 * D * FF + 2 * D))
    grad_norm, (new_attend, new_output, new_gated, new_down, new_gains) = adam(
        jnp.full((1,), me, jnp.int32),
        clip,
        (
            (D ** (-0.5), WEIGHT_DECAY),
            (max(D // 64, 1) ** (-0.5), WEIGHT_DECAY),
            (D ** (-0.5), WEIGHT_DECAY),
            (FF ** (-0.5), WEIGHT_DECAY),
            (0.4, 0.0),
        ),
        (message, received, att_red, late_red, early_red),
        (
            (attend_weight, attend_first, attend_second),
            (output_weight, output_first, output_second),
            (gated_weight, gated_first, gated_second),
            (down_weight.T, down_first.T, down_second.T),
            (norm_gains, gains_first, gains_second),
        ),
    )
    new_down = [value.T for value in new_down]
    return (
        layer_output, input_grad, grad_norm,
        *new_attend, *new_output, *new_gated, *new_down, *new_gains,
    )


def solution(mesh):
    rows = P(("wide", "narrow"), None)
    stacked = P(None, "wide", "narrow")
    turned = P("narrow", "wide")
    gains = P(None, "wide")
    params = (stacked,) * 3 + (turned,) * 3 + (stacked,) * 3 + (turned,) * 3 + (gains,) * 3
    return jax.shard_map(
        per_device,
        mesh=mesh,
        in_specs=(rows, rows) + params,
        out_specs=(rows, rows, P()) + params,
        check_vma=False,
    )
```

profile of v0, /device:TPU:0, one launch (start us, length us, event | category | flops | bytes accessed | tf_op | source)
XLA Modules:
  0.0 255.5 jit_solution(14908113839702265873)
XLA Ops:
  2.8 4.1 %collective-permute-start = (bf16[96,768]{1,0:T(8,128)(2,1)S(1)}, bf16[96,768]{1,0:T(8,128)(2,1)S(1)}, u32[]{:S(2)}, u32[]{:S(2)}) collective-permute-start(bf16[96,768]{1,0:T(8,128)(2,1)S(1)} %pad_maximum_fusion.11), channel_id=1, source_target_pairs={{0,16},{4,20},{8,24},{12,28},{16,0},{20,4},{24,8},{28,12},{1,17},{... | collective-permute-start | bytes 442376 | tf_op jit(solution)/shard_map/ppermute | solution.py:31
  29.4 3.5 %fusion.11 = (f32[1024,128]{1,0:T(8,128)}, f32[1024,128]{1,0:T(8,128)}) fusion(f32[128]{0:T(128)S(1)} %get-tuple-element.298, f32[128]{0:T(128)S(1)} %get-tuple-element.299, f32[1024]{0:T(1024)S(1)} %iota.22), kind=kLoop, calls=%fused_computation.50 | loop fusion | flops 262144 | bytes 1053696 | tf_op jit(solution)/shard_map/mul | solution.py:618
  32.9 5.6 %collective-permute-done.10 = f32[4,2,96]{2,1,0:T(2,128)S(1)} collective-permute-done((f32[4,2,96]{2,1,0:T(2,128)S(1)}, f32[4,2,96]{2,1,0:T(2,128)S(1)}, u32[]{:S(2)}, u32[]{:S(2)}) %collective-permute-start.10) | collective-permute-done | bytes 3104 | tf_op jit(solution)/shard_map/ppermute | solution.py:31
  46.2 11.6 %attend_forward.2 = (bf16[3,1024,64]{2,1,0:T(8,128)(2,1)}, bf16[3,1024,64]{2,1,0:T(8,128)(2,1)}, bf16[3,1024,64]{2,1,0:T(8,128)(2,1)}, bf16[1024,192]{1,0:T(8,128)(2,1)}, f32[3,1,1024]{2,1,0:T(1,128)}) custom-call(bf16[1024,768]{1,0:T(8,128)(2,1)} %pad_maximum_fusion.rows_ref, bf16[384,768]{1,0:T(8,128)(2,1)} %copy-done.20, bf16[384,768]{1,0:T(8,128)(2,1)} %copy-done.21, ...), custom_call_target="tpu_custom_call" | custom-call | flops 1000000 | bytes 10000 | tf_op jit(solution)/shard_map/attend_forward/pallas_call | solution.py:180
  60.1 3.4 %collective-permute-start.17 = (bf16[4,1,96,256]{3,2,0,1:T(8,128)(2,1)S(1)}, bf16[4,1,96,256]{3,2,0,1:T(8,128)(2,1)S(1)}, u32[]{:S(2)}, u32[]{:S(2)}) collective-permute-start(bf16[4,1,96,256]{3,2,0,1:T(8,128)(2,1)S(1)} %maximum_bitcast_fusion), channel_id=1, source_target_pairs={{0,16},{4,20},{8,24},{12,28},{16,0},{20,4},{24,8},{28,12},{1,17},{... | collective-permute-start | bytes 589832 | tf_op jit(solution)/shard_map/ppermute | solution.py:31
  64.4 11.6 %attend_forward.3 = (bf16[3,1024,64]{2,1,0:T(8,128)(2,1)}, bf16[3,1024,64]{2,1,0:T(8,128)(2,1)}, bf16[3,1024,64]{2,1,0:T(8,128)(2,1)}, bf16[1024,192]{1,0:T(8,128)(2,1)}, f32[3,1,1024]{2,1,0:T(1,128)}) custom-call(bf16[1024,768]{1,0:T(8,128)(2,1)} %pad_maximum_fusion.rows_ref, bf16[384,768]{1,0:T(8,128)(2,1)} %copy-done.22, bf16[384,768]{1,0:T(8,128)(2,1)} %copy-done.23, ...), custom_call_target="tpu_custom_call" | custom-call | flops 1000000 | bytes 10000 | tf_op jit(solution)/shard_map/attend_forward/pallas_call | solution.py:180
  77.1 3.5 %project.1.mine_ref = bf16[1024,768]{1,0:T(8,128)(2,1)S(1)} custom-call(bf16[1024,192]{1,0:T(8,128)(2,1)S(1)} %copy-done.2, bf16[1024,192]{1,0:T(8,128)(2,1)S(1)} %copy-done.3, bf16[384,768]{1,0:T(8,128)(2,1)} %copy-done.20, bf16[384,768]{1,0:T(8,128)(2,1)} %copy-done.21, bf16[384,768]{1,0:T(8,128)(2,1)} %copy-done.22, bf16[384,768]{1,0:T(8,128)(2,1)} %copy-done.23), custom_call_target="tpu_custom_call" | custom-call | flops 1000000 | bytes 10000 | tf_op jit(solution)/shard_map/project/pallas_call | solution.py:303
  86.4 6.5 %enter.1 = (bf16[1024,768]{1,0:T(8,128)(2,1)}, f32[1024,1]{1,0:T(8,128)}, bf16[1024,768]{1,0:T(8,128)(2,1)S(1)}, bf16[1024,512]{1,0:T(8,128)(2,1)}, bf16[1024,51...) custom-call(bf16[1024,768]{1,0:T(8,128)(2,1)} %pad_maximum_fusion.rows_ref, ...), custom_call_target="tpu_custom_call" | custom-call | flops 1000000 | bytes 10000 | tf_op jit(solution)/shard_map/enter/pallas_call | solution.py:303
  98.9 8.3 %rest.1 = (bf16[1024,512]{1,0:T(8,128)(2,1)}, bf16[1024,512]{1,0:T(8,128)(2,1)}, bf16[1024,512]{1,0:T(8,128)(2,1)S(1)}, bf16[1024,768]{1,0:T(8,128)(2,1)S(1)}, b...) custom-call(bf16[1024,768]{1,0:T(8,128)(2,1)S(1)} %get-tuple-element.186.hidden_ref, ...), custom_call_target="tpu_custom_call" | custom-call | flops 1000000 | bytes 10000 | tf_op jit(solution)/shard_map/rest/pallas_call | solution.py:303
  110.6 4.7 %turn.1 = (bf16[1024,768]{1,0:T(8,128)(2,1)}, bf16[1024,768]{1,0:T(8,128)(2,1)S(1)}, f32[1,768]{1,0:T(1,128)S(1)}) custom-call(bf16[1024,768]{1,0:T(8,128)(2,1)} %get-tuple-element.178.normed_ref, bf16[1024,768]{1,0:T(8,128)(2,1)S(1)} %get-tuple-element.191.mine_ref, bf16[1024,768]{1,0:T(8,128)(2,1)S(1)} %collective-permute-done.23.theirs_ref, ...), custom_call_target="tpu_custom_call" | custom-call | flops 1000000 | bytes 10000 | tf_op jit(solution)/shard_map/turn/pallas_call | solution.py:303
  117.0 5.4 %back.1 = (bf16[1024,1024]{1,0:T(8,128)(2,1)S(1)}, bf16[1024,1024]{1,0:T(8,128)(2,1)S(1)}) custom-call(bf16[1024,768]{1,0:T(8,128)(2,1)S(1)} %get-tuple-element.194.low_ref.grad_two_ref, bf16[1024,512]{1,0:T(8,128)(2,1)} %get-tuple-element.195.gate1_ref, bf16[1024,512]{1,0:T(8,128)(2,1)} %get-tuple-element.196.up1_ref, ...), custom_call_target="tpu_custom_call" | custom-call | flops 1000000 | bytes 10000 | tf_op jit(solution)/shard_map/back/pallas_call | solution.py:303
  125.4 6.1 %mid.1 = (bf16[512,768]{1,0:T(8,128)(2,1)S(1)}, bf16[512,768]{1,0:T(8,128)(2,1)S(1)}) custom-call(bf16[1024,1024]{1,0:T(8,128)(2,1)S(1)} %get-tuple-element.202.gg_ref, bf16[1024,1024]{1,0:T(8,128)(2,1)S(1)} %get-tuple-element.201.ug_ref, bf16[768,1024]{1,0:T(8,128)(2,1)} %get-tuple-element.203.own_ref, bf16[768,1024]{1,0:T(8,128)(2,1)} %get-tuple-element.204.other_ref), custom_call_target="tpu_custom_call" | custom-call | flops 1000000 | bytes 10000 | tf_op jit(solution)/shard_map/mid/pallas_call | solution.py:303
  136.3 7.3 %leave.1 = (bf16[1024,768]{1,0:T(8,128)(2,1)S(1)}, bf16[1024,192]{1,0:T(8,128)(2,1)}, bf16[1024,192]{1,0:T(8,128)(2,1)}, f32[1,768]{1,0:T(1,128)S(1)}) custom-call(bf16[1024,768]{1,0:T(8,128)(2,1)S(1)} %get-tuple-element.194.low_ref.grad_two_ref, bf16[512,768]{1,0:T(8,128)(2,1)S(1)} %get-tuple-element.207.mine_top_ref, ...), custom_call_target="tpu_custom_call" | custom-call | flops 1000000 | bytes 10000 | tf_op jit(solution)/shard_map/leave/pallas_call | solution.py:303
  143.7 11.8 %attend_backward.2 = (bf16[1024,384]{1,0:T(8,128)(2,1)S(1)}, bf16[1024,192]{1,0:T(8,128)(2,1)S(1)}) custom-call(bf16[3,1024,64]{2,1,0:T(8,128)(2,1)} %get-tuple-element.219.q_ref, bf16[3,1024,64]{2,1,0:T(8,128)(2,1)} %get-tuple-element.220.k_ref, bf16[3,1024,64]{2,1,0:T(8,128)(2,1)} %get-tuple-element.221.v_ref, f32[3,1,1024]{2,1,0:T(1,128)} %get-tuple-element.222.lse_ref, ...), custom_call_target="tpu_custom_call" | custom-call | flops 1000000 | bytes 10000 | tf_op jit(solution)/shard_map/attend_backward/pallas_call | solution.py:251
  158.4 3.5 %heads_grad.2 = (bf16[768,384]{1,0:T(8,128)(2,1)}, bf16[768,384]{1,0:T(8,128)(2,1)}) custom-call(bf16[1024,768]{1,0:T(8,128)(2,1)S(1)} %copy-done, bf16[1024,768]{1,0:T(8,128)(2,1)S(1)} %get-tuple-element.212.grad_ref.one_ref, bf16[1024,384]{1,0:T(8,128)(2,1)S(1)} %get-tuple-element.229.qk_ref.qk2_ref, ...), custom_call_target="tpu_custom_call" | custom-call | flops 1000000 | bytes 10000 | tf_op jit(solution)/shard_map/heads_grad/pallas_call | solution.py:496
  165.4 11.5 %attend_backward.3 = (bf16[1024,384]{1,0:T(8,128)(2,1)S(1)}, bf16[1024,192]{1,0:T(8,128)(2,1)S(1)}) custom-call(bf16[3,1024,64]{2,1,0:T(8,128)(2,1)} %get-tuple-element.213.q_ref, bf16[3,1024,64]{2,1,0:T(8,128)(2,1)} %get-tuple-element.214.k_ref, bf16[3,1024,64]{2,1,0:T(8,128)(2,1)} %get-tuple-element.215.v_ref, f32[3,1,1024]{2,1,0:T(1,128)} %get-tuple-element.216.lse_ref, ...), custom_call_target="tpu_custom_call" | custom-call | flops 1000000 | bytes 10000 | tf_op jit(solution)/shard_map/attend_backward/pallas_call | solution.py:251
  181.3 3.5 %heads_grad.3 = (bf16[768,384]{1,0:T(8,128)(2,1)}, bf16[768,384]{1,0:T(8,128)(2,1)}) custom-call(bf16[1024,768]{1,0:T(8,128)(2,1)S(1)} %copy-done, bf16[1024,768]{1,0:T(8,128)(2,1)S(1)} %get-tuple-element.212.grad_ref.one_ref, bf16[1024,384]{1,0:T(8,128)(2,1)S(1)} %get-tuple-element.250.qk_ref.qk1_ref, ...), custom_call_target="tpu_custom_call" | custom-call | flops 1000000 | bytes 10000 | tf_op jit(solution)/shard_map/heads_grad/pallas_call | solution.py:496
  187.3 3.4 %collective-permute-start.37 = (bf16[96,512]{1,0:T(8,128)(2,1)S(1)}, bf16[96,512]{1,0:T(8,128)(2,1)S(1)}, u32[]{:S(2)}, u32[]{:S(2)}) collective-permute-start(bf16[96,512]{1,0:T(8,128)(2,1)S(1)} %slice.260), channel_id=1, source_target_pairs={{0,16},{4,20},{8,24},{12,28},{16,0},{20,4},{24,8},{28,12},{1,17},{... | collective-permute-start | bytes 294920 | tf_op jit(solution)/shard_map/ppermute | solution.py:31
  191.8 8.4 %inputs.1 = (f32[1024,768]{1,0:T(8,128)}, bf16[1024,768]{1,0:T(8,128)(2,1)S(1)}) custom-call(bf16[1024,384]{1,0:T(8,128)(2,1)S(1)} %get-tuple-element.250.qk_ref.qk1_ref, bf16[1024,192]{1,0:T(8,128)(2,1)S(1)} %get-tuple-element.239.v_ref.v1_ref, bf16[1024,384]{1,0:T(8,128)(2,1)S(1)} %get-tuple-element.229.qk_ref.qk2_ref, ...), custom_call_target="tpu_custom_call" | custom-call | flops 1000000 | bytes 10000 | tf_op jit(solution)/shard_map/inputs/pallas_call | solution.py:303
  201.1 7.6 %collective-permute-done.39 = bf16[192,1024]{1,0:T(8,128)(2,1)S(1)} collective-permute-done((bf16[192,1024]{1,0:T(8,128)(2,1)S(1)}, bf16[192,1024]{1,0:T(8,128)(2,1)S(1)}, u32[]{:S(2)}, u32[]{:S(2)}) %collective-permute-start.39) | collective-permute-done | bytes 393248 | tf_op jit(solution)/shard_map/ppermute | solution.py:31
  213.9 6.2 %collective-permute-done.42 = bf16[192,768]{1,0:T(8,128)(2,1)} collective-permute-done((bf16[192,768]{1,0:T(8,128)(2,1)}, bf16[192,768]{1,0:T(8,128)(2,1)}, u32[]{:S(2)}, u32[]{:S(2)}) %collective-permute-start.42) | collective-permute-done | bytes 294944 | tf_op jit(solution)/shard_map/ppermute | solution.py:31
  240.0 3.8 %finish.2 = (f32[512,768]{1,0:T(8,128)}, bf16[512,768]{1,0:T(8,128)(2,1)}) custom-call(s32[1]{0:T(128)} %bitcast.core_ref, bf16[1024,768]{1,0:T(8,128)(2,1)} %copy-done.1, f32[1024,768]{1,0:T(8,128)} %get-tuple-element.252.full_ref, bf16[1024,768]{1,0:T(8,128)(2,1)} %get-tuple-element.253.out_ref, bf16[512,768]{1,0:T(8,128)(2,1)} %copy-done.38, ...), custom_call_target="tpu_custom_call" | custom-call | flops 4000000000 | bytes 8388608 | tf_op jit(solution)/shard_map/finish/pallas_call | solution.py:533
  246.5 4.0 %finish.3 = (f32[512,768]{1,0:T(8,128)}, bf16[512,768]{1,0:T(8,128)(2,1)}) custom-call(s32[1]{0:T(128)} %bitcast.core_ref, bf16[1024,768]{1,0:T(8,128)(2,1)} %copy-done.1, f32[1024,768]{1,0:T(8,128)} %get-tuple-element.252.full_ref, bf16[1024,768]{1,0:T(8,128)(2,1)} %get-tuple-element.253.out_ref, ...), custom_call_target="tpu_custom_call", output_to_operand_aliasing={{0}: (6, {}), {1}: (7, {})} | custom-call | flops 4000000000 | bytes 8388608 | tf_op jit(solution)/shard_map/finish/pallas_call | solution.py:533
  251.2 4.0 %adam.1 = (f32[1,1]{1,0:T(1,128)}, f32[3,96,192]{2,1,0:T(8,128)}, f32[3,96,192]{2,1,0:T(8,128)}, f32[3,96,192]{2,1,0:T(8,128)}, f32[192,96]{1,0:T(8,128)}, /*ind...) custom-call(s32[1]{0:T(128)} %bitcast.17.refs_0_, ...), custom_call_target="tpu_custom_call" | custom-call | tf_op jit(solution)/shard_map/adam/pallas_call | solution.py:603
  (259 shorter events, 101.7 us)
Async XLA Ops:
  22.6 17.7 %collective-permute-start.6 = (bf16[512,768]{1,0:T(8,128)(2,1)S(1)}, bf16[512,768]{1,0:T(8,128)(2,1)S(1)}, u32[]{:S(2)}, u32[]{:S(2)}) collective-permute-start(bf16[512,768]{1,0:T(8,128)(2,1)S(1)} %slice.144), channel_id=1, source_target_pairs={{0,1},{1,0},{2,3},{3,2},{4,5},{5,4},{6,7},{7,6},{8,9},{9,8},{10,11... | collective-permute-start | bytes 2359304 | tf_op jit(solution)/shard_map/ppermute | solution.py:31
  22.7 19.8 %collective-permute-start.7 = (bf16[384,768]{1,0:T(8,128)(2,1)S(1)}, bf16[384,768]{1,0:T(8,128)(2,1)S(1)}, u32[]{:S(2)}, u32[]{:S(2)}) collective-permute-start(bf16[384,768]{1,0:T(8,128)(2,1)S(1)} %pad_maximum_fusion.6.qka_ref.voa_ref.att_ref), channel_id=1, source_target_pairs={{0,4},{4,0},{8,12},{12,8},{16,20},{20,16},{24,28},{28,24},{1,5},{5... | collective-permute-start | bytes 1769480 | tf_op jit(solution)/shard_map/ppermute | solution.py:31
  24.1 18.5 %collective-permute-start.8 = (bf16[384,768]{1,0:T(8,128)(2,1)S(1)}, bf16[384,768]{1,0:T(8,128)(2,1)S(1)}, u32[]{:S(2)}, u32[]{:S(2)}) collective-permute-start(bf16[384,768]{1,0:T(8,128)(2,1)S(1)} %pad_maximum_fusion.6.qka_ref.voa_ref.att_ref), channel_id=1, source_target_pairs={{0,2},{1,3},{2,0},{3,1},{4,6},{5,7},{6,4},{7,5},{8,10},{9,11},{10,... | collective-permute-start | bytes 1769480 | tf_op jit(solution)/shard_map/ppermute | solution.py:31
  25.6 14.7 %collective-permute-start.9 = (bf16[96,1280]{1,0:T(8,128)(2,1)S(1)}, bf16[96,1280]{1,0:T(8,128)(2,1)S(1)}, u32[]{:S(2)}, u32[]{:S(2)}) collective-permute-start(bf16[96,1280]{1,0:T(8,128)(2,1)S(1)} %pad_maximum_fusion.10), channel_id=1, source_target_pairs={{0,16},{4,20},{8,24},{12,28},{16,0},{20,4},{24,8},{28,12},{1,17},{... | collective-permute-start | bytes 737288 | tf_op jit(solution)/shard_map/ppermute | solution.py:31
  42.6 15.3 %collective-permute-start.13 = (bf16[192,1280]{1,0:T(8,128)(2,1)S(1)}, bf16[192,1280]{1,0:T(8,128)(2,1)S(1)}, u32[]{:S(2)}, u32[]{:S(2)}) collective-permute-start(bf16[192,1280]{1,0:T(8,128)(2,1)S(1)} %pad_maximum_fusion.7), channel_id=1, source_target_pairs={{0,8},{4,12},{8,0},{12,4},{16,24},{20,28},{24,16},{28,20},{1,9},{5... | collective-permute-start | bytes 1474568 | tf_op jit(solution)/shard_map/ppermute | solution.py:31
  43.4 14.6 %collective-permute-start.11 = (bf16[384,384]{1,0:T(8,128)(2,1)S(1)}, bf16[384,384]{1,0:T(8,128)(2,1)S(1)}, u32[]{:S(2)}, u32[]{:S(2)}) collective-permute-start(bf16[384,384]{1,0:T(8,128)(2,1)S(1)} %slice.148), channel_id=1, source_target_pairs={{0,2},{1,3},{2,0},{3,1},{4,6},{5,7},{6,4},{7,5},{8,10},{9,11},{10,... | collective-permute-start | bytes 884744 | tf_op jit(solution)/shard_map/ppermute | solution.py:31
  44.1 13.9 %collective-permute-start.12 = (bf16[384,384]{1,0:T(8,128)(2,1)S(1)}, bf16[384,384]{1,0:T(8,128)(2,1)S(1)}, u32[]{:S(2)}, u32[]{:S(2)}) collective-permute-start(bf16[384,384]{1,0:T(8,128)(2,1)S(1)} %slice.149), channel_id=1, source_target_pairs={{0,4},{4,0},{8,12},{12,8},{16,20},{20,16},{24,28},{28,24},{1,5},{5... | collective-permute-start | bytes 884744 | tf_op jit(solution)/shard_map/ppermute | solution.py:31
  58.0 22.8 %collective-permute-start.15 = (bf16[384,1280]{1,0:T(8,128)(2,1)S(1)}, bf16[384,1280]{1,0:T(8,128)(2,1)S(1)}, u32[]{:S(2)}, u32[]{:S(2)}) collective-permute-start(bf16[384,1280]{1,0:T(8,128)(2,1)S(1)} %pad_maximum_fusion.3.own_ref.low_own_ref), channel_id=1, source_target_pairs={{0,4},{4,0},{8,12},{12,8},{16,20},{20,16},{24,28},{28,24},{1,5},{5... | collective-permute-start | bytes 2949128 | tf_op jit(solution)/shard_map/ppermute | solution.py:31
  59.4 22.3 %collective-permute-start.16 = (bf16[384,1280]{1,0:T(8,128)(2,1)S(1)}, bf16[384,1280]{1,0:T(8,128)(2,1)S(1)}, u32[]{:S(2)}, u32[]{:S(2)}) collective-permute-start(bf16[384,1280]{1,0:T(8,128)(2,1)S(1)} %pad_maximum_fusion.3.own_ref.low_own_ref), channel_id=1, source_target_pairs={{0,2},{1,3},{2,0},{3,1},{4,6},{5,7},{6,4},{7,5},{8,10},{9,11},{10,... | collective-permute-start | bytes 2949128 | tf_op jit(solution)/shard_map/ppermute | solution.py:31
  60.1 20.6 %collective-permute-start.17 = (bf16[4,1,96,256]{3,2,0,1:T(8,128)(2,1)S(1)}, bf16[4,1,96,256]{3,2,0,1:T(8,128)(2,1)S(1)}, u32[]{:S(2)}, u32[]{:S(2)}) collective-permute-start(bf16[4,1,96,256]{3,2,0,1:T(8,128)(2,1)S(1)} %maximum_bitcast_fusion), channel_id=1, source_target_pairs={{0,16},{4,20},{8,24},{12,28},{16,0},{20,4},{24,8},{28,12},{1,17},{... | collective-permute-start | bytes 589832 | tf_op jit(solution)/shard_map/ppermute | solution.py:31
  81.7 13.7 %collective-permute-start.19 = (bf16[512,768]{1,0:T(8,128)(2,1)}, bf16[512,768]{1,0:T(8,128)(2,1)}, u32[]{:S(2)}, u32[]{:S(2)}) collective-permute-start(bf16[512,768]{1,0:T(8,128)(2,1)} %get-tuple-element.184), channel_id=1, source_target_pairs={{0,1},{1,0},{2,3},{3,2},{4,5},{5,4},{6,7},{7,6},{8,9},{9,8},{10,11... | collective-permute-start | bytes 2359304 | tf_op jit(solution)/shard_map/ppermute | solution.py:31
  83.7 15.2 %collective-permute-start.22 = (bf16[384,768]{1,0:T(8,128)(2,1)}, bf16[384,768]{1,0:T(8,128)(2,1)S(1)}, u32[]{:S(2)}, u32[]{:S(2)}) collective-permute-start(bf16[384,768]{1,0:T(8,128)(2,1)} %slice.152), channel_id=1, source_target_pairs={{0,4},{4,0},{8,12},{12,8},{16,20},{20,16},{24,28},{28,24},{1,5},{5... | collective-permute-start | bytes 1769480 | tf_op jit(solution)/shard_map/ppermute | solution.py:31
  85.3 12.7 %collective-permute-start.21 = (bf16[384,512]{1,0:T(8,128)(2,1)S(1)}, bf16[384,512]{1,0:T(8,128)(2,1)S(1)}, u32[]{:S(2)}, u32[]{:S(2)}) collective-permute-start(bf16[384,512]{1,0:T(8,128)(2,1)S(1)} %slice.151), channel_id=1, source_target_pairs={{0,2},{1,3},{2,0},{3,1},{4,6},{5,7},{6,4},{7,5},{8,10},{9,11},{10,... | collective-permute-start | bytes 1179656 | tf_op jit(solution)/shard_map/ppermute | solution.py:31
  116.4 20.0 %collective-permute-start.26 = (bf16[768,512]{1,0:T(8,128)(2,1)S(1)}, bf16[768,512]{1,0:T(8,128)(2,1)S(1)}, u32[]{:S(2)}, u32[]{:S(2)}) collective-permute-start(bf16[768,512]{1,0:T(8,128)(2,1)S(1)} %convolution_convert_fusion.2), channel_id=1, source_target_pairs={{0,2},{1,3},{2,0},{3,1},{4,6},{5,7},{6,4},{7,5},{8,10},{9,11},{10,... | collective-permute-start | bytes 2359304 | tf_op jit(solution)/shard_map/ppermute | solution.py:31
  124.4 31.1 %collective-permute-start.27 = (bf16[384,1024]{1,0:T(8,128)(2,1)S(1)}, bf16[384,1024]{1,0:T(8,128)(2,1)S(1)}, u32[]{:S(2)}, u32[]{:S(2)}) collective-permute-start(bf16[384,1024]{1,0:T(8,128)(2,1)S(1)} %convolution_convert_fusion.6), channel_id=1, source_target_pairs={{0,4},{4,0},{8,12},{12,8},{16,20},{20,16},{24,28},{28,24},{1,5},{5... | collective-permute-start | bytes 2359304 | tf_op jit(solution)/shard_map/ppermute | solution.py:31
  133.1 43.8 %collective-permute-start.28 = (bf16[384,1024]{1,0:T(8,128)(2,1)S(1)}, bf16[384,1024]{1,0:T(8,128)(2,1)S(1)}, u32[]{:S(2)}, u32[]{:S(2)}) collective-permute-start(bf16[384,1024]{1,0:T(8,128)(2,1)S(1)} %convolution_convert_fusion.5), channel_id=1, source_target_pairs={{0,4},{4,0},{8,12},{12,8},{16,20},{20,16},{24,28},{28,24},{1,5},{5... | collective-permute-start | bytes 2359304 | tf_op jit(solution)/shard_map/ppermute | solution.py:31
  155.9 21.1 %collective-permute-start.29 = (bf16[384,512]{1,0:T(8,128)(2,1)S(1)}, bf16[384,512]{1,0:T(8,128)(2,1)S(1)}, u32[]{:S(2)}, u32[]{:S(2)}) collective-permute-start(bf16[384,512]{1,0:T(8,128)(2,1)S(1)} %slice.253), channel_id=1, source_target_pairs={{0,4},{4,0},{8,12},{12,8},{16,20},{20,16},{24,28},{28,24},{1,5},{5... | collective-permute-start | bytes 1179656 | tf_op jit(solution)/shard_map/ppermute | solution.py:31
  157.2 19.8 %collective-permute-start.31 = (bf16[384,512]{1,0:T(8,128)(2,1)S(1)}, bf16[384,512]{1,0:T(8,128)(2,1)S(1)}, u32[]{:S(2)}, u32[]{:S(2)}) collective-permute-start(bf16[384,512]{1,0:T(8,128)(2,1)S(1)} %slice.254), channel_id=1, source_target_pairs={{0,2},{1,3},{2,0},{3,1},{4,6},{5,7},{6,4},{7,5},{8,10},{9,11},{10,... | collective-permute-start | bytes 1179656 | tf_op jit(solution)/shard_map/ppermute | solution.py:31
  162.8 14.1 %collective-permute-start.30 = (bf16[384,384]{1,0:T(8,128)(2,1)S(1)}, bf16[384,384]{1,0:T(8,128)(2,1)S(1)}, u32[]{:S(2)}, u32[]{:S(2)}) collective-permute-start(bf16[384,384]{1,0:T(8,128)(2,1)S(1)} %slice.156), channel_id=1, source_target_pairs={{0,4},{4,0},{8,12},{12,8},{16,20},{20,16},{24,28},{28,24},{1,5},{5... | collective-permute-start | bytes 884744 | tf_op jit(solution)/shard_map/ppermute | solution.py:31
  164.4 26.3 %collective-permute-start.34 = (bf16[768,384]{1,0:T(8,128)(2,1)}, bf16[768,384]{1,0:T(8,128)(2,1)S(1)}, u32[]{:S(2)}, u32[]{:S(2)}) collective-permute-start(bf16[768,384]{1,0:T(8,128)(2,1)} %get-tuple-element.231), channel_id=1, source_target_pairs={{0,2},{1,3},{2,0},{3,1},{4,6},{5,7},{6,4},{7,5},{8,10},{9,11},{10,... | collective-permute-start | bytes 1769480 | tf_op jit(solution)/shard_map/ppermute | solution.py:31
  177.4 23.0 %collective-permute-start.38 = (bf16[384,512]{1,0:T(8,128)(2,1)S(1)}, bf16[384,512]{1,0:T(8,128)(2,1)S(1)}, u32[]{:S(2)}, u32[]{:S(2)}) collective-permute-start(bf16[384,512]{1,0:T(8,128)(2,1)S(1)} %slice.252), channel_id=1, source_target_pairs={{0,2},{1,3},{2,0},{3,1},{4,6},{5,7},{6,4},{7,5},{8,10},{9,11},{10,... | collective-permute-start | bytes 1179656 | tf_op jit(solution)/shard_map/ppermute | solution.py:31
  180.6 19.6 %collective-permute-start.33 = (bf16[384,384]{1,0:T(8,128)(2,1)S(1)}, bf16[384,384]{1,0:T(8,128)(2,1)S(1)}, u32[]{:S(2)}, u32[]{:S(2)}) collective-permute-start(bf16[384,384]{1,0:T(8,128)(2,1)S(1)} %add_convert_fusion), channel_id=1, source_target_pairs={{0,2},{1,3},{2,0},{3,1},{4,6},{5,7},{6,4},{7,5},{8,10},{9,11},{10,... | collective-permute-start | bytes 884744 | tf_op jit(solution)/shard_map/ppermute | solution.py:31
  185.8 14.4 %collective-permute-start.32 = (bf16[384,384]{1,0:T(8,128)(2,1)S(1)}, bf16[384,384]{1,0:T(8,128)(2,1)S(1)}, u32[]{:S(2)}, u32[]{:S(2)}) collective-permute-start(bf16[384,384]{1,0:T(8,128)(2,1)S(1)} %slice.159), channel_id=1, source_target_pairs={{0,4},{4,0},{8,12},{12,8},{16,20},{20,16},{24,28},{28,24},{1,5},{5... | collective-permute-start | bytes 884744 | tf_op jit(solution)/shard_map/ppermute | solution.py:31
  187.3 12.9 %collective-permute-start.37 = (bf16[96,512]{1,0:T(8,128)(2,1)S(1)}, bf16[96,512]{1,0:T(8,128)(2,1)S(1)}, u32[]{:S(2)}, u32[]{:S(2)}) collective-permute-start(bf16[96,512]{1,0:T(8,128)(2,1)S(1)} %slice.260), channel_id=1, source_target_pairs={{0,16},{4,20},{8,24},{12,28},{16,0},{20,4},{24,8},{28,12},{1,17},{... | collective-permute-start | bytes 294920 | tf_op jit(solution)/shard_map/ppermute | solution.py:31
  (64 other events, 432.3 us)
where the time goes:
time: 259 us; the launch traced here: 255 us
  Pallas kernels  116 us (45%)
  starting transfers between devices  51.7 us (20%)
  waiting for transfers between devices  41.6 us (16%)
  other arithmetic  22 us (8%)
  local copies, waits for them, and re-layouts  11 us (4%)
  matrix products  9.41 us (4%)
  between operations  3.92 us (2%)
    ppermute x49, starting transfers between devices, swap(): return lax.ppermute(value, axis, [(i, i ^ bit) for i in range(size)])  51.7 us
    pallas_call x8, Pallas kernels, by_rows(): pl.pallas_call(kernel, grid=(L // step,), in_specs=specs + list(held_spec...  50.4 us
    ppermute x49, waiting for transfers between devices, swap(): return lax.ppermute(value, axis, [(i, i ^ bit) for i in range(size)])  41.6 us
    pallas_call x2, Pallas kernels, attend_backward(): pl.pallas_call(attend_back_kernel, grid=(heads,), in_specs=[by_head((1, L...  23.4 us
    pallas_call x2, Pallas kernels, attend_forward(): pl.pallas_call(attend_kernel, grid=(1,), in_specs=list(specs), out_specs=...  23.3 us
    pallas_call x2, Pallas kernels, finish(): pl.pallas_call(finish_kernel, grid_spec=pltpu.PrefetchScalarGridSpec(num_...  7.83 us
    pallas_call x2, Pallas kernels, heads_grad(): pl.pallas_call(heads_grad_kernel, grid=(D // 256,), in_specs=[split, spli...  7 us
    dot_general x6, matrix products, tn(): lax.dot_general(rows, grads, (((0,), (0,)), ((), ())), preferred_element_...  6.03 us
  transfers between devices with their start and end apart: 49, of which 15 were waited for; matrix products, arithmetic and copies ran while one was open for 13% of the time, Pallas kernels for 39%

commit v1 on v0

--- a/solution.py
+++ b/solution.py
@@ -173,7 +173,7 @@
     headed = pltpu.HBM((heads, L, HD), LOW)
     outs = (
         headed, headed, headed,
-        pltpu.HBM((L, heads * HD), LOW),
+        jax.ShapeDtypeStruct((L, heads * HD), LOW),
         pltpu.HBM((heads, 1, L), FULL),
     )
     args, specs = zip(*[columns(p) for p in (rows, *qk, *vo, cosine, sine)])
@@ -187,7 +187,7 @@
         compiler_params=pltpu.CompilerParams(vmem_limit_bytes=24 << 20),
         cost_estimate=SMALL,
         name="attend_forward",
-    )(*[pinned(a) for a in args])
+    )(*args)
 
 
 def attend_back_kernel(
@@ -338,7 +338,7 @@
         held_ref[0, :half] = att_ref[:, 3 * width :]
         held_ref[0, half:] = y_ref[:, 3 * width :]
         held_ref[1, :half] = x_ref[:, 3 * width :]
-        held_ref[1, half:] = corner_ref[:, 3 * width :]
+        held_ref[1, half:] = corner_ref[:, width:]
 
 
 def project_kernel(one_ref, two_ref, att_ref, y_ref, x_ref, corner_ref, out_ref, held_ref):
@@ -446,12 +446,19 @@
 def leave_kernel(
     grad_two_ref, mine_top_ref, mine_bottom_ref, theirs_top_ref, theirs_bottom_ref,
     normed_ref, inv_ref, gains_ref, att_ref, y_ref, x_ref, corner_ref,
-    low_ref, ctx1_ref, ctx2_ref, sum_ref, held_ref,
+    low_ref, ctx1_ref, ctx2_ref, sum_ref, held_ref, mid_ref,
 ):
     heads_out(held_ref, (att_ref, y_ref, x_ref, corner_ref))
-    top = add(mine_top_ref[...], theirs_top_ref[...])
-    bottom = add(mine_bottom_ref[...], theirs_bottom_ref[...])
-    hidden_grad = grad_two_ref[...].astype(FULL) + jnp.where(in_top(), top, bottom)
+
+    @pl.when(in_top())
+    def _():
+        mid_ref[...] = add(mine_top_ref[...], theirs_top_ref[...])
+
+    @pl.when(jnp.logical_not(in_top()))
+    def _():
+        mid_ref[...] = add(mine_bottom_ref[...], theirs_bottom_ref[...])
+
+    hidden_grad = grad_two_ref[...].astype(FULL) + mid_ref[...]
     normed = normed_ref[...].astype(FULL)
     column_sum(sum_ref, hidden_grad * normed)
     low = norm_back(hidden_grad * gains_ref[0], normed, inv_ref[...]).astype(LOW)
@@ -461,7 +468,7 @@
 
 
 def input_kernel(
-    qk1_ref, v1_ref, qk2_ref, v2_ref, att_ref, y_ref, x_ref, corner_ref,
+    qk1_ref, v1_ref, qk2_ref, v2_ref, att_ref, y_ref, x_ref, qk_corner_ref, vo_corner_ref,
     full_ref, low_ref, held_ref,
 ):
     half, width = att_ref.shape[0], v1_ref.shape[1]
@@ -472,7 +479,8 @@
         held_ref[0, :half] = att_ref[:, : pair + width]
         held_ref[0, half:] = y_ref[:, : pair + width]
         held_ref[1, :half] = x_ref[:, : pair + width]
-        held_ref[1, half:] = corner_ref[:, : pair + width]
+        held_ref[1, half:, :pair] = qk_corner_ref[...]
+        held_ref[1, half:, pair:] = vo_corner_ref[:, :width]
 
     total = 0.0
     for x, qk_ref, v_ref in ((0, qk1_ref, v1_ref), (1, qk2_ref, v2_ref)):
@@ -550,6 +558,24 @@
     )(core, grad_one, pinned(part_full), pinned(layer_output), theirs, mover, *done)
 
 
+def last_kernel(kept_ref, received_ref, square_ref, sum_ref, total_ref):
+    value = kept_ref[...] + received_ref[...].astype(FULL)
+    sum_ref[...] = value
+    total = jnp.sum(jnp.sum(value * value, axis=0, keepdims=True), axis=1, keepdims=True)
+    total_ref[...] = square_ref[...] + total
+
+
+def last_sum(kept, received, square):
+    vmem = pl.BlockSpec(memory_space=pltpu.VMEM)
+    return pl.pallas_call(
+        last_kernel,
+        in_specs=[vmem] * 3,
+        out_specs=[vmem] * 2,
+        out_shape=[jax.ShapeDtypeStruct(kept.shape, FULL), jax.ShapeDtypeStruct((1, 128), FULL)],
+        name="last_sum",
+    )(kept, received, square)
+
+
 def adam_kernel(clip, rates, *refs):
     me = refs[0][0]
     message = refs[1][...] + refs[2][...]
@@ -571,7 +597,7 @@
             ref[at] = value
 
     width, hid = att_ref.shape[1] // 4, ffn_ref.shape[1] // 2
-    step = 32 if block % 32 == 0 else block
+    step = 16 if block % 16 == 0 else block
 
     def some(i, carry):
         rows = pl.ds(pl.multiple_of(i * step, step), step) if step < block else slice(None)
@@ -611,11 +637,16 @@
 
 
 def rope_tables(place):
-    half = HD // 2
+    half, low = HD // 2, place.shape[0] // 2
     lane = jnp.arange(128) % HD
     freq = jnp.exp(-jnp.log(10000.0) * (lane % half).astype(FULL) / half)
     angle = place[:, None] * freq[None, :]
-    return jnp.cos(angle), jnp.where(lane < half, -1.0, 1.0)[None, :] * jnp.sin(angle)
+    cosine, sine = jnp.cos(angle), jnp.sin(angle)
+    c1, s1 = cosine[:low, None], sine[:low, None]
+    c2, s2 = cosine[None, low:], sine[None, low:]
+    sign = jnp.where(lane < half, -1.0, 1.0)[None, None, :]
+    both = c1 * c2 - s1 * s2, sign * (s1 * c2 + c1 * s2)
+    return [table.reshape(L, 128) for table in both]
 
 
 def adam_update(weight, first, second, grad, ratio, rate, decay):
@@ -691,15 +722,17 @@
     down_x = swap(down, "narrow", 2)
     both = jnp.concatenate([layer_input, layer_cotangent], axis=0)
     moved = jnp.dot(both, mover, preferred_element_type=FULL).astype(LOW)
-    place = jnp.arange(L, dtype=FULL)
+    place = jnp.arange(32, dtype=FULL)
+    place = jnp.concatenate([32.0 * place, place])
     att, down_y, down_x, gains, moved, place = lax.optimization_barrier(
         (att, down_y, down_x, gains, moved, place)
     )
     att_y = swap(att, "wide", 1)
     att_x = swap(att, "narrow", 2)
     ffn = widen(after(ffn, att), near[:1])
+    inputs = both_halves(moved[:rows], swap(moved[:rows], "narrow", 1))
+    inputs, gains = lax.optimization_barrier((inputs, gains))
     gains = widen(gains, bits[-1:])
-    inputs = both_halves(moved[:rows], swap(moved[:rows], "narrow", 1))
     moved_up = moved[rows:]
     cosine, sine = rope_tables(place)
     inputs, att, att_y, att_x, ffn, gains, cosine, sine = lax.optimization_barrier(
@@ -720,13 +753,12 @@
     down = jnp.stack([down, down_y, down_x, down_corner])[:, None]
     for bit in near[:1]:
         down = jnp.concatenate([down, swap(down, "wide", bit)], axis=1)
-    corner = jnp.concatenate([qk_corner, vo_corner], axis=1)
-    qk[1][1], vo[1][1] = (corner, pair, 0), (corner, pair, 1)
+    qk[1][1], vo[1][1] = qk_corner, vo_corner
     ffn_y = swap(ffn, "wide", 1)
     ffn_x = swap(ffn, "narrow", 2)
     saved.append(attend_forward(second_in, qk[1], vo[1], cosine, sine))
     context = [s[3] for s in saved]
-    att_out = [att, att_y, att_x, corner]
+    att_out = [att, att_y, att_x, vo_corner]
     held = [pltpu.VMEM((2, D, cols), LOW)]
     low_d, full_d = (D, LOW, False), (D, FULL, True)
     (attn_part,) = by_rows(
@@ -792,7 +824,7 @@
         leave_kernel, "leave",
         [grad_two_low, tuple(mid_part), tuple(mid_other), pinned(normed_one), pinned(inv_one)],
         [gains, *att_out], [low_d, (cols, LOW, True), (cols, LOW, True)],
-        sums=1, scratch=held,
+        sums=1, scratch=held + [pltpu.VMEM((QB, D), FULL)],
     )
 
     q, k, v, _, lse = saved[1]
@@ -823,10 +855,10 @@
     vo_y = swap(vo_far, "wide", 1)
     late = jnp.concatenate([add(gate_sum[:, :hid], gate_x), add(up_sum[:, :hid], up_x)], axis=1)
     early_red = narrow_down(early, back[1:])
-    dqk1, vo_sum = lax.optimization_barrier((dqk1, vo_sum))
+    dqk1, vo_sum, late = lax.optimization_barrier((dqk1, vo_sum, late))
     part_full, part_low = by_rows(
         input_kernel, "inputs", [dqk1, dv1, dqk2, dv2],
-        att_out, [full_d, low_d], step=128,
+        [att, att_y, att_x, qk_corner, vo_corner], [full_d, low_d], step=128,
         scratch=[pltpu.VMEM((2, D, 3 * cols), LOW)],
     )
     late = narrow_down(late, back[:1])
@@ -845,9 +877,12 @@
     last = narrow_down(last, back[:1])
     late_red = narrow_down(late, back[1:])
     early_square = jnp.sum(early_red * early_red) + jnp.sum(late_red * late_red)
-    att_red = narrow_down(last, back[1:])
-
-    square = jnp.full((1, 128), early_square + jnp.sum(att_red * att_red), FULL)
+    last = narrow_down(last, back[1:-1])
+    att_red, square = last_sum(
+        last[:block], swap(last[block:].astype(LOW), "wide", back[-1]),
+        jnp.full((1, 128), early_square, FULL),
+    )
+
     square = square + swap(square, "narrow", 1)
     message = jnp.concatenate([gain_grads.reshape(1, 2 * D), square], axis=1)
     message = message + swap(message, "narrow", 2)

time: 259 us -> 254 us (0.981); the launches traced: 255 us -> 253 us
  starting transfers between devices: 51.7 us -> 61.8 us
  other arithmetic: 22 us -> 15.2 us
  Pallas kernels: 116 us -> 112 us
    ppermute x49, starting transfers between devices: 51.7 us -> 61.8 us  [swap(): return lax.ppermute(value, axis, [(i, i ^ bit) for i in range(size)])]
    pallas_call x2, Pallas kernels: 23.3 us -> 18.1 us  [attend_forward(): pl.pallas_call(attend_kernel, grid=(1,), in_specs=list(specs), out_specs=...]
    mul x1 -> x2, other arithmetic: 3.54 us -> 0.05 us  [the longest x1 0.04 us: rope_tables(): both = (c1 * c2 - s1 * s2, sign * (s1 * c2 + c1 * s2))]
  transfers between devices with their start and end apart: 49 -> 49, of which waited for: 15 -> 17; matrix products, arithmetic and copies ran while one was open for 13% -> 12% of each run, Pallas kernels for 39% -> 37%
where the time goes in v1:
time: 254 us; the launch traced here: 253 us
  Pallas kernels  112 us (44%)
  starting transfers between devices  61.8 us (24%)
  waiting for transfers between devices  41.2 us (16%)
  other arithmetic  15.2 us (6%)
  local copies, waits for them, and re-layouts  10.4 us (4%)
  matrix products  9.3 us (4%)
  between operations  3.26 us (1%)
    ppermute x49, starting transfers between devices, swap(): return lax.ppermute(value, axis, [(i, i ^ bit) for i in range(size)])  61.8 us
    pallas_call x8, Pallas kernels, by_rows(): pl.pallas_call(kernel, grid=(L // step,), in_specs=specs + list(held_spec...  49.6 us
    ppermute x49, waiting for transfers between devices, swap(): return lax.ppermute(value, axis, [(i, i ^ bit) for i in range(size)])  41.2 us
    pallas_call x2, Pallas kernels, attend_backward(): pl.pallas_call(attend_back_kernel, grid=(heads,), in_specs=[by_head((1, L...  23.3 us
    pallas_call x2, Pallas kernels, attend_forward(): pl.pallas_call(attend_kernel, grid=(1,), in_specs=list(specs), out_specs=...  18.1 us
    pallas_call x2, Pallas kernels, finish(): pl.pallas_call(finish_kernel, grid_spec=pltpu.PrefetchScalarGridSpec(num_...  7.83 us
    pallas_call x2, Pallas kernels, heads_grad(): pl.pallas_call(heads_grad_kernel, grid=(D // 256,), in_specs=[split, spli...  7.01 us
    dot_general x6, matrix products, tn(): lax.dot_general(rows, grads, (((0,), (0,)), ((), ())), preferred_element_...  5.99 us
  transfers between devices with their start and end apart: 49, of which 17 were waited for; matrix products, arithmetic and copies ran while one was open for 12% of the time, Pallas kernels for 37%

profile of v1, /device:TPU:0, one launch (start us, length us, event | category | flops | bytes accessed | tf_op | source)
XLA Modules:
  0.0 253.2 jit_solution(11901966913697421653)
XLA Ops:
  2.9 4.1 %collective-permute-start = (bf16[96,768]{1,0:T(8,128)(2,1)S(1)}, bf16[96,768]{1,0:T(8,128)(2,1)S(1)}, u32[]{:S(2)}, u32[]{:S(2)}) collective-permute-start(bf16[96,768]{1,0:T(8,128)(2,1)S(1)} %pad_maximum_fusion.11), channel_id=1, source_target_pairs={{0,16},{4,20},{8,24},{12,28},{16,0},{20,4},{24,8},{28,12},{1,17},{... | collective-permute-start | bytes 442376 | tf_op jit(solution)/shard_map/ppermute | solution.py:31
  30.3 10.5 %collective-permute-done.9 = bf16[96,1280]{1,0:T(8,128)(2,1)S(1)} collective-permute-done((bf16[96,1280]{1,0:T(8,128)(2,1)S(1)}, bf16[96,1280]{1,0:T(8,128)(2,1)S(1)}, u32[]{:S(2)}, u32[]{:S(2)}) %collective-permute-start.9) | collective-permute-done | bytes 245792 | tf_op jit(solution)/shard_map/ppermute | solution.py:31
  44.4 9.2 %attend_forward.2 = (bf16[3,1024,64]{2,1,0:T(8,128)(2,1)}, bf16[3,1024,64]{2,1,0:T(8,128)(2,1)}, bf16[3,1024,64]{2,1,0:T(8,128)(2,1)}, bf16[1024,192]{1,0:T(8,128)(2,1)S(1)}, f32[3,1,1024]{2,1,0:T(1,128)}) custom-call(bf16[1024,768]{1,0:T(8,128)(2,1)S(1)} %pad_maximum_fusion.rows_ref, bf16[384,768]{1,0:T(8,128)(2,1)S(1)} %pad_maximum_fusion.6.qka_ref.voa_ref.att_ref, ...), custom_call_target="tpu_custom_call" | custom-call | flops 1000000 | bytes 10000 | tf_op jit(solution)/shard_map/attend_forward/pallas_call | solution.py:180
  59.4 9.0 %attend_forward.3 = (bf16[3,1024,64]{2,1,0:T(8,128)(2,1)}, bf16[3,1024,64]{2,1,0:T(8,128)(2,1)}, bf16[3,1024,64]{2,1,0:T(8,128)(2,1)}, bf16[1024,192]{1,0:T(8,128)(2,1)S(1)}, f32[3,1,1024]{2,1,0:T(1,128)}) custom-call(bf16[1024,768]{1,0:T(8,128)(2,1)S(1)} %pad_maximum_fusion.rows_ref, bf16[384,768]{1,0:T(8,128)(2,1)S(1)} %collective-permute-done.8.qka_ref.voa_ref.x_ref, ...), custom_call_target="tpu_custom_call" | custom-call | flops 1000000 | bytes 10000 | tf_op jit(solution)/shard_map/attend_forward/pallas_call | solution.py:180
  68.3 3.5 %project.1.mine_ref = bf16[1024,768]{1,0:T(8,128)(2,1)S(1)} custom-call(bf16[1024,192]{1,0:T(8,128)(2,1)S(1)} %get-tuple-element.170.one_ref.ctx_ref, bf16[1024,192]{1,0:T(8,128)(2,1)S(1)} %get-tuple-element.179.two_ref.ctx_ref, bf16[384,768]{1,0:T(8,128)(2,1)} %copy-done.2, bf16[384,768]{1,0:T(8,128)(2,1)} %copy-done.3, bf16[384,768]{1,0:T(8,128)(2,1)} %copy-done.4, ...), custom_call_target="tpu_custom_call" | custom-call | flops 1000000 | bytes 10000 | tf_op jit(solution)/shard_map/project/pallas_call | solution.py:303
  72.6 4.2 %collective-permute-done.15.y_ref.low_y_ref = bf16[384,1280]{1,0:T(8,128)(2,1)S(1)} collective-permute-done((bf16[384,1280]{1,0:T(8,128)(2,1)S(1)}, bf16[384,1280]{1,0:T(8,128)(2,1)S(1)}, u32[]{:S(2)}, u32[]{:S(2)}) %collective-permute-start.15) | collective-permute-done | bytes 983072 | tf_op jit(solution)/shard_map/ppermute | solution.py:31
  82.8 6.5 %enter.1 = (bf16[1024,768]{1,0:T(8,128)(2,1)}, f32[1024,1]{1,0:T(8,128)}, bf16[1024,768]{1,0:T(8,128)(2,1)S(1)}, bf16[1024,512]{1,0:T(8,128)(2,1)}, bf16[1024,51...) custom-call(bf16[1024,768]{1,0:T(8,128)(2,1)} %copy-done, ...), custom_call_target="tpu_custom_call" | custom-call | flops 1000000 | bytes 10000 | tf_op jit(solution)/shard_map/enter/pallas_call | solution.py:303
  95.3 8.3 %rest.1 = (bf16[1024,512]{1,0:T(8,128)(2,1)}, bf16[1024,512]{1,0:T(8,128)(2,1)}, bf16[1024,512]{1,0:T(8,128)(2,1)S(1)}, bf16[1024,768]{1,0:T(8,128)(2,1)S(1)}, b...) custom-call(bf16[1024,768]{1,0:T(8,128)(2,1)S(1)} %get-tuple-element.193.hidden_ref, ...), custom_call_target="tpu_custom_call" | custom-call | flops 1000000 | bytes 10000 | tf_op jit(solution)/shard_map/rest/pallas_call | solution.py:303
  107.0 4.7 %turn.1 = (bf16[1024,768]{1,0:T(8,128)(2,1)}, bf16[1024,768]{1,0:T(8,128)(2,1)S(1)}, f32[1,768]{1,0:T(1,128)S(1)}) custom-call(bf16[1024,768]{1,0:T(8,128)(2,1)} %get-tuple-element.185.normed_ref, bf16[1024,768]{1,0:T(8,128)(2,1)S(1)} %get-tuple-element.198.mine_ref, bf16[1024,768]{1,0:T(8,128)(2,1)S(1)} %collective-permute-done.23.theirs_ref, ...), custom_call_target="tpu_custom_call" | custom-call | flops 1000000 | bytes 10000 | tf_op jit(solution)/shard_map/turn/pallas_call | solution.py:303
  113.3 5.5 %back.1 = (bf16[1024,1024]{1,0:T(8,128)(2,1)S(1)}, bf16[1024,1024]{1,0:T(8,128)(2,1)S(1)}) custom-call(bf16[1024,768]{1,0:T(8,128)(2,1)S(1)} %get-tuple-element.201.low_ref.grad_two_ref, bf16[1024,512]{1,0:T(8,128)(2,1)} %get-tuple-element.202.gate1_ref, bf16[1024,512]{1,0:T(8,128)(2,1)} %get-tuple-element.203.up1_ref, ...), custom_call_target="tpu_custom_call" | custom-call | flops 1000000 | bytes 10000 | tf_op jit(solution)/shard_map/back/pallas_call | solution.py:303
  121.8 6.1 %mid.1 = (bf16[512,768]{1,0:T(8,128)(2,1)S(1)}, bf16[512,768]{1,0:T(8,128)(2,1)S(1)}) custom-call(bf16[1024,1024]{1,0:T(8,128)(2,1)S(1)} %get-tuple-element.209.gg_ref, bf16[1024,1024]{1,0:T(8,128)(2,1)S(1)} %get-tuple-element.208.ug_ref, bf16[768,1024]{1,0:T(8,128)(2,1)} %get-tuple-element.210.own_ref, bf16[768,1024]{1,0:T(8,128)(2,1)} %get-tuple-element.211.other_ref), custom_call_target="tpu_custom_call" | custom-call | flops 1000000 | bytes 10000 | tf_op jit(solution)/shard_map/mid/pallas_call | solution.py:303
  132.7 6.6 %leave.1 = (bf16[1024,768]{1,0:T(8,128)(2,1)S(1)}, bf16[1024,192]{1,0:T(8,128)(2,1)}, bf16[1024,192]{1,0:T(8,128)(2,1)}, f32[1,768]{1,0:T(1,128)S(1)}) custom-call(bf16[1024,768]{1,0:T(8,128)(2,1)S(1)} %get-tuple-element.201.low_ref.grad_two_ref, bf16[512,768]{1,0:T(8,128)(2,1)S(1)} %get-tuple-element.214.mine_top_ref, ...), custom_call_target="tpu_custom_call" | custom-call | flops 1000000 | bytes 10000 | tf_op jit(solution)/shard_map/leave/pallas_call | solution.py:303
  139.3 11.9 %attend_backward.2 = (bf16[1024,384]{1,0:T(8,128)(2,1)S(1)}, bf16[1024,192]{1,0:T(8,128)(2,1)S(1)}) custom-call(bf16[3,1024,64]{2,1,0:T(8,128)(2,1)} %get-tuple-element.226.q_ref, bf16[3,1024,64]{2,1,0:T(8,128)(2,1)} %get-tuple-element.227.k_ref, bf16[3,1024,64]{2,1,0:T(8,128)(2,1)} %get-tuple-element.228.v_ref, f32[3,1,1024]{2,1,0:T(1,128)} %get-tuple-element.229.lse_ref, ...), custom_call_target="tpu_custom_call" | custom-call | flops 1000000 | bytes 10000 | tf_op jit(solution)/shard_map/attend_backward/pallas_call | solution.py:251
  154.4 3.5 %heads_grad.2 = (bf16[768,384]{1,0:T(8,128)(2,1)}, bf16[768,384]{1,0:T(8,128)(2,1)}) custom-call(bf16[1024,768]{1,0:T(8,128)(2,1)S(1)} %copy-done.1, bf16[1024,768]{1,0:T(8,128)(2,1)S(1)} %get-tuple-element.219.grad_ref.one_ref, bf16[1024,384]{1,0:T(8,128)(2,1)S(1)} %get-tuple-element.236.qk_ref.qk2_ref, ...), custom_call_target="tpu_custom_call" | custom-call | flops 1000000 | bytes 10000 | tf_op jit(solution)/shard_map/heads_grad/pallas_call | solution.py:504
  161.1 11.5 %attend_backward.3 = (bf16[1024,384]{1,0:T(8,128)(2,1)S(1)}, bf16[1024,192]{1,0:T(8,128)(2,1)S(1)}) custom-call(bf16[3,1024,64]{2,1,0:T(8,128)(2,1)} %get-tuple-element.220.q_ref, bf16[3,1024,64]{2,1,0:T(8,128)(2,1)} %get-tuple-element.221.k_ref, bf16[3,1024,64]{2,1,0:T(8,128)(2,1)} %get-tuple-element.222.v_ref, f32[3,1,1024]{2,1,0:T(1,128)} %get-tuple-element.223.lse_ref, ...), custom_call_target="tpu_custom_call" | custom-call | flops 1000000 | bytes 10000 | tf_op jit(solution)/shard_map/attend_backward/pallas_call | solution.py:251
  176.4 3.5 %heads_grad.3 = (bf16[768,384]{1,0:T(8,128)(2,1)}, bf16[768,384]{1,0:T(8,128)(2,1)}) custom-call(bf16[1024,768]{1,0:T(8,128)(2,1)S(1)} %copy-done.1, bf16[1024,768]{1,0:T(8,128)(2,1)S(1)} %get-tuple-element.219.grad_ref.one_ref, bf16[1024,384]{1,0:T(8,128)(2,1)S(1)} %get-tuple-element.258.qk_ref.qk1_ref, ...), custom_call_target="tpu_custom_call" | custom-call | flops 1000000 | bytes 10000 | tf_op jit(solution)/shard_map/heads_grad/pallas_call | solution.py:504
  192.3 8.4 %inputs.1 = (f32[1024,768]{1,0:T(8,128)}, bf16[1024,768]{1,0:T(8,128)(2,1)S(1)}) custom-call(bf16[1024,384]{1,0:T(8,128)(2,1)S(1)} %get-tuple-element.258.qk_ref.qk1_ref, bf16[1024,192]{1,0:T(8,128)(2,1)S(1)} %get-tuple-element.246.v_ref.v1_ref, bf16[1024,384]{1,0:T(8,128)(2,1)S(1)} %get-tuple-element.236.qk_ref.qk2_ref, ...), custom_call_target="tpu_custom_call" | custom-call | flops 1000000 | bytes 10000 | tf_op jit(solution)/shard_map/inputs/pallas_call | solution.py:303
  203.8 3.5 %collective-permute-start.43 = (bf16[96,1024]{1,0:T(8,128)(2,1)S(1)}, bf16[96,1024]{1,0:T(8,128)(2,1)S(1)}, u32[]{:S(2)}, u32[]{:S(2)}) collective-permute-start(bf16[96,1024]{1,0:T(8,128)(2,1)S(1)} %slice.270), channel_id=1, source_target_pairs={{0,16},{4,20},{8,24},{12,28},{16,0},{20,4},{24,8},{28,12},{1,17},{... | collective-permute-start | bytes 589832 | tf_op jit(solution)/shard_map/ppermute | solution.py:31
  211.5 5.1 %collective-permute-start.42 = (bf16[96,768]{1,0:T(8,128)(2,1)S(1)}, bf16[96,768]{1,0:T(8,128)(2,1)S(1)}, u32[]{:S(2)}, u32[]{:S(2)}) collective-permute-start(bf16[96,768]{1,0:T(8,128)(2,1)S(1)} %slice.272), channel_id=1, source_target_pairs={{0,16},{4,20},{8,24},{12,28},{16,0},{20,4},{24,8},{28,12},{1,17},{... | collective-permute-start | bytes 442376 | tf_op jit(solution)/shard_map/ppermute | solution.py:31
  216.6 3.8 %collective-permute-done.43 = bf16[96,1024]{1,0:T(8,128)(2,1)S(1)} collective-permute-done((bf16[96,1024]{1,0:T(8,128)(2,1)S(1)}, bf16[96,1024]{1,0:T(8,128)(2,1)S(1)}, u32[]{:S(2)}, u32[]{:S(2)}) %collective-permute-start.43) | collective-permute-done | bytes 196640 | tf_op jit(solution)/shard_map/ppermute | solution.py:31
  235.8 3.8 %finish.2 = (f32[512,768]{1,0:T(8,128)}, bf16[512,768]{1,0:T(8,128)(2,1)}) custom-call(s32[1]{0:T(128)} %bitcast.core_ref, bf16[1024,768]{1,0:T(8,128)(2,1)} %copy-done.7, f32[1024,768]{1,0:T(8,128)} %get-tuple-element.260.full_ref, bf16[1024,768]{1,0:T(8,128)(2,1)} %get-tuple-element.261.out_ref, bf16[512,768]{1,0:T(8,128)(2,1)} %collective-permute-done.40.theirs_ref, ...), custom_call_target="tpu_custom_call" | custom-call | flops 4000000000 | bytes 8388608 | tf_op jit(solution)/shard_map/finish/pallas_call | solution.py:541
  239.6 4.1 %collective-permute-start.48 = (f32[1,1664]{1,0:T(1,128)S(1)}, f32[1,1664]{1,0:T(1,128)S(1)}, u32[]{:S(2)}, u32[]{:S(2)}) collective-permute-start(f32[1,1664]{1,0:T(1,128)S(1)} %add.155.refs_1_), channel_id=1, source_target_pairs={{0,16},{4,20},{8,24},{12,28},{16,0},{20,4},{24,8},{28,12},{1,17},{... | collective-permute-start | bytes 19976 | tf_op jit(solution)/shard_map/ppermute | solution.py:31
  243.8 4.0 %finish.3 = (f32[512,768]{1,0:T(8,128)}, bf16[512,768]{1,0:T(8,128)(2,1)}) custom-call(s32[1]{0:T(128)} %bitcast.core_ref, bf16[1024,768]{1,0:T(8,128)(2,1)} %copy-done.7, f32[1024,768]{1,0:T(8,128)} %get-tuple-element.260.full_ref, bf16[1024,768]{1,0:T(8,128)(2,1)} %get-tuple-element.261.out_ref, ...), custom_call_target="tpu_custom_call", output_to_operand_aliasing={{0}: (6, {}), {1}: (7, {})} | custom-call | flops 4000000000 | bytes 8388608 | tf_op jit(solution)/shard_map/finish/pallas_call | solution.py:541
  248.6 4.4 %adam.1 = (f32[1,1]{1,0:T(1,128)}, f32[3,96,192]{2,1,0:T(8,128)}, f32[3,96,192]{2,1,0:T(8,128)}, f32[3,96,192]{2,1,0:T(8,128)}, f32[192,96]{1,0:T(8,128)}, /*ind...) custom-call(s32[1]{0:T(128)} %bitcast.19.refs_0_, ...), custom_call_target="tpu_custom_call" | custom-call | tf_op jit(solution)/shard_map/adam/pallas_call | solution.py:629
  (271 shorter events, 104.3 us)
Async XLA Ops:
  22.6 18.3 %collective-permute-start.7 = (bf16[384,768]{1,0:T(8,128)(2,1)S(1)}, bf16[384,768]{1,0:T(8,128)(2,1)S(1)}, u32[]{:S(2)}, u32[]{:S(2)}) collective-permute-start(bf16[384,768]{1,0:T(8,128)(2,1)S(1)} %pad_maximum_fusion.6.qka_ref.voa_ref.att_ref), channel_id=1, source_target_pairs={{0,4},{4,0},{8,12},{12,8},{16,20},{20,16},{24,28},{28,24},{1,5},{5... | collective-permute-start | bytes 1769480 | tf_op jit(solution)/shard_map/ppermute | solution.py:31
  24.0 16.9 %collective-permute-start.8 = (bf16[384,768]{1,0:T(8,128)(2,1)S(1)}, bf16[384,768]{1,0:T(8,128)(2,1)S(1)}, u32[]{:S(2)}, u32[]{:S(2)}) collective-permute-start(bf16[384,768]{1,0:T(8,128)(2,1)S(1)} %pad_maximum_fusion.6.qka_ref.voa_ref.att_ref), channel_id=1, source_target_pairs={{0,2},{1,3},{2,0},{3,1},{4,6},{5,7},{6,4},{7,5},{8,10},{9,11},{10,... | collective-permute-start | bytes 1769480 | tf_op jit(solution)/shard_map/ppermute | solution.py:31
  25.6 15.2 %collective-permute-start.9 = (bf16[96,1280]{1,0:T(8,128)(2,1)S(1)}, bf16[96,1280]{1,0:T(8,128)(2,1)S(1)}, u32[]{:S(2)}, u32[]{:S(2)}) collective-permute-start(bf16[96,1280]{1,0:T(8,128)(2,1)S(1)} %pad_maximum_fusion.10), channel_id=1, source_target_pairs={{0,16},{4,20},{8,24},{12,28},{16,0},{20,4},{24,8},{28,12},{1,17},{... | collective-permute-start | bytes 737288 | tf_op jit(solution)/shard_map/ppermute | solution.py:31
  40.9 13.0 %collective-permute-start.13 = (bf16[192,1280]{1,0:T(8,128)(2,1)S(1)}, bf16[192,1280]{1,0:T(8,128)(2,1)S(1)}, u32[]{:S(2)}, u32[]{:S(2)}) collective-permute-start(bf16[192,1280]{1,0:T(8,128)(2,1)S(1)} %pad_maximum_fusion.7), channel_id=1, source_target_pairs={{0,8},{4,12},{8,0},{12,4},{16,24},{20,28},{24,16},{28,20},{1,9},{5... | collective-permute-start | bytes 1474568 | tf_op jit(solution)/shard_map/ppermute | solution.py:31
  41.7 12.3 %collective-permute-start.11 = (bf16[384,384]{1,0:T(8,128)(2,1)S(1)}, bf16[384,384]{1,0:T(8,128)(2,1)S(1)}, u32[]{:S(2)}, u32[]{:S(2)}) collective-permute-start(bf16[384,384]{1,0:T(8,128)(2,1)S(1)} %slice.164), channel_id=1, source_target_pairs={{0,2},{1,3},{2,0},{3,1},{4,6},{5,7},{6,4},{7,5},{8,10},{9,11},{10,... | collective-permute-start | bytes 884744 | tf_op jit(solution)/shard_map/ppermute | solution.py:31
  54.1 22.7 %collective-permute-start.15 = (bf16[384,1280]{1,0:T(8,128)(2,1)S(1)}, bf16[384,1280]{1,0:T(8,128)(2,1)S(1)}, u32[]{:S(2)}, u32[]{:S(2)}) collective-permute-start(bf16[384,1280]{1,0:T(8,128)(2,1)S(1)} %pad_maximum_fusion.4.own_ref.low_own_ref), channel_id=1, source_target_pairs={{0,4},{4,0},{8,12},{12,8},{16,20},{20,16},{24,28},{28,24},{1,5},{5... | collective-permute-start | bytes 2949128 | tf_op jit(solution)/shard_map/ppermute | solution.py:31
  55.4 22.3 %collective-permute-start.16 = (bf16[384,1280]{1,0:T(8,128)(2,1)S(1)}, bf16[384,1280]{1,0:T(8,128)(2,1)S(1)}, u32[]{:S(2)}, u32[]{:S(2)}) collective-permute-start(bf16[384,1280]{1,0:T(8,128)(2,1)S(1)} %pad_maximum_fusion.4.own_ref.low_own_ref), channel_id=1, source_target_pairs={{0,2},{1,3},{2,0},{3,1},{4,6},{5,7},{6,4},{7,5},{8,10},{9,11},{10,... | collective-permute-start | bytes 2949128 | tf_op jit(solution)/shard_map/ppermute | solution.py:31
  55.9 15.9 %collective-permute-start.17 = (bf16[4,1,96,256]{3,2,0,1:T(8,128)(2,1)S(1)}, bf16[4,1,96,256]{3,2,0,1:T(8,128)(2,1)S(1)}, u32[]{:S(2)}, u32[]{:S(2)}) collective-permute-start(bf16[4,1,96,256]{3,2,0,1:T(8,128)(2,1)S(1)} %maximum_bitcast_fusion), channel_id=1, source_target_pairs={{0,16},{4,20},{8,24},{12,28},{16,0},{20,4},{24,8},{28,12},{1,17},{... | collective-permute-start | bytes 589832 | tf_op jit(solution)/shard_map/ppermute | solution.py:31
  77.7 14.0 %collective-permute-start.19 = (bf16[512,768]{1,0:T(8,128)(2,1)S(1)}, bf16[512,768]{1,0:T(8,128)(2,1)}, u32[]{:S(2)}, u32[]{:S(2)}) collective-permute-start(bf16[512,768]{1,0:T(8,128)(2,1)S(1)} %get-tuple-element.191), channel_id=1, source_target_pairs={{0,1},{1,0},{2,3},{3,2},{4,5},{5,4},{6,7},{7,6},{8,9},{9,8},{10,11... | collective-permute-start | bytes 2359304 | tf_op jit(solution)/shard_map/ppermute | solution.py:31
  80.1 15.2 %collective-permute-start.22 = (bf16[384,768]{1,0:T(8,128)(2,1)}, bf16[384,768]{1,0:T(8,128)(2,1)S(1)}, u32[]{:S(2)}, u32[]{:S(2)}) collective-permute-start(bf16[384,768]{1,0:T(8,128)(2,1)} %slice.168), channel_id=1, source_target_pairs={{0,4},{4,0},{8,12},{12,8},{16,20},{20,16},{24,28},{28,24},{1,5},{5... | collective-permute-start | bytes 1769480 | tf_op jit(solution)/shard_map/ppermute | solution.py:31
  82.2 12.1 %collective-permute-start.21 = (bf16[384,512]{1,0:T(8,128)(2,1)S(1)}, bf16[384,512]{1,0:T(8,128)(2,1)S(1)}, u32[]{:S(2)}, u32[]{:S(2)}) collective-permute-start(bf16[384,512]{1,0:T(8,128)(2,1)S(1)} %slice.167), channel_id=1, source_target_pairs={{0,2},{1,3},{2,0},{3,1},{4,6},{5,7},{6,4},{7,5},{8,10},{9,11},{10,... | collective-permute-start | bytes 1179656 | tf_op jit(solution)/shard_map/ppermute | solution.py:31
  112.7 20.0 %collective-permute-start.26 = (bf16[768,512]{1,0:T(8,128)(2,1)S(1)}, bf16[768,512]{1,0:T(8,128)(2,1)S(1)}, u32[]{:S(2)}, u32[]{:S(2)}) collective-permute-start(bf16[768,512]{1,0:T(8,128)(2,1)S(1)} %convolution_convert_fusion.2), channel_id=1, source_target_pairs={{0,2},{1,3},{2,0},{3,1},{4,6},{5,7},{6,4},{7,5},{8,10},{9,11},{10,... | collective-permute-start | bytes 2359304 | tf_op jit(solution)/shard_map/ppermute | solution.py:31
  120.8 30.4 %collective-permute-start.27 = (bf16[384,1024]{1,0:T(8,128)(2,1)S(1)}, bf16[384,1024]{1,0:T(8,128)(2,1)S(1)}, u32[]{:S(2)}, u32[]{:S(2)}) collective-permute-start(bf16[384,1024]{1,0:T(8,128)(2,1)S(1)} %convolution_convert_fusion.6), channel_id=1, source_target_pairs={{0,4},{4,0},{8,12},{12,8},{16,20},{20,16},{24,28},{28,24},{1,5},{5... | collective-permute-start | bytes 2359304 | tf_op jit(solution)/shard_map/ppermute | solution.py:31
  129.5 43.0 %collective-permute-start.28 = (bf16[384,1024]{1,0:T(8,128)(2,1)S(1)}, bf16[384,1024]{1,0:T(8,128)(2,1)S(1)}, u32[]{:S(2)}, u32[]{:S(2)}) collective-permute-start(bf16[384,1024]{1,0:T(8,128)(2,1)S(1)} %convolution_convert_fusion.5), channel_id=1, source_target_pairs={{0,4},{4,0},{8,12},{12,8},{16,20},{20,16},{24,28},{28,24},{1,5},{5... | collective-permute-start | bytes 2359304 | tf_op jit(solution)/shard_map/ppermute | solution.py:31
  151.5 21.1 %collective-permute-start.29 = (bf16[384,512]{1,0:T(8,128)(2,1)S(1)}, bf16[384,512]{1,0:T(8,128)(2,1)S(1)}, u32[]{:S(2)}, u32[]{:S(2)}) collective-permute-start(bf16[384,512]{1,0:T(8,128)(2,1)S(1)} %slice.266), channel_id=1, source_target_pairs={{0,4},{4,0},{8,12},{12,8},{16,20},{20,16},{24,28},{28,24},{1,5},{5... | collective-permute-start | bytes 1179656 | tf_op jit(solution)/shard_map/ppermute | solution.py:31
  152.9 19.7 %collective-permute-start.31 = (bf16[384,512]{1,0:T(8,128)(2,1)S(1)}, bf16[384,512]{1,0:T(8,128)(2,1)S(1)}, u32[]{:S(2)}, u32[]{:S(2)}) collective-permute-start(bf16[384,512]{1,0:T(8,128)(2,1)S(1)} %slice.267), channel_id=1, source_target_pairs={{0,2},{1,3},{2,0},{3,1},{4,6},{5,7},{6,4},{7,5},{8,10},{9,11},{10,... | collective-permute-start | bytes 1179656 | tf_op jit(solution)/shard_map/ppermute | solution.py:31
  158.9 13.7 %collective-permute-start.30 = (bf16[384,384]{1,0:T(8,128)(2,1)S(1)}, bf16[384,384]{1,0:T(8,128)(2,1)S(1)}, u32[]{:S(2)}, u32[]{:S(2)}) collective-permute-start(bf16[384,384]{1,0:T(8,128)(2,1)S(1)} %slice.172), channel_id=1, source_target_pairs={{0,4},{4,0},{8,12},{12,8},{16,20},{20,16},{24,28},{28,24},{1,5},{5... | collective-permute-start | bytes 884744 | tf_op jit(solution)/shard_map/ppermute | solution.py:31
  160.1 25.5 %collective-permute-start.34 = (bf16[768,384]{1,0:T(8,128)(2,1)}, bf16[768,384]{1,0:T(8,128)(2,1)S(1)}, u32[]{:S(2)}, u32[]{:S(2)}) collective-permute-start(bf16[768,384]{1,0:T(8,128)(2,1)} %get-tuple-element.238), channel_id=1, source_target_pairs={{0,2},{1,3},{2,0},{3,1},{4,6},{5,7},{6,4},{7,5},{8,10},{9,11},{10,... | collective-permute-start | bytes 1769480 | tf_op jit(solution)/shard_map/ppermute | solution.py:31
  173.0 18.0 %collective-permute-start.35 = (bf16[384,512]{1,0:T(8,128)(2,1)S(1)}, bf16[384,512]{1,0:T(8,128)(2,1)S(1)}, u32[]{:S(2)}, u32[]{:S(2)}) collective-permute-start(bf16[384,512]{1,0:T(8,128)(2,1)S(1)} %slice.265), channel_id=1, source_target_pairs={{0,2},{1,3},{2,0},{3,1},{4,6},{5,7},{6,4},{7,5},{8,10},{9,11},{10,... | collective-permute-start | bytes 1179656 | tf_op jit(solution)/shard_map/ppermute | solution.py:31
  175.8 15.1 %collective-permute-start.33 = (bf16[384,384]{1,0:T(8,128)(2,1)S(1)}, bf16[384,384]{1,0:T(8,128)(2,1)S(1)}, u32[]{:S(2)}, u32[]{:S(2)}) collective-permute-start(bf16[384,384]{1,0:T(8,128)(2,1)S(1)} %add_convert_fusion), channel_id=1, source_target_pairs={{0,2},{1,3},{2,0},{3,1},{4,6},{5,7},{6,4},{7,5},{8,10},{9,11},{10,... | collective-permute-start | bytes 884744 | tf_op jit(solution)/shard_map/ppermute | solution.py:31
  185.7 15.0 %collective-permute-start.36 = (bf16[384,384]{1,0:T(8,128)(2,1)S(1)}, bf16[384,384]{1,0:T(8,128)(2,1)S(1)}, u32[]{:S(2)}, u32[]{:S(2)}) collective-permute-start(bf16[384,384]{1,0:T(8,128)(2,1)S(1)} %slice.269), channel_id=1, source_target_pairs={{0,4},{4,0},{8,12},{12,8},{16,20},{20,16},{24,28},{28,24},{1,5},{5... | collective-permute-start | bytes 884744 | tf_op jit(solution)/shard_map/ppermute | solution.py:31
  203.8 29.4 %collective-permute-start.40 = (bf16[512,768]{1,0:T(8,128)(2,1)}, bf16[512,768]{1,0:T(8,128)(2,1)}, u32[]{:S(2)}, u32[]{:S(2)}) collective-permute-start(bf16[512,768]{1,0:T(8,128)(2,1)} %constant_dynamic-slice_fusion), channel_id=1, source_target_pairs={{0,1},{1,0},{2,3},{3,2},{4,5},{5,4},{6,7},{7,6},{8,9},{9,8},{10,11... | collective-permute-start | bytes 2359304 | tf_op jit(solution)/shard_map/ppermute | solution.py:31
  203.8 16.6 %collective-permute-start.43 = (bf16[96,1024]{1,0:T(8,128)(2,1)S(1)}, bf16[96,1024]{1,0:T(8,128)(2,1)S(1)}, u32[]{:S(2)}, u32[]{:S(2)}) collective-permute-start(bf16[96,1024]{1,0:T(8,128)(2,1)S(1)} %slice.270), channel_id=1, source_target_pairs={{0,16},{4,20},{8,24},{12,28},{16,0},{20,4},{24,8},{28,12},{1,17},{... | collective-permute-start | bytes 589832 | tf_op jit(solution)/shard_map/ppermute | solution.py:31
  211.5 12.4 %collective-permute-start.42 = (bf16[96,768]{1,0:T(8,128)(2,1)S(1)}, bf16[96,768]{1,0:T(8,128)(2,1)S(1)}, u32[]{:S(2)}, u32[]{:S(2)}) collective-permute-start(bf16[96,768]{1,0:T(8,128)(2,1)S(1)} %slice.272), channel_id=1, source_target_pairs={{0,16},{4,20},{8,24},{12,28},{16,0},{20,4},{24,8},{28,12},{1,17},{... | collective-permute-start | bytes 442376 | tf_op jit(solution)/shard_map/ppermute | solution.py:31
  (67 other events, 557.0 us)

commit v2 on v1

--- a/solution.py
+++ b/solution.py
@@ -490,10 +490,23 @@
     low_ref[...] = total.astype(LOW)
 
 
-def heads_grad_kernel(rows_ref, grad_ref, qk_ref, v_ref, ctx_ref, out_ref, vo_ref):
+def heads_grad_kernel(
+    rows_ref, grad_ref, qk_ref, v_ref, ctx_ref, near_ref, far_ref, vo_ref
+):
     width = v_ref.shape[1]
     rows = flip(rows_ref[...]).astype(LOW)
-    out_ref[...] = nn(rows, qk_ref[...]).astype(LOW)
+    qk = nn(rows, qk_ref[...]).astype(LOW)
+    step, half = qk.shape[0], near_ref.shape[0]
+    for i in range(D // step):
+
+        @pl.when(pl.program_id(0) == i)
+        def _(start=i * step):
+            near = max(min(half - start, step), 0)
+            if near:
+                near_ref[start : start + near] = qk[:near]
+            if near < step:
+                far_ref[start + near - half : start + step - half] = qk[near:]
+
     vo_ref[:, :width] = nn(rows, v_ref[...]).astype(LOW)
     vo_ref[:, width:] = nn(flip(grad_ref[...]).astype(LOW), ctx_ref[...]).astype(LOW)
 
@@ -501,17 +514,17 @@
 def heads_grad(rows, grad, dqk, dv, context):
     half, pair = D // 2, dqk.shape[1]
     split = pl.BlockSpec((L, 256), lambda i: (0, i))
-    qk, vo = pl.pallas_call(
+    held = pl.BlockSpec((half, pair), lambda i: (0, 0))
+    return pl.pallas_call(
         heads_grad_kernel,
         grid=(D // 256,),
         in_specs=[split, split] + [held_once(g) for g in (dqk, dv, context)],
-        out_specs=[pl.BlockSpec((256, pair), lambda i: (i, 0))] * 2,
-        out_shape=[pltpu.HBM((D, pair), LOW)] * 2,
+        out_specs=[held, held, pl.BlockSpec((256, pair), lambda i: (i, 0))],
+        out_shape=[pltpu.HBM((half, pair), LOW)] * 2 + [pltpu.HBM((D, pair), LOW)],
         compiler_params=pltpu.CompilerParams(vmem_limit_bytes=24 << 20),
         cost_estimate=SMALL,
         name="heads_grad",
     )(rows, grad, dqk, dv, context)
-    return qk[:half], qk[half:], vo
 
 
 def in_order(value, mover):
@@ -524,38 +537,33 @@
 
 
 def finish_kernel(
-    core_ref, one_ref, full_ref, out_ref, theirs_ref, mover_ref, *refs
+    core_ref, one_ref, full_ref, out_ref, theirs_ref, mover_ref, grad_ref, low_ref
 ):
-    grad_ref, low_ref = refs[-2:]
     mover = mover_ref[...]
     grad = one_ref[...].astype(FULL) + full_ref[...] + theirs_ref[...].astype(FULL)
     grad_ref[...] = in_order(grad, mover)
     low_ref[...] = nt(out_ref[...], mover).astype(LOW)
 
 
-def finish(part, done, core, grad_one, part_full, layer_output, theirs, mover):
+def finish(core, grad_one, part_full, layer_output, theirs, mover):
     rows = theirs.shape[0]
     steps = rows // QB
-    mine = pl.BlockSpec((QB, D), lambda i, c: (c[0] * steps + part, 0))
-    plain = pl.BlockSpec((QB, D), lambda i, c: (part, 0))
+    mine = pl.BlockSpec((QB, D), lambda i, c: (c[0] * steps + i, 0))
+    plain = pl.BlockSpec((QB, D), lambda i, c: (i, 0))
     return pl.pallas_call(
         finish_kernel,
         grid_spec=pltpu.PrefetchScalarGridSpec(
             num_scalar_prefetch=1,
-            grid=(1,),
-            in_specs=[mine, mine, mine, plain, held_once(mover)]
-            + [pl.BlockSpec(memory_space=pl.ANY)] * len(done),
+            grid=(steps,),
+            in_specs=[mine, mine, mine, plain, held_once(mover)],
             out_specs=[plain, plain],
         ),
         out_shape=[
             jax.ShapeDtypeStruct((rows, D), FULL), jax.ShapeDtypeStruct((rows, D), LOW)
         ],
-        input_output_aliases={6 + i: i for i in range(len(done))},
-        cost_estimate=pl.CostEstimate(
-            flops=4 * 10**9, bytes_accessed=8 << 20, transcendentals=0
-        ),
+        cost_estimate=SMALL,
         name="finish",
-    )(core, grad_one, pinned(part_full), pinned(layer_output), theirs, mover, *done)
+    )(core, grad_one, pinned(part_full), pinned(layer_output), theirs, mover)
 
 
 def last_kernel(kept_ref, received_ref, square_ref, sum_ref, total_ref):
@@ -835,17 +843,20 @@
     gate_far = gate_sum[:, hid:].astype(LOW)
     gate_x = swap(gate_far, "narrow", 2)
     qk_near2, qk_send2, vo_send = heads_grad(inputs, grad_one_low, after(dqk2, gate_far), dv2, context[1])
-    vo_x = swap(vo_send, "narrow", 2)
     qk_y2 = swap(qk_send2, "wide", 1)
     back = near[::-1]
     q, k, v, _, lse = saved[0]
-    dqk1, dv1 = attend_backward(q, k, v, lse, after(dctx1, vo_send, qk_send2), cosine, sine)
-    dqk1, dv1, up_y, down_y, qk_y2, gate_x = lax.optimization_barrier(
-        (dqk1, dv1, up_y, down_y, qk_y2, gate_x)
+    up_y, vo_done = lax.optimization_barrier((up_y, vo_send))
+    up_sum = add(up_own, up_y)
+    up_far = up_sum[:, hid:].astype(LOW)
+    dctx1, up_far, vo_done = lax.optimization_barrier((dctx1, up_far, vo_done))
+    up_x = swap(up_far, "narrow", 2)
+    vo_x = swap(vo_done, "narrow", 2)
+    dqk1, dv1 = attend_backward(q, k, v, lse, dctx1, cosine, sine)
+    dqk1, dv1, down_y, qk_y2, gate_x = lax.optimization_barrier(
+        (dqk1, dv1, down_y, qk_y2, gate_x)
     )
     early = narrow_down(add(down_sum[:half], down_y), back[:1])
-    up_sum = add(up_own, up_y)
-    up_x = swap(up_sum[:, hid:].astype(LOW), "narrow", 2)
     qk_near1, qk_send1, vo_own = heads_grad(inputs, grad_one_low, dqk1, dv1, context[0])
     qk_y1 = swap(qk_send1, "wide", 1)
     qk_far = add(qk_near2, qk_y2).astype(LOW)
@@ -853,15 +864,15 @@
     vo_sum = add(vo_own, vo_x)
     vo_far = vo_sum[half:].astype(LOW)
     vo_y = swap(vo_far, "wide", 1)
+    early_red = narrow_down(early, back[1:])
     late = jnp.concatenate([add(gate_sum[:, :hid], gate_x), add(up_sum[:, :hid], up_x)], axis=1)
-    early_red = narrow_down(early, back[1:])
     dqk1, vo_sum, late = lax.optimization_barrier((dqk1, vo_sum, late))
+    late = narrow_down(late, back[:1])
     part_full, part_low = by_rows(
         input_kernel, "inputs", [dqk1, dv1, dqk2, dv2],
-        [att, att_y, att_x, qk_corner, vo_corner], [full_d, low_d], step=128,
+        [att, att_y, att_x, qk_corner, vo_corner], [full_d, low_d],
         scratch=[pltpu.VMEM((2, D, 3 * cols), LOW)],
     )
-    late = narrow_down(late, back[:1])
     theirs = lax.dynamic_slice_in_dim(part_low, (1 - core) * rows, rows, axis=0)
     theirs = swap(theirs, "narrow", 1)
     qk_sum = add(qk_near1, qk_y1)
@@ -871,26 +882,25 @@
     gain_rest = (gain_grads - gain_low.astype(FULL)).astype(LOW)
     gain_grads = nt(jnp.concatenate([gain_low, gain_rest], axis=0), mover)
     gain_grads = gain_grads[:2] + gain_grads[2:]
-    last, early_red, late, gain_grads, part_full = lax.optimization_barrier(
-        (last, early_red, late, gain_grads, part_full)
+    last, early_red, late, gain_grads = lax.optimization_barrier(
+        (last, early_red, late, gain_grads)
     )
     last = narrow_down(last, back[:1])
     late_red = narrow_down(late, back[1:])
     early_square = jnp.sum(early_red * early_red) + jnp.sum(late_red * late_red)
     last = narrow_down(last, back[1:-1])
-    att_red, square = last_sum(
-        last[:block], swap(last[block:].astype(LOW), "wide", back[-1]),
-        jnp.full((1, 128), early_square, FULL),
-    )
+    received = swap(last[block:].astype(LOW), "wide", back[-1])
+    input_grad, layer_output = finish(
+        jnp.full((1,), core, jnp.int32), grad_one_low, part_full, layer_output, theirs, mover
+    )
+    received, early_square, input_grad, layer_output = lax.optimization_barrier(
+        (received, early_square, input_grad, layer_output)
+    )
+    att_red, square = last_sum(last[:block], received, jnp.full((1, 128), early_square, FULL))
 
     square = square + swap(square, "narrow", 1)
     message = jnp.concatenate([gain_grads.reshape(1, 2 * D), square], axis=1)
     message = message + swap(message, "narrow", 2)
-    which, done = jnp.full((1,), core, jnp.int32), ()
-    theirs = after(theirs, message)
-    for part in range(rows // QB):
-        done = finish(part, done, which, grad_one_low, part_full, layer_output, theirs, mover)
-    input_grad, layer_output = done
     for bit in bits[::-1][:-1]:
         message = message + swap(message, "wide", bit)
     received = swap(message, "wide", bits[0])

time: 254 us -> 254 us (level)
  waiting for transfers between devices: 41.2 us -> 47.8 us
  starting transfers between devices: 61.8 us -> 57.3 us
  Pallas kernels: 112 us -> 109 us
    ppermute x49, waiting for transfers between devices: 41.2 us -> 47.8 us  [swap(): return lax.ppermute(value, axis, [(i, i ^ bit) for i in range(size)])]
    unnamed x86 -> x108, local copies, waits for them, and re-layouts: 1.97 us -> 7.09 us
    ppermute x49, starting transfers between devices: 61.8 us -> 57.3 us  [swap(): return lax.ppermute(value, axis, [(i, i ^ bit) for i in range(size)])]
    pallas_call x2 -> x1, Pallas kernels: 7.83 us -> 5.44 us  [finish(): pl.pallas_call(finish_kernel, grid_spec=pltpu.PrefetchScalarGridSpec(num_...]
  transfers between devices with their start and end apart: 49 -> 49, of which waited for: 17 -> 17; matrix products, arithmetic and copies ran while one was open for 12% -> 10% of each run, Pallas kernels for 37% -> 35%
where the time goes in v2:
time: 254 us; the launch traced here: 253 us
  Pallas kernels  109 us (43%)
  starting transfers between devices  57.3 us (23%)
  waiting for transfers between devices  47.8 us (19%)
  other arithmetic  14.2 us (6%)
  local copies, waits for them, and re-layouts  12 us (5%)
  matrix products  9.3 us (4%)
  between operations  3.35 us (1%)
    ppermute x49, starting transfers between devices, swap(): return lax.ppermute(value, axis, [(i, i ^ bit) for i in range(size)])  57.3 us
    ppermute x49, waiting for transfers between devices, swap(): return lax.ppermute(value, axis, [(i, i ^ bit) for i in range(size)])  47.8 us
    pallas_call x8, Pallas kernels, by_rows(): pl.pallas_call(kernel, grid=(L // step,), in_specs=specs + list(held_spec...  47.8 us
    pallas_call x2, Pallas kernels, attend_backward(): pl.pallas_call(attend_back_kernel, grid=(heads,), in_specs=[by_head((1, L...  23.3 us
    pallas_call x2, Pallas kernels, attend_forward(): pl.pallas_call(attend_kernel, grid=(1,), in_specs=list(specs), out_specs=...  18.1 us
    pallas_call x2, Pallas kernels, heads_grad(): pl.pallas_call(heads_grad_kernel, grid=(D // 256,), in_specs=[split, spli...  8.3 us
    unnamed x108, local copies, waits for them, and re-layouts  7.09 us
    dot_general x6, matrix products, tn(): lax.dot_general(rows, grads, (((0,), (0,)), ((), ())), preferred_element_...  5.99 us
  transfers between devices with their start and end apart: 49, of which 17 were waited for; matrix products, arithmetic and copies ran while one was open for 10% of the time, Pallas kernels for 35%

profile of v2, /device:TPU:0, one launch (start us, length us, event | category | flops | bytes accessed | tf_op | source)
XLA Modules:
  0.0 253.2 jit_solution(14434771427831472831)
XLA Ops:
  2.9 4.1 %collective-permute-start = (bf16[96,768]{1,0:T(8,128)(2,1)S(1)}, bf16[96,768]{1,0:T(8,128)(2,1)S(1)}, u32[]{:S(2)}, u32[]{:S(2)}) collective-permute-start(bf16[96,768]{1,0:T(8,128)(2,1)S(1)} %pad_maximum_fusion.11), channel_id=1, source_target_pairs={{0,16},{4,20},{8,24},{12,28},{16,0},{20,4},{24,8},{28,12},{1,17},{... | collective-permute-start | bytes 442376 | tf_op jit(solution)/shard_map/ppermute | solution.py:31
  31.2 9.6 %collective-permute-done.9 = bf16[96,1280]{1,0:T(8,128)(2,1)S(1)} collective-permute-done((bf16[96,1280]{1,0:T(8,128)(2,1)S(1)}, bf16[96,1280]{1,0:T(8,128)(2,1)S(1)}, u32[]{:S(2)}, u32[]{:S(2)}) %collective-permute-start.9) | collective-permute-done | bytes 245792 | tf_op jit(solution)/shard_map/ppermute | solution.py:31
  44.4 9.2 %attend_forward.2 = (bf16[3,1024,64]{2,1,0:T(8,128)(2,1)}, bf16[3,1024,64]{2,1,0:T(8,128)(2,1)}, bf16[3,1024,64]{2,1,0:T(8,128)(2,1)}, bf16[1024,192]{1,0:T(8,128)(2,1)S(1)}, f32[3,1,1024]{2,1,0:T(1,128)}) custom-call(bf16[1024,768]{1,0:T(8,128)(2,1)S(1)} %pad_maximum_fusion.rows_ref, bf16[384,768]{1,0:T(8,128)(2,1)S(1)} %pad_maximum_fusion.6.qka_ref.voa_ref.att_ref, ...), custom_call_target="tpu_custom_call" | custom-call | flops 1000000 | bytes 10000 | tf_op jit(solution)/shard_map/attend_forward/pallas_call | solution.py:180
  59.4 9.0 %attend_forward.3 = (bf16[3,1024,64]{2,1,0:T(8,128)(2,1)}, bf16[3,1024,64]{2,1,0:T(8,128)(2,1)}, bf16[3,1024,64]{2,1,0:T(8,128)(2,1)}, bf16[1024,192]{1,0:T(8,128)(2,1)S(1)}, f32[3,1,1024]{2,1,0:T(1,128)}) custom-call(bf16[1024,768]{1,0:T(8,128)(2,1)S(1)} %pad_maximum_fusion.rows_ref, bf16[384,768]{1,0:T(8,128)(2,1)S(1)} %collective-permute-done.8.qka_ref.voa_ref.x_ref, ...), custom_call_target="tpu_custom_call" | custom-call | flops 1000000 | bytes 10000 | tf_op jit(solution)/shard_map/attend_forward/pallas_call | solution.py:180
  68.4 3.6 %project.1.mine_ref = bf16[1024,768]{1,0:T(8,128)(2,1)S(1)} custom-call(bf16[1024,192]{1,0:T(8,128)(2,1)S(1)} %get-tuple-element.175.one_ref.ctx_ref, bf16[1024,192]{1,0:T(8,128)(2,1)S(1)} %get-tuple-element.184.two_ref.ctx_ref, bf16[384,768]{1,0:T(8,128)(2,1)} %copy-done.2, bf16[384,768]{1,0:T(8,128)(2,1)} %copy-done.3, bf16[384,768]{1,0:T(8,128)(2,1)} %copy-done.4, ...), custom_call_target="tpu_custom_call" | custom-call | flops 1000000 | bytes 10000 | tf_op jit(solution)/shard_map/project/pallas_call | solution.py:303
  72.1 4.7 %collective-permute-done.15.y_ref.low_y_ref = bf16[384,1280]{1,0:T(8,128)(2,1)S(1)} collective-permute-done((bf16[384,1280]{1,0:T(8,128)(2,1)S(1)}, bf16[384,1280]{1,0:T(8,128)(2,1)S(1)}, u32[]{:S(2)}, u32[]{:S(2)}) %collective-permute-start.15) | collective-permute-done | bytes 983072 | tf_op jit(solution)/shard_map/ppermute | solution.py:31
  85.3 6.3 %enter.1 = (bf16[1024,768]{1,0:T(8,128)(2,1)}, f32[1024,1]{1,0:T(8,128)}, bf16[1024,768]{1,0:T(8,128)(2,1)S(1)}, bf16[1024,512]{1,0:T(8,128)(2,1)}, bf16[1024,51...) custom-call(bf16[1024,768]{1,0:T(8,128)(2,1)} %copy-done, ...), custom_call_target="tpu_custom_call" | custom-call | flops 1000000 | bytes 10000 | tf_op jit(solution)/shard_map/enter/pallas_call | solution.py:303
  96.8 8.5 %rest.1 = (bf16[1024,512]{1,0:T(8,128)(2,1)}, bf16[1024,512]{1,0:T(8,128)(2,1)}, bf16[1024,512]{1,0:T(8,128)(2,1)S(1)}, bf16[1024,768]{1,0:T(8,128)(2,1)S(1)}, b...) custom-call(bf16[1024,768]{1,0:T(8,128)(2,1)S(1)} %get-tuple-element.198.hidden_ref, ...), custom_call_target="tpu_custom_call" | custom-call | flops 1000000 | bytes 10000 | tf_op jit(solution)/shard_map/rest/pallas_call | solution.py:303
  106.3 3.5 %collective-permute-done.23.theirs_ref = bf16[1024,768]{1,0:T(8,128)(2,1)} collective-permute-done((bf16[1024,768]{1,0:T(8,128)(2,1)S(1)}, bf16[1024,768]{1,0:T(8,128)(2,1)}, u32[]{:S(2)}, u32[]{:S(2)}) %collective-permute-start.23) | collective-permute-done | bytes 1572896 | tf_op jit(solution)/shard_map/ppermute | solution.py:31
  109.8 5.1 %turn.1 = (bf16[1024,768]{1,0:T(8,128)(2,1)}, bf16[1024,768]{1,0:T(8,128)(2,1)S(1)}, f32[1,768]{1,0:T(1,128)S(1)}) custom-call(bf16[1024,768]{1,0:T(8,128)(2,1)} %get-tuple-element.190.normed_ref, bf16[1024,768]{1,0:T(8,128)(2,1)S(1)} %get-tuple-element.203.mine_ref, bf16[1024,768]{1,0:T(8,128)(2,1)} %collective-permute-done.23.theirs_ref, ...), custom_call_target="tpu_custom_call" | custom-call | flops 1000000 | bytes 10000 | tf_op jit(solution)/shard_map/turn/pallas_call | solution.py:303
  117.5 5.5 %back.1 = (bf16[1024,1024]{1,0:T(8,128)(2,1)S(1)}, bf16[1024,1024]{1,0:T(8,128)(2,1)S(1)}) custom-call(bf16[1024,768]{1,0:T(8,128)(2,1)S(1)} %get-tuple-element.206.low_ref.grad_two_ref, bf16[1024,512]{1,0:T(8,128)(2,1)} %get-tuple-element.207.gate1_ref, bf16[1024,512]{1,0:T(8,128)(2,1)} %get-tuple-element.208.up1_ref, ...), custom_call_target="tpu_custom_call" | custom-call | flops 1000000 | bytes 10000 | tf_op jit(solution)/shard_map/back/pallas_call | solution.py:303
  126.1 6.2 %mid.1 = (bf16[512,768]{1,0:T(8,128)(2,1)S(1)}, bf16[512,768]{1,0:T(8,128)(2,1)S(1)}) custom-call(bf16[1024,1024]{1,0:T(8,128)(2,1)S(1)} %get-tuple-element.214.gg_ref, bf16[1024,1024]{1,0:T(8,128)(2,1)S(1)} %get-tuple-element.213.ug_ref, bf16[768,1024]{1,0:T(8,128)(2,1)} %get-tuple-element.215.own_ref, bf16[768,1024]{1,0:T(8,128)(2,1)} %get-tuple-element.216.other_ref), custom_call_target="tpu_custom_call" | custom-call | flops 1000000 | bytes 10000 | tf_op jit(solution)/shard_map/mid/pallas_call | solution.py:303
  137.0 6.6 %leave.1 = (bf16[1024,768]{1,0:T(8,128)(2,1)S(1)}, bf16[1024,192]{1,0:T(8,128)(2,1)}, bf16[1024,192]{1,0:T(8,128)(2,1)}, f32[1,768]{1,0:T(1,128)S(1)}) custom-call(bf16[1024,768]{1,0:T(8,128)(2,1)S(1)} %get-tuple-element.206.low_ref.grad_two_ref, bf16[512,768]{1,0:T(8,128)(2,1)S(1)} %get-tuple-element.219.mine_top_ref, ...), custom_call_target="tpu_custom_call" | custom-call | flops 1000000 | bytes 10000 | tf_op jit(solution)/shard_map/leave/pallas_call | solution.py:303
  143.6 11.9 %attend_backward.2 = (bf16[1024,384]{1,0:T(8,128)(2,1)S(1)}, bf16[1024,192]{1,0:T(8,128)(2,1)S(1)}) custom-call(bf16[3,1024,64]{2,1,0:T(8,128)(2,1)} %get-tuple-element.232.q_ref, bf16[3,1024,64]{2,1,0:T(8,128)(2,1)} %get-tuple-element.233.k_ref, bf16[3,1024,64]{2,1,0:T(8,128)(2,1)} %get-tuple-element.234.v_ref, f32[3,1,1024]{2,1,0:T(1,128)} %get-tuple-element.235.lse_ref, ...), custom_call_target="tpu_custom_call" | custom-call | flops 1000000 | bytes 10000 | tf_op jit(solution)/shard_map/attend_backward/pallas_call | solution.py:251
  157.9 4.1 %heads_grad.2 = (bf16[384,384]{1,0:T(8,128)(2,1)}, bf16[384,384]{1,0:T(8,128)(2,1)}, bf16[768,384]{1,0:T(8,128)(2,1)}) custom-call(bf16[1024,768]{1,0:T(8,128)(2,1)S(1)} %copy-done.1, bf16[1024,768]{1,0:T(8,128)(2,1)S(1)} %get-tuple-element.224.grad_ref.one_ref, bf16[1024,384]{1,0:T(8,128)(2,1)S(1)} %get-tuple-element.242.qk_ref.qk2_ref, ...), custom_call_target="tpu_custom_call" | custom-call | flops 1000000 | bytes 10000 | tf_op jit(solution)/shard_map/heads_grad/pallas_call | solution.py:518
  166.8 11.5 %attend_backward.3 = (bf16[1024,384]{1,0:T(8,128)(2,1)S(1)}, bf16[1024,192]{1,0:T(8,128)(2,1)S(1)}) custom-call(bf16[3,1024,64]{2,1,0:T(8,128)(2,1)} %get-tuple-element.225.q_ref, bf16[3,1024,64]{2,1,0:T(8,128)(2,1)} %get-tuple-element.226.k_ref, bf16[3,1024,64]{2,1,0:T(8,128)(2,1)} %get-tuple-element.227.v_ref, f32[3,1,1024]{2,1,0:T(1,128)} %get-tuple-element.228.lse_ref, ...), custom_call_target="tpu_custom_call" | custom-call | flops 1000000 | bytes 10000 | tf_op jit(solution)/shard_map/attend_backward/pallas_call | solution.py:251
  180.7 4.2 %heads_grad.3 = (bf16[384,384]{1,0:T(8,128)(2,1)}, bf16[384,384]{1,0:T(8,128)(2,1)}, bf16[768,384]{1,0:T(8,128)(2,1)}) custom-call(bf16[1024,768]{1,0:T(8,128)(2,1)S(1)} %copy-done.1, bf16[1024,768]{1,0:T(8,128)(2,1)S(1)} %get-tuple-element.224.grad_ref.one_ref, bf16[1024,384]{1,0:T(8,128)(2,1)S(1)} %get-tuple-element.271.qk_ref.qk1_ref, ...), custom_call_target="tpu_custom_call" | custom-call | flops 1000000 | bytes 10000 | tf_op jit(solution)/shard_map/heads_grad/pallas_call | solution.py:518
  186.5 3.4 %collective-permute-start.38 = (bf16[96,512]{1,0:T(8,128)(2,1)S(1)}, bf16[96,512]{1,0:T(8,128)(2,1)S(1)}, u32[]{:S(2)}, u32[]{:S(2)}) collective-permute-start(bf16[96,512]{1,0:T(8,128)(2,1)S(1)} %slice.255), channel_id=1, source_target_pairs={{0,16},{4,20},{8,24},{12,28},{16,0},{20,4},{24,8},{28,12},{1,17},{... | collective-permute-start | bytes 294920 | tf_op jit(solution)/shard_map/ppermute | solution.py:31
  192.5 6.0 %inputs.1 = (f32[1024,768]{1,0:T(8,128)}, bf16[1024,768]{1,0:T(8,128)(2,1)S(1)}) custom-call(bf16[1024,384]{1,0:T(8,128)(2,1)S(1)} %get-tuple-element.271.qk_ref.qk1_ref, bf16[1024,192]{1,0:T(8,128)(2,1)S(1)} %get-tuple-element.254.v_ref.v1_ref, bf16[1024,384]{1,0:T(8,128)(2,1)S(1)} %get-tuple-element.242.qk_ref.qk2_ref, ...), custom_call_target="tpu_custom_call" | custom-call | flops 1000000 | bytes 10000 | tf_op jit(solution)/shard_map/inputs/pallas_call | solution.py:303
  207.9 4.3 %collective-permute-start.41 = (bf16[96,768]{1,0:T(8,128)(2,1)S(1)}, bf16[96,768]{1,0:T(8,128)(2,1)S(1)}, u32[]{:S(2)}, u32[]{:S(2)}) collective-permute-start(bf16[96,768]{1,0:T(8,128)(2,1)S(1)} %slice.254), channel_id=1, source_target_pairs={{0,16},{4,20},{8,24},{12,28},{16,0},{20,4},{24,8},{28,12},{1,17},{... | collective-permute-start | bytes 442376 | tf_op jit(solution)/shard_map/ppermute | solution.py:31
  212.2 5.5 %collective-permute-done.42 = bf16[96,1024]{1,0:T(8,128)(2,1)S(1)} collective-permute-done((bf16[96,1024]{1,0:T(8,128)(2,1)S(1)}, bf16[96,1024]{1,0:T(8,128)(2,1)S(1)}, u32[]{:S(2)}, u32[]{:S(2)}) %collective-permute-start.42) | collective-permute-done | bytes 196640 | tf_op jit(solution)/shard_map/ppermute | solution.py:31
  222.3 5.4 %finish.1 = (f32[512,768]{1,0:T(8,128)}, bf16[512,768]{1,0:T(8,128)(2,1)}) custom-call(s32[1]{0:T(128)} %bitcast.18.core_ref, bf16[1024,768]{1,0:T(8,128)(2,1)} %copy-done.5, f32[1024,768]{1,0:T(8,128)} %get-tuple-element.272.full_ref, bf16[1024,768]{1,0:T(8,128)(2,1)} %get-tuple-element.273.out_ref, bf16[512,768]{1,0:T(8,128)(2,1)} %copy-done.42, ...), custom_call_target="tpu_custom_call" | custom-call | flops 1000000 | bytes 10000 | tf_op jit(solution)/shard_map/finish/pallas_call | solution.py:553
  239.7 3.6 %collective-permute-done.47 = f32[1,1664]{1,0:T(1,128)S(1)} collective-permute-done((f32[1,1664]{1,0:T(1,128)S(1)}, f32[1,1664]{1,0:T(1,128)S(1)}, u32[]{:S(2)}, u32[]{:S(2)}) %collective-permute-start.47) | collective-permute-done | bytes 6688 | tf_op jit(solution)/shard_map/ppermute | solution.py:31
  248.6 4.4 %adam.1 = (f32[1,1]{1,0:T(1,128)}, f32[3,96,192]{2,1,0:T(8,128)}, f32[3,96,192]{2,1,0:T(8,128)}, f32[3,96,192]{2,1,0:T(8,128)}, f32[192,96]{1,0:T(8,128)}, /*ind...) custom-call(s32[1]{0:T(128)} %bitcast.19.refs_0_, ...), custom_call_target="tpu_custom_call" | custom-call | tf_op jit(solution)/shard_map/adam/pallas_call | solution.py:637
  (290 shorter events, 103.6 us)
Async XLA Ops:
  22.6 18.3 %collective-permute-start.7 = (bf16[384,768]{1,0:T(8,128)(2,1)S(1)}, bf16[384,768]{1,0:T(8,128)(2,1)S(1)}, u32[]{:S(2)}, u32[]{:S(2)}) collective-permute-start(bf16[384,768]{1,0:T(8,128)(2,1)S(1)} %pad_maximum_fusion.6.qka_ref.voa_ref.att_ref), channel_id=1, source_target_pairs={{0,4},{4,0},{8,12},{12,8},{16,20},{20,16},{24,28},{28,24},{1,5},{5... | collective-permute-start | bytes 1769480 | tf_op jit(solution)/shard_map/ppermute | solution.py:31
  24.0 16.9 %collective-permute-start.8 = (bf16[384,768]{1,0:T(8,128)(2,1)S(1)}, bf16[384,768]{1,0:T(8,128)(2,1)S(1)}, u32[]{:S(2)}, u32[]{:S(2)}) collective-permute-start(bf16[384,768]{1,0:T(8,128)(2,1)S(1)} %pad_maximum_fusion.6.qka_ref.voa_ref.att_ref), channel_id=1, source_target_pairs={{0,2},{1,3},{2,0},{3,1},{4,6},{5,7},{6,4},{7,5},{8,10},{9,11},{10,... | collective-permute-start | bytes 1769480 | tf_op jit(solution)/shard_map/ppermute | solution.py:31
  25.6 15.2 %collective-permute-start.9 = (bf16[96,1280]{1,0:T(8,128)(2,1)S(1)}, bf16[96,1280]{1,0:T(8,128)(2,1)S(1)}, u32[]{:S(2)}, u32[]{:S(2)}) collective-permute-start(bf16[96,1280]{1,0:T(8,128)(2,1)S(1)} %pad_maximum_fusion.10), channel_id=1, source_target_pairs={{0,16},{4,20},{8,24},{12,28},{16,0},{20,4},{24,8},{28,12},{1,17},{... | collective-permute-start | bytes 737288 | tf_op jit(solution)/shard_map/ppermute | solution.py:31
  40.9 13.0 %collective-permute-start.13 = (bf16[192,1280]{1,0:T(8,128)(2,1)S(1)}, bf16[192,1280]{1,0:T(8,128)(2,1)S(1)}, u32[]{:S(2)}, u32[]{:S(2)}) collective-permute-start(bf16[192,1280]{1,0:T(8,128)(2,1)S(1)} %pad_maximum_fusion.7), channel_id=1, source_target_pairs={{0,8},{4,12},{8,0},{12,4},{16,24},{20,28},{24,16},{28,20},{1,9},{5... | collective-permute-start | bytes 1474568 | tf_op jit(solution)/shard_map/ppermute | solution.py:31
  54.1 22.7 %collective-permute-start.15 = (bf16[384,1280]{1,0:T(8,128)(2,1)S(1)}, bf16[384,1280]{1,0:T(8,128)(2,1)S(1)}, u32[]{:S(2)}, u32[]{:S(2)}) collective-permute-start(bf16[384,1280]{1,0:T(8,128)(2,1)S(1)} %pad_maximum_fusion.4.own_ref.low_own_ref), channel_id=1, source_target_pairs={{0,4},{4,0},{8,12},{12,8},{16,20},{20,16},{24,28},{28,24},{1,5},{5... | collective-permute-start | bytes 2949128 | tf_op jit(solution)/shard_map/ppermute | solution.py:31
  55.4 22.3 %collective-permute-start.16 = (bf16[384,1280]{1,0:T(8,128)(2,1)S(1)}, bf16[384,1280]{1,0:T(8,128)(2,1)S(1)}, u32[]{:S(2)}, u32[]{:S(2)}) collective-permute-start(bf16[384,1280]{1,0:T(8,128)(2,1)S(1)} %pad_maximum_fusion.4.own_ref.low_own_ref), channel_id=1, source_target_pairs={{0,2},{1,3},{2,0},{3,1},{4,6},{5,7},{6,4},{7,5},{8,10},{9,11},{10,... | collective-permute-start | bytes 2949128 | tf_op jit(solution)/shard_map/ppermute | solution.py:31
  55.9 16.1 %collective-permute-start.17 = (bf16[4,1,96,256]{3,2,0,1:T(8,128)(2,1)S(1)}, bf16[4,1,96,256]{3,2,0,1:T(8,128)(2,1)S(1)}, u32[]{:S(2)}, u32[]{:S(2)}) collective-permute-start(bf16[4,1,96,256]{3,2,0,1:T(8,128)(2,1)S(1)} %maximum_bitcast_fusion), channel_id=1, source_target_pairs={{0,16},{4,20},{8,24},{12,28},{16,0},{20,4},{24,8},{28,12},{1,17},{... | collective-permute-start | bytes 589832 | tf_op jit(solution)/shard_map/ppermute | solution.py:31
  77.7 16.3 %collective-permute-start.19 = (bf16[512,768]{1,0:T(8,128)(2,1)}, bf16[512,768]{1,0:T(8,128)(2,1)}, u32[]{:S(2)}, u32[]{:S(2)}) collective-permute-start(bf16[512,768]{1,0:T(8,128)(2,1)} %get-tuple-element.196), channel_id=1, source_target_pairs={{0,1},{1,0},{2,3},{3,2},{4,5},{5,4},{6,7},{7,6},{8,9},{9,8},{10,11... | collective-permute-start | bytes 2359304 | tf_op jit(solution)/shard_map/ppermute | solution.py:31
  78.2 13.5 %collective-permute-start.20 = (bf16[4,2,96,256]{3,2,0,1:T(8,128)(2,1)S(1)}, bf16[4,2,96,256]{3,2,0,1:T(8,128)(2,1)}, u32[]{:S(2)}, u32[]{:S(2)}) collective-permute-start(bf16[4,2,96,256]{3,2,0,1:T(8,128)(2,1)S(1)} %pad_maximum_fusion.8), channel_id=1, source_target_pairs={{0,8},{4,12},{8,0},{12,4},{16,24},{20,28},{24,16},{28,20},{1,9},{5... | collective-permute-start | bytes 1179656 | tf_op jit(solution)/shard_map/ppermute | solution.py:31
  80.1 16.6 %collective-permute-start.22 = (bf16[384,768]{1,0:T(8,128)(2,1)}, bf16[384,768]{1,0:T(8,128)(2,1)}, u32[]{:S(2)}, u32[]{:S(2)}) collective-permute-start(bf16[384,768]{1,0:T(8,128)(2,1)} %slice.156), channel_id=1, source_target_pairs={{0,4},{4,0},{8,12},{12,8},{16,20},{20,16},{24,28},{28,24},{1,5},{5... | collective-permute-start | bytes 1769480 | tf_op jit(solution)/shard_map/ppermute | solution.py:31
  82.2 14.6 %collective-permute-start.21 = (bf16[384,512]{1,0:T(8,128)(2,1)S(1)}, bf16[384,512]{1,0:T(8,128)(2,1)S(1)}, u32[]{:S(2)}, u32[]{:S(2)}) collective-permute-start(bf16[384,512]{1,0:T(8,128)(2,1)S(1)} %slice.155), channel_id=1, source_target_pairs={{0,2},{1,3},{2,0},{3,1},{4,6},{5,7},{6,4},{7,5},{8,10},{9,11},{10,... | collective-permute-start | bytes 1179656 | tf_op jit(solution)/shard_map/ppermute | solution.py:31
  115.9 21.1 %collective-permute-start.26 = (bf16[768,512]{1,0:T(8,128)(2,1)S(1)}, bf16[768,512]{1,0:T(8,128)(2,1)S(1)}, u32[]{:S(2)}, u32[]{:S(2)}) collective-permute-start(bf16[768,512]{1,0:T(8,128)(2,1)S(1)} %convolution_convert_fusion.2), channel_id=1, source_target_pairs={{0,2},{1,3},{2,0},{3,1},{4,6},{5,7},{6,4},{7,5},{8,10},{9,11},{10,... | collective-permute-start | bytes 2359304 | tf_op jit(solution)/shard_map/ppermute | solution.py:31
  125.0 30.5 %collective-permute-start.28 = (bf16[384,1024]{1,0:T(8,128)(2,1)S(1)}, bf16[384,1024]{1,0:T(8,128)(2,1)S(1)}, u32[]{:S(2)}, u32[]{:S(2)}) collective-permute-start(bf16[384,1024]{1,0:T(8,128)(2,1)S(1)} %convolution_convert_fusion.6), channel_id=1, source_target_pairs={{0,4},{4,0},{8,12},{12,8},{16,20},{20,16},{24,28},{28,24},{1,5},{5... | collective-permute-start | bytes 2359304 | tf_op jit(solution)/shard_map/ppermute | solution.py:31
  133.9 28.4 %collective-permute-start.27 = (bf16[384,1024]{1,0:T(8,128)(2,1)S(1)}, bf16[384,1024]{1,0:T(8,128)(2,1)S(1)}, u32[]{:S(2)}, u32[]{:S(2)}) collective-permute-start(bf16[384,1024]{1,0:T(8,128)(2,1)S(1)} %convolution_convert_fusion.5), channel_id=1, source_target_pairs={{0,4},{4,0},{8,12},{12,8},{16,20},{20,16},{24,28},{28,24},{1,5},{5... | collective-permute-start | bytes 2359304 | tf_op jit(solution)/shard_map/ppermute | solution.py:31
  155.8 22.6 %collective-permute-start.29 = (bf16[384,512]{1,0:T(8,128)(2,1)S(1)}, bf16[384,512]{1,0:T(8,128)(2,1)S(1)}, u32[]{:S(2)}, u32[]{:S(2)}) collective-permute-start(bf16[384,512]{1,0:T(8,128)(2,1)S(1)} %slice.247), channel_id=1, source_target_pairs={{0,4},{4,0},{8,12},{12,8},{16,20},{20,16},{24,28},{28,24},{1,5},{5... | collective-permute-start | bytes 1179656 | tf_op jit(solution)/shard_map/ppermute | solution.py:31
  157.3 21.1 %collective-permute-start.31 = (bf16[384,512]{1,0:T(8,128)(2,1)S(1)}, bf16[384,512]{1,0:T(8,128)(2,1)S(1)}, u32[]{:S(2)}, u32[]{:S(2)}) collective-permute-start(bf16[384,512]{1,0:T(8,128)(2,1)S(1)} %slice.249), channel_id=1, source_target_pairs={{0,2},{1,3},{2,0},{3,1},{4,6},{5,7},{6,4},{7,5},{8,10},{9,11},{10,... | collective-permute-start | bytes 1179656 | tf_op jit(solution)/shard_map/ppermute | solution.py:31
  163.3 15.1 %collective-permute-start.30 = (bf16[384,384]{1,0:T(8,128)(2,1)S(1)}, bf16[384,384]{1,0:T(8,128)(2,1)S(1)}, u32[]{:S(2)}, u32[]{:S(2)}) collective-permute-start(bf16[384,384]{1,0:T(8,128)(2,1)S(1)} %copy-done.51), channel_id=1, source_target_pairs={{0,4},{4,0},{8,12},{12,8},{16,20},{20,16},{24,28},{28,24},{1,5},{5... | collective-permute-start | bytes 884744 | tf_op jit(solution)/shard_map/ppermute | solution.py:31
  164.3 21.8 %collective-permute-start.35 = (bf16[384,512]{1,0:T(8,128)(2,1)S(1)}, bf16[384,512]{1,0:T(8,128)(2,1)S(1)}, u32[]{:S(2)}, u32[]{:S(2)}) collective-permute-start(bf16[384,512]{1,0:T(8,128)(2,1)S(1)} %slice.248), channel_id=1, source_target_pairs={{0,2},{1,3},{2,0},{3,1},{4,6},{5,7},{6,4},{7,5},{8,10},{9,11},{10,... | collective-permute-start | bytes 1179656 | tf_op jit(solution)/shard_map/ppermute | solution.py:31
  165.4 25.0 %collective-permute-start.34 = (bf16[768,384]{1,0:T(8,128)(2,1)S(1)}, bf16[768,384]{1,0:T(8,128)(2,1)S(1)}, u32[]{:S(2)}, u32[]{:S(2)}) collective-permute-start(bf16[768,384]{1,0:T(8,128)(2,1)S(1)} %copy-done.50), channel_id=1, source_target_pairs={{0,2},{1,3},{2,0},{3,1},{4,6},{5,7},{6,4},{7,5},{8,10},{9,11},{10,... | collective-permute-start | bytes 1769480 | tf_op jit(solution)/shard_map/ppermute | solution.py:31
  179.6 18.9 %collective-permute-start.33 = (bf16[384,384]{1,0:T(8,128)(2,1)S(1)}, bf16[384,384]{1,0:T(8,128)(2,1)S(1)}, u32[]{:S(2)}, u32[]{:S(2)}) collective-permute-start(bf16[384,384]{1,0:T(8,128)(2,1)S(1)} %add_convert_fusion), channel_id=1, source_target_pairs={{0,2},{1,3},{2,0},{3,1},{4,6},{5,7},{6,4},{7,5},{8,10},{9,11},{10,... | collective-permute-start | bytes 884744 | tf_op jit(solution)/shard_map/ppermute | solution.py:31
  184.9 13.7 %collective-permute-start.32 = (bf16[384,384]{1,0:T(8,128)(2,1)}, bf16[384,384]{1,0:T(8,128)(2,1)S(1)}, u32[]{:S(2)}, u32[]{:S(2)}) collective-permute-start(bf16[384,384]{1,0:T(8,128)(2,1)} %get-tuple-element.256), channel_id=1, source_target_pairs={{0,4},{4,0},{8,12},{12,8},{16,20},{20,16},{24,28},{28,24},{1,5},{5... | collective-permute-start | bytes 884744 | tf_op jit(solution)/shard_map/ppermute | solution.py:31
  201.4 19.7 %collective-permute-start.43 = (bf16[512,768]{1,0:T(8,128)(2,1)S(1)}, bf16[512,768]{1,0:T(8,128)(2,1)S(1)}, u32[]{:S(2)}, u32[]{:S(2)}) collective-permute-start(bf16[512,768]{1,0:T(8,128)(2,1)S(1)} %constant_dynamic-slice_fusion), channel_id=1, source_target_pairs={{0,1},{1,0},{2,3},{3,2},{4,5},{5,4},{6,7},{7,6},{8,9},{9,8},{10,11... | collective-permute-start | bytes 2359304 | tf_op jit(solution)/shard_map/ppermute | solution.py:31
  201.5 16.2 %collective-permute-start.42 = (bf16[96,1024]{1,0:T(8,128)(2,1)S(1)}, bf16[96,1024]{1,0:T(8,128)(2,1)S(1)}, u32[]{:S(2)}, u32[]{:S(2)}) collective-permute-start(bf16[96,1024]{1,0:T(8,128)(2,1)S(1)} %slice.252), channel_id=1, source_target_pairs={{0,16},{4,20},{8,24},{12,28},{16,0},{20,4},{24,8},{28,12},{1,17},{... | collective-permute-start | bytes 589832 | tf_op jit(solution)/shard_map/ppermute | solution.py:31
  207.9 19.9 %collective-permute-start.41 = (bf16[96,768]{1,0:T(8,128)(2,1)S(1)}, bf16[96,768]{1,0:T(8,128)(2,1)S(1)}, u32[]{:S(2)}, u32[]{:S(2)}) collective-permute-start(bf16[96,768]{1,0:T(8,128)(2,1)S(1)} %slice.254), channel_id=1, source_target_pairs={{0,16},{4,20},{8,24},{12,28},{16,0},{20,4},{24,8},{28,12},{1,17},{... | collective-permute-start | bytes 442376 | tf_op jit(solution)/shard_map/ppermute | solution.py:31
  (78 other events, 904.0 us)

commit v3 on v2

--- a/solution.py
+++ b/solution.py
@@ -566,22 +566,30 @@
     )(core, grad_one, pinned(part_full), pinned(layer_output), theirs, mover)
 
 
-def last_kernel(kept_ref, received_ref, square_ref, sum_ref, total_ref):
+def last_kernel(
+    kept_ref, received_ref, late_ref, late_received_ref, early_ref, sum_ref, late_sum_ref, total_ref
+):
+    def squares(value):
+        return jnp.sum(jnp.sum(value * value, axis=0, keepdims=True), axis=1, keepdims=True)
+
     value = kept_ref[...] + received_ref[...].astype(FULL)
+    late = late_ref[...] + late_received_ref[...].astype(FULL)
     sum_ref[...] = value
-    total = jnp.sum(jnp.sum(value * value, axis=0, keepdims=True), axis=1, keepdims=True)
-    total_ref[...] = square_ref[...] + total
-
-
-def last_sum(kept, received, square):
+    late_sum_ref[...] = late
+    total = squares(value) + squares(late) + squares(early_ref[...])
+    total_ref[...] = jnp.broadcast_to(total, total_ref.shape)
+
+
+def last_sums(kept, received, late, late_received, early):
     vmem = pl.BlockSpec(memory_space=pltpu.VMEM)
     return pl.pallas_call(
         last_kernel,
-        in_specs=[vmem] * 3,
-        out_specs=[vmem] * 2,
-        out_shape=[jax.ShapeDtypeStruct(kept.shape, FULL), jax.ShapeDtypeStruct((1, 128), FULL)],
-        name="last_sum",
-    )(kept, received, square)
+        in_specs=[vmem] * 5,
+        out_specs=[vmem] * 3,
+        out_shape=[jax.ShapeDtypeStruct(a.shape, FULL) for a in (kept, late)]
+        + [jax.ShapeDtypeStruct((1, 128), FULL)],
+        name="last_sums",
+    )(kept, received, late, late_received, early)
 
 
 def adam_kernel(clip, rates, *refs):
@@ -779,7 +787,7 @@
     up_corner = swap(ffn_x[:, hid:], "wide", 1)
     flow = [(hid, LOW, True), (hid, LOW, True), (hid, LOW, False)]
     normed_one, inv_one, hidden_low, gate1, up1, act1, gu_own = by_rows(
-        enter_kernel, "enter", [pinned(inputs), attn_part, attn_other],
+        enter_kernel, "enter", [pinned(inputs), attn_part, pinned(attn_other)],
         [gains, (ffn, 2 * hid, 0), (ffn_y, 2 * hid, 0)],
         [(D, LOW, True), (1, FULL, True), low_d] + flow, kept=[(D, 2 * hid)],
     )
@@ -864,17 +872,15 @@
     vo_sum = add(vo_own, vo_x)
     vo_far = vo_sum[half:].astype(LOW)
     vo_y = swap(vo_far, "wide", 1)
+    late = jnp.concatenate([add(gate_sum[:, :hid], gate_x), add(up_sum[:, :hid], up_x)], axis=1)
+    dqk1, vo_sum, late, early = lax.optimization_barrier((dqk1, vo_sum, late, early))
     early_red = narrow_down(early, back[1:])
-    late = jnp.concatenate([add(gate_sum[:, :hid], gate_x), add(up_sum[:, :hid], up_x)], axis=1)
-    dqk1, vo_sum, late = lax.optimization_barrier((dqk1, vo_sum, late))
     late = narrow_down(late, back[:1])
     part_full, part_low = by_rows(
         input_kernel, "inputs", [dqk1, dv1, dqk2, dv2],
         [att, att_y, att_x, qk_corner, vo_corner], [full_d, low_d],
         scratch=[pltpu.VMEM((2, D, 3 * cols), LOW)],
     )
-    theirs = lax.dynamic_slice_in_dim(part_low, (1 - core) * rows, rows, axis=0)
-    theirs = swap(theirs, "narrow", 1)
     qk_sum = add(qk_near1, qk_y1)
     last = jnp.concatenate([add(qk_sum, qk_x), add(vo_sum[:half], vo_y)], axis=1)
     gain_grads = jnp.concatenate([gain_one_grad, gain_two_grad], axis=0)
@@ -882,21 +888,25 @@
     gain_rest = (gain_grads - gain_low.astype(FULL)).astype(LOW)
     gain_grads = nt(jnp.concatenate([gain_low, gain_rest], axis=0), mover)
     gain_grads = gain_grads[:2] + gain_grads[2:]
-    last, early_red, late, gain_grads = lax.optimization_barrier(
-        (last, early_red, late, gain_grads)
-    )
+    last, early_red, late, gain_grads, part_low = lax.optimization_barrier(
+        (last, early_red, late, gain_grads, part_low)
+    )
+    theirs = lax.dynamic_slice_in_dim(part_low, (1 - core) * rows, rows, axis=0)
+    theirs = swap(theirs, "narrow", 1)
     last = narrow_down(last, back[:1])
-    late_red = narrow_down(late, back[1:])
-    early_square = jnp.sum(early_red * early_red) + jnp.sum(late_red * late_red)
+    late = narrow_down(late, back[1:-1])
+    late_received = swap(late[block:].astype(LOW), "wide", back[-1])
     last = narrow_down(last, back[1:-1])
     received = swap(last[block:].astype(LOW), "wide", back[-1])
     input_grad, layer_output = finish(
         jnp.full((1,), core, jnp.int32), grad_one_low, part_full, layer_output, theirs, mover
     )
-    received, early_square, input_grad, layer_output = lax.optimization_barrier(
-        (received, early_square, input_grad, layer_output)
-    )
-    att_red, square = last_sum(last[:block], received, jnp.full((1, 128), early_square, FULL))
+    received, input_grad, layer_output = lax.optimization_barrier(
+        (received, input_grad, layer_output)
+    )
+    att_red, late_red, square = last_sums(
+        last[:block], received, late[:block], late_received, early_red
+    )
 
     square = square + swap(square, "narrow", 1)
     message = jnp.concatenate([gain_grads.reshape(1, 2 * D), square], axis=1)

time: 254 us -> 252 us (level)
  waiting for transfers between devices: 47.8 us -> 54.6 us
  starting transfers between devices: 57.3 us -> 53.1 us
    ppermute x49, waiting for transfers between devices: 47.8 us -> 54.6 us  [swap(): return lax.ppermute(value, axis, [(i, i ^ bit) for i in range(size)])]
    ppermute x49, starting transfers between devices: 57.3 us -> 53.1 us  [swap(): return lax.ppermute(value, axis, [(i, i ^ bit) for i in range(size)])]
    unnamed x108 -> x102, local copies, waits for them, and re-layouts: 7.09 us -> 5.18 us
  transfers between devices with their start and end apart: 49 -> 49, of which waited for: 17 -> 18; matrix products, arithmetic and copies ran while one was open for 10% -> 9% of each run, Pallas kernels for 35% -> 36%
where the time goes in v3:
time: 252 us; the launch traced here: 251 us
  Pallas kernels  110 us (44%)
  waiting for transfers between devices  54.6 us (22%)
  starting transfers between devices  53.1 us (21%)
  other arithmetic  12.5 us (5%)
  local copies, waits for them, and re-layouts  9.95 us (4%)
  matrix products  9.3 us (4%)
    ppermute x49, waiting for transfers between devices, swap(): return lax.ppermute(value, axis, [(i, i ^ bit) for i in range(size)])  54.6 us
    ppermute x49, starting transfers between devices, swap(): return lax.ppermute(value, axis, [(i, i ^ bit) for i in range(size)])  53.1 us
    pallas_call x8, Pallas kernels, by_rows(): pl.pallas_call(kernel, grid=(L // step,), in_specs=specs + list(held_spec...  48 us
    pallas_call x2, Pallas kernels, attend_backward(): pl.pallas_call(attend_back_kernel, grid=(heads,), in_specs=[by_head((1, L...  23.2 us
    pallas_call x2, Pallas kernels, attend_forward(): pl.pallas_call(attend_kernel, grid=(1,), in_specs=list(specs), out_specs=...  18.1 us
    pallas_call x2, Pallas kernels, heads_grad(): pl.pallas_call(heads_grad_kernel, grid=(D // 256,), in_specs=[split, spli...  8.26 us
    dot_general x6, matrix products, tn(): lax.dot_general(rows, grads, (((0,), (0,)), ((), ())), preferred_element_...  5.98 us
    pallas_call x1, Pallas kernels, finish(): pl.pallas_call(finish_kernel, grid_spec=pltpu.PrefetchScalarGridSpec(num_...  5.4 us
  transfers between devices with their start and end apart: 49, of which 18 were waited for; matrix products, arithmetic and copies ran while one was open for 9% of the time, Pallas kernels for 36%

profile of v3, /device:TPU:0, one launch (start us, length us, event | category | flops | bytes accessed | tf_op | source)
XLA Modules:
  0.0 251.0 jit_solution(5299817219328591878)
XLA Ops:
  2.9 4.1 %collective-permute-start = (bf16[96,768]{1,0:T(8,128)(2,1)S(1)}, bf16[96,768]{1,0:T(8,128)(2,1)S(1)}, u32[]{:S(2)}, u32[]{:S(2)}) collective-permute-start(bf16[96,768]{1,0:T(8,128)(2,1)S(1)} %pad_maximum_fusion.11), channel_id=1, source_target_pairs={{0,16},{4,20},{8,24},{12,28},{16,0},{20,4},{24,8},{28,12},{1,17},{... | collective-permute-start | bytes 442376 | tf_op jit(solution)/shard_map/ppermute | solution.py:31
  31.2 9.6 %collective-permute-done.9 = bf16[96,1280]{1,0:T(8,128)(2,1)S(1)} collective-permute-done((bf16[96,1280]{1,0:T(8,128)(2,1)S(1)}, bf16[96,1280]{1,0:T(8,128)(2,1)S(1)}, u32[]{:S(2)}, u32[]{:S(2)}) %collective-permute-start.9) | collective-permute-done | bytes 245792 | tf_op jit(solution)/shard_map/ppermute | solution.py:31
  44.4 9.2 %attend_forward.2 = (bf16[3,1024,64]{2,1,0:T(8,128)(2,1)}, bf16[3,1024,64]{2,1,0:T(8,128)(2,1)}, bf16[3,1024,64]{2,1,0:T(8,128)(2,1)}, bf16[1024,192]{1,0:T(8,128)(2,1)S(1)}, f32[3,1,1024]{2,1,0:T(1,128)}) custom-call(bf16[1024,768]{1,0:T(8,128)(2,1)S(1)} %pad_maximum_fusion.rows_ref, bf16[384,768]{1,0:T(8,128)(2,1)S(1)} %pad_maximum_fusion.6.qka_ref.voa_ref.att_ref, ...), custom_call_target="tpu_custom_call" | custom-call | flops 1000000 | bytes 10000 | tf_op jit(solution)/shard_map/attend_forward/pallas_call | solution.py:180
  55.9 3.4 %collective-permute-start.17 = (bf16[4,1,96,256]{3,2,0,1:T(8,128)(2,1)S(1)}, bf16[4,1,96,256]{3,2,0,1:T(8,128)(2,1)S(1)}, u32[]{:S(2)}, u32[]{:S(2)}) collective-permute-start(bf16[4,1,96,256]{3,2,0,1:T(8,128)(2,1)S(1)} %maximum_bitcast_fusion), channel_id=1, source_target_pairs={{0,16},{4,20},{8,24},{12,28},{16,0},{20,4},{24,8},{28,12},{1,17},{... | collective-permute-start | bytes 589832 | tf_op jit(solution)/shard_map/ppermute | solution.py:31
  59.4 9.0 %attend_forward.3 = (bf16[3,1024,64]{2,1,0:T(8,128)(2,1)}, bf16[3,1024,64]{2,1,0:T(8,128)(2,1)}, bf16[3,1024,64]{2,1,0:T(8,128)(2,1)}, bf16[1024,192]{1,0:T(8,128)(2,1)S(1)}, f32[3,1,1024]{2,1,0:T(1,128)}) custom-call(bf16[1024,768]{1,0:T(8,128)(2,1)S(1)} %pad_maximum_fusion.rows_ref, bf16[384,768]{1,0:T(8,128)(2,1)S(1)} %collective-permute-done.8.qka_ref.voa_ref.x_ref, ...), custom_call_target="tpu_custom_call" | custom-call | flops 1000000 | bytes 10000 | tf_op jit(solution)/shard_map/attend_forward/pallas_call | solution.py:180
  68.4 3.6 %project.1.mine_ref = bf16[1024,768]{1,0:T(8,128)(2,1)S(1)} custom-call(bf16[1024,192]{1,0:T(8,128)(2,1)S(1)} %get-tuple-element.177.one_ref.ctx_ref, bf16[1024,192]{1,0:T(8,128)(2,1)S(1)} %get-tuple-element.186.two_ref.ctx_ref, bf16[384,768]{1,0:T(8,128)(2,1)} %copy-done.2, bf16[384,768]{1,0:T(8,128)(2,1)} %copy-done.3, bf16[384,768]{1,0:T(8,128)(2,1)} %copy-done.4, ...), custom_call_target="tpu_custom_call" | custom-call | flops 1000000 | bytes 10000 | tf_op jit(solution)/shard_map/project/pallas_call | solution.py:303
  72.1 4.7 %collective-permute-done.15.y_ref.low_y_ref = bf16[384,1280]{1,0:T(8,128)(2,1)S(1)} collective-permute-done((bf16[384,1280]{1,0:T(8,128)(2,1)S(1)}, bf16[384,1280]{1,0:T(8,128)(2,1)S(1)}, u32[]{:S(2)}, u32[]{:S(2)}) %collective-permute-start.15) | collective-permute-done | bytes 983072 | tf_op jit(solution)/shard_map/ppermute | solution.py:31
  81.8 6.6 %enter.1 = (bf16[1024,768]{1,0:T(8,128)(2,1)}, f32[1024,1]{1,0:T(8,128)}, bf16[1024,768]{1,0:T(8,128)(2,1)S(1)}, bf16[1024,512]{1,0:T(8,128)(2,1)}, bf16[1024,51...) custom-call(bf16[1024,768]{1,0:T(8,128)(2,1)} %copy-done, ...), custom_call_target="tpu_custom_call" | custom-call | flops 1000000 | bytes 10000 | tf_op jit(solution)/shard_map/enter/pallas_call | solution.py:303
  95.4 8.5 %rest.1 = (bf16[1024,512]{1,0:T(8,128)(2,1)}, bf16[1024,512]{1,0:T(8,128)(2,1)}, bf16[1024,512]{1,0:T(8,128)(2,1)S(1)}, bf16[1024,768]{1,0:T(8,128)(2,1)S(1)}, b...) custom-call(bf16[1024,768]{1,0:T(8,128)(2,1)S(1)} %get-tuple-element.200.hidden_ref, ...), custom_call_target="tpu_custom_call" | custom-call | flops 1000000 | bytes 10000 | tf_op jit(solution)/shard_map/rest/pallas_call | solution.py:303
  104.9 3.5 %collective-permute-done.23.theirs_ref = bf16[1024,768]{1,0:T(8,128)(2,1)} collective-permute-done((bf16[1024,768]{1,0:T(8,128)(2,1)S(1)}, bf16[1024,768]{1,0:T(8,128)(2,1)}, u32[]{:S(2)}, u32[]{:S(2)}) %collective-permute-start.23) | collective-permute-done | bytes 1572896 | tf_op jit(solution)/shard_map/ppermute | solution.py:31
  108.5 5.1 %turn.1 = (bf16[1024,768]{1,0:T(8,128)(2,1)}, bf16[1024,768]{1,0:T(8,128)(2,1)S(1)}, f32[1,768]{1,0:T(1,128)S(1)}) custom-call(bf16[1024,768]{1,0:T(8,128)(2,1)} %get-tuple-element.192.normed_ref, bf16[1024,768]{1,0:T(8,128)(2,1)S(1)} %get-tuple-element.205.mine_ref, bf16[1024,768]{1,0:T(8,128)(2,1)} %collective-permute-done.23.theirs_ref, ...), custom_call_target="tpu_custom_call" | custom-call | flops 1000000 | bytes 10000 | tf_op jit(solution)/shard_map/turn/pallas_call | solution.py:303
  115.1 5.5 %back.1 = (bf16[1024,1024]{1,0:T(8,128)(2,1)S(1)}, bf16[1024,1024]{1,0:T(8,128)(2,1)S(1)}) custom-call(bf16[1024,768]{1,0:T(8,128)(2,1)S(1)} %get-tuple-element.208.low_ref.grad_two_ref, bf16[1024,512]{1,0:T(8,128)(2,1)} %get-tuple-element.209.gate1_ref, bf16[1024,512]{1,0:T(8,128)(2,1)} %get-tuple-element.210.up1_ref, ...), custom_call_target="tpu_custom_call" | custom-call | flops 1000000 | bytes 10000 | tf_op jit(solution)/shard_map/back/pallas_call | solution.py:303
  123.6 6.1 %mid.1 = (bf16[512,768]{1,0:T(8,128)(2,1)S(1)}, bf16[512,768]{1,0:T(8,128)(2,1)S(1)}) custom-call(bf16[1024,1024]{1,0:T(8,128)(2,1)S(1)} %get-tuple-element.216.gg_ref, bf16[1024,1024]{1,0:T(8,128)(2,1)S(1)} %get-tuple-element.215.ug_ref, bf16[768,1024]{1,0:T(8,128)(2,1)} %get-tuple-element.217.own_ref, bf16[768,1024]{1,0:T(8,128)(2,1)} %get-tuple-element.218.other_ref), custom_call_target="tpu_custom_call" | custom-call | flops 1000000 | bytes 10000 | tf_op jit(solution)/shard_map/mid/pallas_call | solution.py:303
  134.6 6.6 %leave.1 = (bf16[1024,768]{1,0:T(8,128)(2,1)S(1)}, bf16[1024,192]{1,0:T(8,128)(2,1)}, bf16[1024,192]{1,0:T(8,128)(2,1)}, f32[1,768]{1,0:T(1,128)S(1)}) custom-call(bf16[1024,768]{1,0:T(8,128)(2,1)S(1)} %get-tuple-element.208.low_ref.grad_two_ref, bf16[512,768]{1,0:T(8,128)(2,1)S(1)} %get-tuple-element.221.mine_top_ref, ...), custom_call_target="tpu_custom_call" | custom-call | flops 1000000 | bytes 10000 | tf_op jit(solution)/shard_map/leave/pallas_call | solution.py:303
  141.2 11.9 %attend_backward.2 = (bf16[1024,384]{1,0:T(8,128)(2,1)S(1)}, bf16[1024,192]{1,0:T(8,128)(2,1)S(1)}) custom-call(bf16[3,1024,64]{2,1,0:T(8,128)(2,1)} %get-tuple-element.234.q_ref, bf16[3,1024,64]{2,1,0:T(8,128)(2,1)} %get-tuple-element.235.k_ref, bf16[3,1024,64]{2,1,0:T(8,128)(2,1)} %get-tuple-element.236.v_ref, f32[3,1,1024]{2,1,0:T(1,128)} %get-tuple-element.237.lse_ref, ...), custom_call_target="tpu_custom_call" | custom-call | flops 1000000 | bytes 10000 | tf_op jit(solution)/shard_map/attend_backward/pallas_call | solution.py:251
  156.3 4.1 %heads_grad.2 = (bf16[384,384]{1,0:T(8,128)(2,1)}, bf16[384,384]{1,0:T(8,128)(2,1)}, bf16[768,384]{1,0:T(8,128)(2,1)}) custom-call(bf16[1024,768]{1,0:T(8,128)(2,1)S(1)} %copy-done.1, bf16[1024,768]{1,0:T(8,128)(2,1)S(1)} %get-tuple-element.226.grad_ref.one_ref, bf16[1024,384]{1,0:T(8,128)(2,1)S(1)} %get-tuple-element.244.qk_ref.qk2_ref, ...), custom_call_target="tpu_custom_call" | custom-call | flops 1000000 | bytes 10000 | tf_op jit(solution)/shard_map/heads_grad/pallas_call | solution.py:518
  163.9 11.4 %attend_backward.3 = (bf16[1024,384]{1,0:T(8,128)(2,1)S(1)}, bf16[1024,192]{1,0:T(8,128)(2,1)S(1)}) custom-call(bf16[3,1024,64]{2,1,0:T(8,128)(2,1)} %get-tuple-element.227.q_ref, bf16[3,1024,64]{2,1,0:T(8,128)(2,1)} %get-tuple-element.228.k_ref, bf16[3,1024,64]{2,1,0:T(8,128)(2,1)} %get-tuple-element.229.v_ref, f32[3,1,1024]{2,1,0:T(1,128)} %get-tuple-element.230.lse_ref, ...), custom_call_target="tpu_custom_call" | custom-call | flops 1000000 | bytes 10000 | tf_op jit(solution)/shard_map/attend_backward/pallas_call | solution.py:251
  178.0 4.2 %heads_grad.3 = (bf16[384,384]{1,0:T(8,128)(2,1)}, bf16[384,384]{1,0:T(8,128)(2,1)}, bf16[768,384]{1,0:T(8,128)(2,1)}) custom-call(bf16[1024,768]{1,0:T(8,128)(2,1)S(1)} %copy-done.1, bf16[1024,768]{1,0:T(8,128)(2,1)S(1)} %get-tuple-element.226.grad_ref.one_ref, bf16[1024,384]{1,0:T(8,128)(2,1)S(1)} %get-tuple-element.271.qk_ref.qk1_ref, ...), custom_call_target="tpu_custom_call" | custom-call | flops 1000000 | bytes 10000 | tf_op jit(solution)/shard_map/heads_grad/pallas_call | solution.py:518
  183.9 4.0 %collective-permute-done.34 = bf16[768,384]{1,0:T(8,128)(2,1)S(1)} collective-permute-done((bf16[768,384]{1,0:T(8,128)(2,1)S(1)}, bf16[768,384]{1,0:T(8,128)(2,1)S(1)}, u32[]{:S(2)}, u32[]{:S(2)}) %collective-permute-start.34) | collective-permute-done | bytes 589856 | tf_op jit(solution)/shard_map/ppermute | solution.py:31
  188.0 3.4 %collective-permute-start.38 = (bf16[96,512]{1,0:T(8,128)(2,1)S(1)}, bf16[96,512]{1,0:T(8,128)(2,1)S(1)}, u32[]{:S(2)}, u32[]{:S(2)}) collective-permute-start(bf16[96,512]{1,0:T(8,128)(2,1)S(1)} %slice.253), channel_id=1, source_target_pairs={{0,16},{4,20},{8,24},{12,28},{16,0},{20,4},{24,8},{28,12},{1,17},{... | collective-permute-start | bytes 294920 | tf_op jit(solution)/shard_map/ppermute | solution.py:31
  193.6 6.0 %inputs.1 = (f32[1024,768]{1,0:T(8,128)}, bf16[1024,768]{1,0:T(8,128)(2,1)S(1)}) custom-call(bf16[1024,384]{1,0:T(8,128)(2,1)S(1)} %get-tuple-element.271.qk_ref.qk1_ref, bf16[1024,192]{1,0:T(8,128)(2,1)S(1)} %get-tuple-element.256.v_ref.v1_ref, bf16[1024,384]{1,0:T(8,128)(2,1)S(1)} %get-tuple-element.244.qk_ref.qk2_ref, ...), custom_call_target="tpu_custom_call" | custom-call | flops 1000000 | bytes 10000 | tf_op jit(solution)/shard_map/inputs/pallas_call | solution.py:303
  203.0 12.1 %collective-permute-done.40 = bf16[192,768]{1,0:T(8,128)(2,1)S(1)} collective-permute-done((bf16[192,768]{1,0:T(8,128)(2,1)S(1)}, bf16[192,768]{1,0:T(8,128)(2,1)S(1)}, u32[]{:S(2)}, u32[]{:S(2)}) %collective-permute-start.40) | collective-permute-done | bytes 294944 | tf_op jit(solution)/shard_map/ppermute | solution.py:31
  218.4 5.4 %finish.1 = (f32[512,768]{1,0:T(8,128)}, bf16[512,768]{1,0:T(8,128)(2,1)}) custom-call(s32[1]{0:T(128)} %bitcast.18.core_ref, bf16[1024,768]{1,0:T(8,128)(2,1)} %copy-done.5, f32[1024,768]{1,0:T(8,128)} %get-tuple-element.274.full_ref, bf16[1024,768]{1,0:T(8,128)(2,1)} %get-tuple-element.275.out_ref, bf16[512,768]{1,0:T(8,128)(2,1)} %copy-done.39, ...), custom_call_target="tpu_custom_call" | custom-call | flops 1000000 | bytes 10000 | tf_op jit(solution)/shard_map/finish/pallas_call | solution.py:553
  246.4 4.4 %adam.1 = (f32[1,1]{1,0:T(1,128)}, f32[3,96,192]{2,1,0:T(8,128)}, f32[3,96,192]{2,1,0:T(8,128)}, f32[3,96,192]{2,1,0:T(8,128)}, f32[192,96]{1,0:T(8,128)}, /*ind...) custom-call(s32[1]{0:T(128)} %bitcast.19.refs_0_, ...), custom_call_target="tpu_custom_call" | custom-call | tf_op jit(solution)/shard_map/adam/pallas_call | solution.py:645
  (282 shorter events, 96.7 us)
Async XLA Ops:
  22.6 18.3 %collective-permute-start.7 = (bf16[384,768]{1,0:T(8,128)(2,1)S(1)}, bf16[384,768]{1,0:T(8,128)(2,1)S(1)}, u32[]{:S(2)}, u32[]{:S(2)}) collective-permute-start(bf16[384,768]{1,0:T(8,128)(2,1)S(1)} %pad_maximum_fusion.6.qka_ref.voa_ref.att_ref), channel_id=1, source_target_pairs={{0,4},{4,0},{8,12},{12,8},{16,20},{20,16},{24,28},{28,24},{1,5},{5... | collective-permute-start | bytes 1769480 | tf_op jit(solution)/shard_map/ppermute | solution.py:31
  24.0 16.9 %collective-permute-start.8 = (bf16[384,768]{1,0:T(8,128)(2,1)S(1)}, bf16[384,768]{1,0:T(8,128)(2,1)S(1)}, u32[]{:S(2)}, u32[]{:S(2)}) collective-permute-start(bf16[384,768]{1,0:T(8,128)(2,1)S(1)} %pad_maximum_fusion.6.qka_ref.voa_ref.att_ref), channel_id=1, source_target_pairs={{0,2},{1,3},{2,0},{3,1},{4,6},{5,7},{6,4},{7,5},{8,10},{9,11},{10,... | collective-permute-start | bytes 1769480 | tf_op jit(solution)/shard_map/ppermute | solution.py:31
  25.6 15.2 %collective-permute-start.9 = (bf16[96,1280]{1,0:T(8,128)(2,1)S(1)}, bf16[96,1280]{1,0:T(8,128)(2,1)S(1)}, u32[]{:S(2)}, u32[]{:S(2)}) collective-permute-start(bf16[96,1280]{1,0:T(8,128)(2,1)S(1)} %pad_maximum_fusion.10), channel_id=1, source_target_pairs={{0,16},{4,20},{8,24},{12,28},{16,0},{20,4},{24,8},{28,12},{1,17},{... | collective-permute-start | bytes 737288 | tf_op jit(solution)/shard_map/ppermute | solution.py:31
  40.9 13.0 %collective-permute-start.13 = (bf16[192,1280]{1,0:T(8,128)(2,1)S(1)}, bf16[192,1280]{1,0:T(8,128)(2,1)S(1)}, u32[]{:S(2)}, u32[]{:S(2)}) collective-permute-start(bf16[192,1280]{1,0:T(8,128)(2,1)S(1)} %pad_maximum_fusion.7), channel_id=1, source_target_pairs={{0,8},{4,12},{8,0},{12,4},{16,24},{20,28},{24,16},{28,20},{1,9},{5... | collective-permute-start | bytes 1474568 | tf_op jit(solution)/shard_map/ppermute | solution.py:31
  41.7 12.3 %collective-permute-start.11 = (bf16[384,384]{1,0:T(8,128)(2,1)S(1)}, bf16[384,384]{1,0:T(8,128)(2,1)S(1)}, u32[]{:S(2)}, u32[]{:S(2)}) collective-permute-start(bf16[384,384]{1,0:T(8,128)(2,1)S(1)} %slice.152), channel_id=1, source_target_pairs={{0,2},{1,3},{2,0},{3,1},{4,6},{5,7},{6,4},{7,5},{8,10},{9,11},{10,... | collective-permute-start | bytes 884744 | tf_op jit(solution)/shard_map/ppermute | solution.py:31
  54.1 22.7 %collective-permute-start.15 = (bf16[384,1280]{1,0:T(8,128)(2,1)S(1)}, bf16[384,1280]{1,0:T(8,128)(2,1)S(1)}, u32[]{:S(2)}, u32[]{:S(2)}) collective-permute-start(bf16[384,1280]{1,0:T(8,128)(2,1)S(1)} %pad_maximum_fusion.4.own_ref.low_own_ref), channel_id=1, source_target_pairs={{0,4},{4,0},{8,12},{12,8},{16,20},{20,16},{24,28},{28,24},{1,5},{5... | collective-permute-start | bytes 2949128 | tf_op jit(solution)/shard_map/ppermute | solution.py:31
  55.4 22.3 %collective-permute-start.16 = (bf16[384,1280]{1,0:T(8,128)(2,1)S(1)}, bf16[384,1280]{1,0:T(8,128)(2,1)S(1)}, u32[]{:S(2)}, u32[]{:S(2)}) collective-permute-start(bf16[384,1280]{1,0:T(8,128)(2,1)S(1)} %pad_maximum_fusion.4.own_ref.low_own_ref), channel_id=1, source_target_pairs={{0,2},{1,3},{2,0},{3,1},{4,6},{5,7},{6,4},{7,5},{8,10},{9,11},{10,... | collective-permute-start | bytes 2949128 | tf_op jit(solution)/shard_map/ppermute | solution.py:31
  55.9 16.1 %collective-permute-start.17 = (bf16[4,1,96,256]{3,2,0,1:T(8,128)(2,1)S(1)}, bf16[4,1,96,256]{3,2,0,1:T(8,128)(2,1)S(1)}, u32[]{:S(2)}, u32[]{:S(2)}) collective-permute-start(bf16[4,1,96,256]{3,2,0,1:T(8,128)(2,1)S(1)} %maximum_bitcast_fusion), channel_id=1, source_target_pairs={{0,16},{4,20},{8,24},{12,28},{16,0},{20,4},{24,8},{28,12},{1,17},{... | collective-permute-start | bytes 589832 | tf_op jit(solution)/shard_map/ppermute | solution.py:31
  77.7 13.7 %collective-permute-start.19 = (bf16[512,768]{1,0:T(8,128)(2,1)}, bf16[512,768]{1,0:T(8,128)(2,1)}, u32[]{:S(2)}, u32[]{:S(2)}) collective-permute-start(bf16[512,768]{1,0:T(8,128)(2,1)} %get-tuple-element.198), channel_id=1, source_target_pairs={{0,1},{1,0},{2,3},{3,2},{4,5},{5,4},{6,7},{7,6},{8,9},{9,8},{10,11... | collective-permute-start | bytes 2359304 | tf_op jit(solution)/shard_map/ppermute | solution.py:31
  80.1 15.3 %collective-permute-start.22 = (bf16[384,768]{1,0:T(8,128)(2,1)}, bf16[384,768]{1,0:T(8,128)(2,1)}, u32[]{:S(2)}, u32[]{:S(2)}) collective-permute-start(bf16[384,768]{1,0:T(8,128)(2,1)} %slice.156), channel_id=1, source_target_pairs={{0,4},{4,0},{8,12},{12,8},{16,20},{20,16},{24,28},{28,24},{1,5},{5... | collective-permute-start | bytes 1769480 | tf_op jit(solution)/shard_map/ppermute | solution.py:31
  81.2 12.9 %collective-permute-start.21 = (bf16[384,512]{1,0:T(8,128)(2,1)S(1)}, bf16[384,512]{1,0:T(8,128)(2,1)S(1)}, u32[]{:S(2)}, u32[]{:S(2)}) collective-permute-start(bf16[384,512]{1,0:T(8,128)(2,1)S(1)} %slice.155), channel_id=1, source_target_pairs={{0,2},{1,3},{2,0},{3,1},{4,6},{5,7},{6,4},{7,5},{8,10},{9,11},{10,... | collective-permute-start | bytes 1179656 | tf_op jit(solution)/shard_map/ppermute | solution.py:31
  114.5 20.0 %collective-permute-start.26 = (bf16[768,512]{1,0:T(8,128)(2,1)S(1)}, bf16[768,512]{1,0:T(8,128)(2,1)S(1)}, u32[]{:S(2)}, u32[]{:S(2)}) collective-permute-start(bf16[768,512]{1,0:T(8,128)(2,1)S(1)} %convolution_convert_fusion.2), channel_id=1, source_target_pairs={{0,2},{1,3},{2,0},{3,1},{4,6},{5,7},{6,4},{7,5},{8,10},{9,11},{10,... | collective-permute-start | bytes 2359304 | tf_op jit(solution)/shard_map/ppermute | solution.py:31
  122.6 30.4 %collective-permute-start.28 = (bf16[384,1024]{1,0:T(8,128)(2,1)S(1)}, bf16[384,1024]{1,0:T(8,128)(2,1)S(1)}, u32[]{:S(2)}, u32[]{:S(2)}) collective-permute-start(bf16[384,1024]{1,0:T(8,128)(2,1)S(1)} %convolution_convert_fusion.6), channel_id=1, source_target_pairs={{0,4},{4,0},{8,12},{12,8},{16,20},{20,16},{24,28},{28,24},{1,5},{5... | collective-permute-start | bytes 2359304 | tf_op jit(solution)/shard_map/ppermute | solution.py:31
  131.4 29.0 %collective-permute-start.27 = (bf16[384,1024]{1,0:T(8,128)(2,1)S(1)}, bf16[384,1024]{1,0:T(8,128)(2,1)S(1)}, u32[]{:S(2)}, u32[]{:S(2)}) collective-permute-start(bf16[384,1024]{1,0:T(8,128)(2,1)S(1)} %convolution_convert_fusion.5), channel_id=1, source_target_pairs={{0,4},{4,0},{8,12},{12,8},{16,20},{20,16},{24,28},{28,24},{1,5},{5... | collective-permute-start | bytes 2359304 | tf_op jit(solution)/shard_map/ppermute | solution.py:31
  153.3 22.4 %collective-permute-start.29 = (bf16[384,512]{1,0:T(8,128)(2,1)S(1)}, bf16[384,512]{1,0:T(8,128)(2,1)S(1)}, u32[]{:S(2)}, u32[]{:S(2)}) collective-permute-start(bf16[384,512]{1,0:T(8,128)(2,1)S(1)} %slice.245), channel_id=1, source_target_pairs={{0,4},{4,0},{8,12},{12,8},{16,20},{20,16},{24,28},{28,24},{1,5},{5... | collective-permute-start | bytes 1179656 | tf_op jit(solution)/shard_map/ppermute | solution.py:31
  154.7 21.1 %collective-permute-start.31 = (bf16[384,512]{1,0:T(8,128)(2,1)S(1)}, bf16[384,512]{1,0:T(8,128)(2,1)S(1)}, u32[]{:S(2)}, u32[]{:S(2)}) collective-permute-start(bf16[384,512]{1,0:T(8,128)(2,1)S(1)} %slice.247), channel_id=1, source_target_pairs={{0,2},{1,3},{2,0},{3,1},{4,6},{5,7},{6,4},{7,5},{8,10},{9,11},{10,... | collective-permute-start | bytes 1179656 | tf_op jit(solution)/shard_map/ppermute | solution.py:31
  160.4 15.4 %collective-permute-start.30 = (bf16[384,384]{1,0:T(8,128)(2,1)}, bf16[384,384]{1,0:T(8,128)(2,1)S(1)}, u32[]{:S(2)}, u32[]{:S(2)}) collective-permute-start(bf16[384,384]{1,0:T(8,128)(2,1)} %get-tuple-element.254), channel_id=1, source_target_pairs={{0,4},{4,0},{8,12},{12,8},{16,20},{20,16},{24,28},{28,24},{1,5},{5... | collective-permute-start | bytes 884744 | tf_op jit(solution)/shard_map/ppermute | solution.py:31
  161.8 21.7 %collective-permute-start.35 = (bf16[384,512]{1,0:T(8,128)(2,1)S(1)}, bf16[384,512]{1,0:T(8,128)(2,1)S(1)}, u32[]{:S(2)}, u32[]{:S(2)}) collective-permute-start(bf16[384,512]{1,0:T(8,128)(2,1)S(1)} %slice.246), channel_id=1, source_target_pairs={{0,2},{1,3},{2,0},{3,1},{4,6},{5,7},{6,4},{7,5},{8,10},{9,11},{10,... | collective-permute-start | bytes 1179656 | tf_op jit(solution)/shard_map/ppermute | solution.py:31
  162.9 25.0 %collective-permute-start.34 = (bf16[768,384]{1,0:T(8,128)(2,1)S(1)}, bf16[768,384]{1,0:T(8,128)(2,1)S(1)}, u32[]{:S(2)}, u32[]{:S(2)}) collective-permute-start(bf16[768,384]{1,0:T(8,128)(2,1)S(1)} %copy-done.48), channel_id=1, source_target_pairs={{0,2},{1,3},{2,0},{3,1},{4,6},{5,7},{6,4},{7,5},{8,10},{9,11},{10,... | collective-permute-start | bytes 1769480 | tf_op jit(solution)/shard_map/ppermute | solution.py:31
  177.0 23.3 %collective-permute-start.33 = (bf16[384,384]{1,0:T(8,128)(2,1)S(1)}, bf16[384,384]{1,0:T(8,128)(2,1)S(1)}, u32[]{:S(2)}, u32[]{:S(2)}) collective-permute-start(bf16[384,384]{1,0:T(8,128)(2,1)S(1)} %add_convert_fusion), channel_id=1, source_target_pairs={{0,2},{1,3},{2,0},{3,1},{4,6},{5,7},{6,4},{7,5},{8,10},{9,11},{10,... | collective-permute-start | bytes 884744 | tf_op jit(solution)/shard_map/ppermute | solution.py:31
  182.2 18.1 %collective-permute-start.32 = (bf16[384,384]{1,0:T(8,128)(2,1)}, bf16[384,384]{1,0:T(8,128)(2,1)S(1)}, u32[]{:S(2)}, u32[]{:S(2)}) collective-permute-start(bf16[384,384]{1,0:T(8,128)(2,1)} %get-tuple-element.258), channel_id=1, source_target_pairs={{0,4},{4,0},{8,12},{12,8},{16,20},{20,16},{24,28},{28,24},{1,5},{5... | collective-permute-start | bytes 884744 | tf_op jit(solution)/shard_map/ppermute | solution.py:31
  201.2 16.0 %collective-permute-start.42 = (bf16[512,768]{1,0:T(8,128)(2,1)S(1)}, bf16[512,768]{1,0:T(8,128)(2,1)S(1)}, u32[]{:S(2)}, u32[]{:S(2)}) collective-permute-start(bf16[512,768]{1,0:T(8,128)(2,1)S(1)} %constant_dynamic-slice_fusion), channel_id=1, source_target_pairs={{0,1},{1,0},{2,3},{3,2},{4,5},{5,4},{6,7},{7,6},{8,9},{9,8},{10,11... | collective-permute-start | bytes 2359304 | tf_op jit(solution)/shard_map/ppermute | solution.py:31
  201.4 13.7 %collective-permute-start.40 = (bf16[192,768]{1,0:T(8,128)(2,1)S(1)}, bf16[192,768]{1,0:T(8,128)(2,1)S(1)}, u32[]{:S(2)}, u32[]{:S(2)}) collective-permute-start(bf16[192,768]{1,0:T(8,128)(2,1)S(1)} %slice.248), channel_id=1, source_target_pairs={{0,8},{4,12},{8,0},{12,4},{16,24},{20,28},{24,16},{28,20},{1,9},{5... | collective-permute-start | bytes 884744 | tf_op jit(solution)/shard_map/ppermute | solution.py:31
  202.2 22.2 %collective-permute-start.43 = (bf16[96,1024]{1,0:T(8,128)(2,1)S(1)}, bf16[96,1024]{1,0:T(8,128)(2,1)S(1)}, u32[]{:S(2)}, u32[]{:S(2)}) collective-permute-start(bf16[96,1024]{1,0:T(8,128)(2,1)S(1)} %slice.250), channel_id=1, source_target_pairs={{0,16},{4,20},{8,24},{12,28},{16,0},{20,4},{24,8},{28,12},{1,17},{... | collective-permute-start | bytes 589832 | tf_op jit(solution)/shard_map/ppermute | solution.py:31
  (75 other events, 911.0 us)

commit v4 on v3

--- a/solution.py
+++ b/solution.py
@@ -146,6 +146,10 @@
 
 def pinned(array):
     return pltpu.with_memory_space_constraint(array, pltpu.HBM)
+
+
+def near_core(array):
+    return pltpu.with_memory_space_constraint(array, pltpu.VMEM)
 
 
 def whole(array):
@@ -563,7 +567,7 @@
         ],
         cost_estimate=SMALL,
         name="finish",
-    )(core, grad_one, pinned(part_full), pinned(layer_output), theirs, mover)
+    )(core, grad_one, pinned(part_full), pinned(layer_output), pinned(theirs), mover)
 
 
 def last_kernel(
@@ -572,8 +576,9 @@
     def squares(value):
         return jnp.sum(jnp.sum(value * value, axis=0, keepdims=True), axis=1, keepdims=True)
 
-    value = kept_ref[...] + received_ref[...].astype(FULL)
-    late = late_ref[...] + late_received_ref[...].astype(FULL)
+    block = received_ref.shape[0]
+    value = kept_ref[:block] + received_ref[...].astype(FULL)
+    late = late_ref[:block] + late_received_ref[...].astype(FULL)
     sum_ref[...] = value
     late_sum_ref[...] = late
     total = squares(value) + squares(late) + squares(early_ref[...])
@@ -586,10 +591,10 @@
         last_kernel,
         in_specs=[vmem] * 5,
         out_specs=[vmem] * 3,
-        out_shape=[jax.ShapeDtypeStruct(a.shape, FULL) for a in (kept, late)]
+        out_shape=[jax.ShapeDtypeStruct(a.shape, FULL) for a in (received, late_received)]
         + [jax.ShapeDtypeStruct((1, 128), FULL)],
         name="last_sums",
-    )(kept, received, late, late_received, early)
+    )(kept, near_core(received), late, near_core(late_received), early)
 
 
 def adam_kernel(clip, rates, *refs):
@@ -905,7 +910,7 @@
         (received, input_grad, layer_output)
     )
     att_red, late_red, square = last_sums(
-        last[:block], received, late[:block], late_received, early_red
+        last, received, late, late_received, early_red
     )
 
     square = square + swap(square, "narrow", 1)
@@ -926,7 +931,7 @@
             (FF ** (-0.5), WEIGHT_DECAY),
             (0.4, 0.0),
         ),
-        (message, received, att_red, late_red, early_red),
+        (message, near_core(received), att_red, late_red, early_red),
         (
             (attend_weight, attend_first, attend_second),
             (output_weight, output_first, output_second),

time: 252 us -> 250 us (level)
  waiting for transfers between devices: 54.6 us -> 58 us
  local copies, waits for them, and re-layouts: 9.95 us -> 6.83 us
    ppermute x49, waiting for transfers between devices: 54.6 us -> 58 us  [swap(): return lax.ppermute(value, axis, [(i, i ^ bit) for i in range(size)])]
    unnamed x102 -> x100, local copies, waits for them, and re-layouts: 5.18 us -> 4.23 us
where the time goes in v4:
time: 250 us; the launch traced here: 249 us
  Pallas kernels  110 us (44%)
  waiting for transfers between devices  58 us (23%)
  starting transfers between devices  51.1 us (20%)
  other arithmetic  12.5 us (5%)
  matrix products  9.3 us (4%)
  local copies, waits for them, and re-layouts  6.83 us (3%)
    ppermute x49, waiting for transfers between devices, swap(): return lax.ppermute(value, axis, [(i, i ^ bit) for i in range(size)])  58 us
    ppermute x49, starting transfers between devices, swap(): return lax.ppermute(value, axis, [(i, i ^ bit) for i in range(size)])  51.1 us
    pallas_call x8, Pallas kernels, by_rows(): pl.pallas_call(kernel, grid=(L // step,), in_specs=specs + list(held_spec...  48 us
    pallas_call x2, Pallas kernels, attend_backward(): pl.pallas_call(attend_back_kernel, grid=(heads,), in_specs=[by_head((1, L...  23.2 us
    pallas_call x2, Pallas kernels, attend_forward(): pl.pallas_call(attend_kernel, grid=(1,), in_specs=list(specs), out_specs=...  18.1 us
    pallas_call x2, Pallas kernels, heads_grad(): pl.pallas_call(heads_grad_kernel, grid=(D // 256,), in_specs=[split, spli...  8.26 us
    dot_general x6, matrix products, tn(): lax.dot_general(rows, grads, (((0,), (0,)), ((), ())), preferred_element_...  5.99 us
    pallas_call x1, Pallas kernels, finish(): pl.pallas_call(finish_kernel, grid_spec=pltpu.PrefetchScalarGridSpec(num_...  5.35 us
  transfers between devices with their start and end apart: 49, of which 18 were waited for; matrix products, arithmetic and copies ran while one was open for 9% of the time, Pallas kernels for 36%

profile of v4, /device:TPU:0, one launch (start us, length us, event | category | flops | bytes accessed | tf_op | source)
XLA Modules:
  0.0 249.3 jit_solution(4742878824568435004)
XLA Ops:
  2.9 4.1 %collective-permute-start = (bf16[96,768]{1,0:T(8,128)(2,1)S(1)}, bf16[96,768]{1,0:T(8,128)(2,1)S(1)}, u32[]{:S(2)}, u32[]{:S(2)}) collective-permute-start(bf16[96,768]{1,0:T(8,128)(2,1)S(1)} %pad_maximum_fusion.11), channel_id=1, source_target_pairs={{0,16},{4,20},{8,24},{12,28},{16,0},{20,4},{24,8},{28,12},{1,17},{... | collective-permute-start | bytes 442376 | tf_op jit(solution)/shard_map/ppermute | solution.py:31
  31.2 9.6 %collective-permute-done.9 = bf16[96,1280]{1,0:T(8,128)(2,1)S(1)} collective-permute-done((bf16[96,1280]{1,0:T(8,128)(2,1)S(1)}, bf16[96,1280]{1,0:T(8,128)(2,1)S(1)}, u32[]{:S(2)}, u32[]{:S(2)}) %collective-permute-start.9) | collective-permute-done | bytes 245792 | tf_op jit(solution)/shard_map/ppermute | solution.py:31
  44.4 9.2 %attend_forward.2 = (bf16[3,1024,64]{2,1,0:T(8,128)(2,1)}, bf16[3,1024,64]{2,1,0:T(8,128)(2,1)}, bf16[3,1024,64]{2,1,0:T(8,128)(2,1)}, bf16[1024,192]{1,0:T(8,128)(2,1)S(1)}, f32[3,1,1024]{2,1,0:T(1,128)}) custom-call(bf16[1024,768]{1,0:T(8,128)(2,1)S(1)} %pad_maximum_fusion.rows_ref, bf16[384,768]{1,0:T(8,128)(2,1)S(1)} %pad_maximum_fusion.6.qka_ref.voa_ref.att_ref, ...), custom_call_target="tpu_custom_call" | custom-call | flops 1000000 | bytes 10000 | tf_op jit(solution)/shard_map/attend_forward/pallas_call | solution.py:184
  59.4 9.0 %attend_forward.3 = (bf16[3,1024,64]{2,1,0:T(8,128)(2,1)}, bf16[3,1024,64]{2,1,0:T(8,128)(2,1)}, bf16[3,1024,64]{2,1,0:T(8,128)(2,1)}, bf16[1024,192]{1,0:T(8,128)(2,1)S(1)}, f32[3,1,1024]{2,1,0:T(1,128)}) custom-call(bf16[1024,768]{1,0:T(8,128)(2,1)S(1)} %pad_maximum_fusion.rows_ref, bf16[384,768]{1,0:T(8,128)(2,1)S(1)} %collective-permute-done.8.qka_ref.voa_ref.x_ref, ...), custom_call_target="tpu_custom_call" | custom-call | flops 1000000 | bytes 10000 | tf_op jit(solution)/shard_map/attend_forward/pallas_call | solution.py:184
  68.4 3.6 %project.1.mine_ref = bf16[1024,768]{1,0:T(8,128)(2,1)S(1)} custom-call(bf16[1024,192]{1,0:T(8,128)(2,1)S(1)} %get-tuple-element.177.one_ref.ctx_ref, bf16[1024,192]{1,0:T(8,128)(2,1)S(1)} %get-tuple-element.186.two_ref.ctx_ref, bf16[384,768]{1,0:T(8,128)(2,1)} %copy-done.2, bf16[384,768]{1,0:T(8,128)(2,1)} %copy-done.3, bf16[384,768]{1,0:T(8,128)(2,1)} %copy-done.4, ...), custom_call_target="tpu_custom_call" | custom-call | flops 1000000 | bytes 10000 | tf_op jit(solution)/shard_map/project/pallas_call | solution.py:307
  72.1 4.7 %collective-permute-done.15.y_ref.low_y_ref = bf16[384,1280]{1,0:T(8,128)(2,1)S(1)} collective-permute-done((bf16[384,1280]{1,0:T(8,128)(2,1)S(1)}, bf16[384,1280]{1,0:T(8,128)(2,1)S(1)}, u32[]{:S(2)}, u32[]{:S(2)}) %collective-permute-start.15) | collective-permute-done | bytes 983072 | tf_op jit(solution)/shard_map/ppermute | solution.py:31
  81.8 6.6 %enter.1 = (bf16[1024,768]{1,0:T(8,128)(2,1)}, f32[1024,1]{1,0:T(8,128)}, bf16[1024,768]{1,0:T(8,128)(2,1)S(1)}, bf16[1024,512]{1,0:T(8,128)(2,1)}, bf16[1024,51...) custom-call(bf16[1024,768]{1,0:T(8,128)(2,1)} %copy-done, ...), custom_call_target="tpu_custom_call" | custom-call | flops 1000000 | bytes 10000 | tf_op jit(solution)/shard_map/enter/pallas_call | solution.py:307
  95.4 8.5 %rest.1 = (bf16[1024,512]{1,0:T(8,128)(2,1)}, bf16[1024,512]{1,0:T(8,128)(2,1)}, bf16[1024,512]{1,0:T(8,128)(2,1)S(1)}, bf16[1024,768]{1,0:T(8,128)(2,1)S(1)}, b...) custom-call(bf16[1024,768]{1,0:T(8,128)(2,1)S(1)} %get-tuple-element.200.hidden_ref, ...), custom_call_target="tpu_custom_call" | custom-call | flops 1000000 | bytes 10000 | tf_op jit(solution)/shard_map/rest/pallas_call | solution.py:307
  104.9 3.5 %collective-permute-done.23.theirs_ref = bf16[1024,768]{1,0:T(8,128)(2,1)} collective-permute-done((bf16[1024,768]{1,0:T(8,128)(2,1)S(1)}, bf16[1024,768]{1,0:T(8,128)(2,1)}, u32[]{:S(2)}, u32[]{:S(2)}) %collective-permute-start.23) | collective-permute-done | bytes 1572896 | tf_op jit(solution)/shard_map/ppermute | solution.py:31
  108.5 5.1 %turn.1 = (bf16[1024,768]{1,0:T(8,128)(2,1)}, bf16[1024,768]{1,0:T(8,128)(2,1)S(1)}, f32[1,768]{1,0:T(1,128)S(1)}) custom-call(bf16[1024,768]{1,0:T(8,128)(2,1)} %get-tuple-element.192.normed_ref, bf16[1024,768]{1,0:T(8,128)(2,1)S(1)} %get-tuple-element.205.mine_ref, bf16[1024,768]{1,0:T(8,128)(2,1)} %collective-permute-done.23.theirs_ref, ...), custom_call_target="tpu_custom_call" | custom-call | flops 1000000 | bytes 10000 | tf_op jit(solution)/shard_map/turn/pallas_call | solution.py:307
  115.2 5.5 %back.1 = (bf16[1024,1024]{1,0:T(8,128)(2,1)S(1)}, bf16[1024,1024]{1,0:T(8,128)(2,1)S(1)}) custom-call(bf16[1024,768]{1,0:T(8,128)(2,1)S(1)} %get-tuple-element.208.low_ref.grad_two_ref, bf16[1024,512]{1,0:T(8,128)(2,1)} %get-tuple-element.209.gate1_ref, bf16[1024,512]{1,0:T(8,128)(2,1)} %get-tuple-element.210.up1_ref, ...), custom_call_target="tpu_custom_call" | custom-call | flops 1000000 | bytes 10000 | tf_op jit(solution)/shard_map/back/pallas_call | solution.py:307
  123.7 6.1 %mid.1 = (bf16[512,768]{1,0:T(8,128)(2,1)S(1)}, bf16[512,768]{1,0:T(8,128)(2,1)S(1)}) custom-call(bf16[1024,1024]{1,0:T(8,128)(2,1)S(1)} %get-tuple-element.216.gg_ref, bf16[1024,1024]{1,0:T(8,128)(2,1)S(1)} %get-tuple-element.215.ug_ref, bf16[768,1024]{1,0:T(8,128)(2,1)} %get-tuple-element.217.own_ref, bf16[768,1024]{1,0:T(8,128)(2,1)} %get-tuple-element.218.other_ref), custom_call_target="tpu_custom_call" | custom-call | flops 1000000 | bytes 10000 | tf_op jit(solution)/shard_map/mid/pallas_call | solution.py:307
  134.6 6.6 %leave.1 = (bf16[1024,768]{1,0:T(8,128)(2,1)S(1)}, bf16[1024,192]{1,0:T(8,128)(2,1)}, bf16[1024,192]{1,0:T(8,128)(2,1)}, f32[1,768]{1,0:T(1,128)S(1)}) custom-call(bf16[1024,768]{1,0:T(8,128)(2,1)S(1)} %get-tuple-element.208.low_ref.grad_two_ref, bf16[512,768]{1,0:T(8,128)(2,1)S(1)} %get-tuple-element.221.mine_top_ref, ...), custom_call_target="tpu_custom_call" | custom-call | flops 1000000 | bytes 10000 | tf_op jit(solution)/shard_map/leave/pallas_call | solution.py:307
  141.2 11.9 %attend_backward.2 = (bf16[1024,384]{1,0:T(8,128)(2,1)S(1)}, bf16[1024,192]{1,0:T(8,128)(2,1)S(1)}) custom-call(bf16[3,1024,64]{2,1,0:T(8,128)(2,1)} %get-tuple-element.234.q_ref, bf16[3,1024,64]{2,1,0:T(8,128)(2,1)} %get-tuple-element.235.k_ref, bf16[3,1024,64]{2,1,0:T(8,128)(2,1)} %get-tuple-element.236.v_ref, f32[3,1,1024]{2,1,0:T(1,128)} %get-tuple-element.237.lse_ref, ...), custom_call_target="tpu_custom_call" | custom-call | flops 1000000 | bytes 10000 | tf_op jit(solution)/shard_map/attend_backward/pallas_call | solution.py:255
  156.3 4.1 %heads_grad.2 = (bf16[384,384]{1,0:T(8,128)(2,1)}, bf16[384,384]{1,0:T(8,128)(2,1)}, bf16[768,384]{1,0:T(8,128)(2,1)}) custom-call(bf16[1024,768]{1,0:T(8,128)(2,1)S(1)} %copy-done.1, bf16[1024,768]{1,0:T(8,128)(2,1)S(1)} %get-tuple-element.226.grad_ref.one_ref, bf16[1024,384]{1,0:T(8,128)(2,1)S(1)} %get-tuple-element.244.qk_ref.qk2_ref, ...), custom_call_target="tpu_custom_call" | custom-call | flops 1000000 | bytes 10000 | tf_op jit(solution)/shard_map/heads_grad/pallas_call | solution.py:522
  163.9 11.4 %attend_backward.3 = (bf16[1024,384]{1,0:T(8,128)(2,1)S(1)}, bf16[1024,192]{1,0:T(8,128)(2,1)S(1)}) custom-call(bf16[3,1024,64]{2,1,0:T(8,128)(2,1)} %get-tuple-element.227.q_ref, bf16[3,1024,64]{2,1,0:T(8,128)(2,1)} %get-tuple-element.228.k_ref, bf16[3,1024,64]{2,1,0:T(8,128)(2,1)} %get-tuple-element.229.v_ref, f32[3,1,1024]{2,1,0:T(1,128)} %get-tuple-element.230.lse_ref, ...), custom_call_target="tpu_custom_call" | custom-call | flops 1000000 | bytes 10000 | tf_op jit(solution)/shard_map/attend_backward/pallas_call | solution.py:255
  178.0 4.2 %heads_grad.3 = (bf16[384,384]{1,0:T(8,128)(2,1)}, bf16[384,384]{1,0:T(8,128)(2,1)}, bf16[768,384]{1,0:T(8,128)(2,1)}) custom-call(bf16[1024,768]{1,0:T(8,128)(2,1)S(1)} %copy-done.1, bf16[1024,768]{1,0:T(8,128)(2,1)S(1)} %get-tuple-element.226.grad_ref.one_ref, bf16[1024,384]{1,0:T(8,128)(2,1)S(1)} %get-tuple-element.271.qk_ref.qk1_ref, ...), custom_call_target="tpu_custom_call" | custom-call | flops 1000000 | bytes 10000 | tf_op jit(solution)/shard_map/heads_grad/pallas_call | solution.py:522
  183.9 4.0 %collective-permute-done.34 = bf16[768,384]{1,0:T(8,128)(2,1)S(1)} collective-permute-done((bf16[768,384]{1,0:T(8,128)(2,1)S(1)}, bf16[768,384]{1,0:T(8,128)(2,1)S(1)}, u32[]{:S(2)}, u32[]{:S(2)}) %collective-permute-start.34) | collective-permute-done | bytes 589856 | tf_op jit(solution)/shard_map/ppermute | solution.py:31
  193.6 6.0 %inputs.1 = (f32[1024,768]{1,0:T(8,128)}, bf16[1024,768]{1,0:T(8,128)(2,1)S(1)}) custom-call(bf16[1024,384]{1,0:T(8,128)(2,1)S(1)} %get-tuple-element.271.qk_ref.qk1_ref, bf16[1024,192]{1,0:T(8,128)(2,1)S(1)} %get-tuple-element.256.v_ref.v1_ref, bf16[1024,384]{1,0:T(8,128)(2,1)S(1)} %get-tuple-element.244.qk_ref.qk2_ref, ...), custom_call_target="tpu_custom_call" | custom-call | flops 1000000 | bytes 10000 | tf_op jit(solution)/shard_map/inputs/pallas_call | solution.py:307
  203.0 12.1 %collective-permute-done.40 = bf16[192,768]{1,0:T(8,128)(2,1)S(1)} collective-permute-done((bf16[192,768]{1,0:T(8,128)(2,1)S(1)}, bf16[192,768]{1,0:T(8,128)(2,1)S(1)}, u32[]{:S(2)}, u32[]{:S(2)}) %collective-permute-start.40) | collective-permute-done | bytes 294944 | tf_op jit(solution)/shard_map/ppermute | solution.py:31
  216.3 5.3 %finish.1 = (f32[512,768]{1,0:T(8,128)}, bf16[512,768]{1,0:T(8,128)(2,1)}) custom-call(s32[1]{0:T(128)} %bitcast.18.core_ref, bf16[1024,768]{1,0:T(8,128)(2,1)} %copy-done.5, f32[1024,768]{1,0:T(8,128)} %get-tuple-element.274.full_ref, bf16[1024,768]{1,0:T(8,128)(2,1)} %get-tuple-element.275.out_ref, bf16[512,768]{1,0:T(8,128)(2,1)} %copy-done.41, ...), custom_call_target="tpu_custom_call" | custom-call | flops 1000000 | bytes 10000 | tf_op jit(solution)/shard_map/finish/pallas_call | solution.py:557
  235.4 3.6 %collective-permute-done.47 = f32[1,1664]{1,0:T(1,128)S(1)} collective-permute-done((f32[1,1664]{1,0:T(1,128)S(1)}, f32[1,1664]{1,0:T(1,128)S(1)}, u32[]{:S(2)}, u32[]{:S(2)}) %collective-permute-start.47) | collective-permute-done | bytes 6688 | tf_op jit(solution)/shard_map/ppermute | solution.py:31
  240.2 3.5 %collective-permute-done.48.refs_2_ = f32[1,1664]{1,0:T(1,128)S(1)} collective-permute-done((f32[1,1664]{1,0:T(1,128)S(1)}, f32[1,1664]{1,0:T(1,128)S(1)}, u32[]{:S(2)}, u32[]{:S(2)}) %collective-permute-start.48) | collective-permute-done | bytes 6688 | tf_op jit(solution)/shard_map/ppermute | solution.py:31
  244.8 4.4 %adam.1 = (f32[1,1]{1,0:T(1,128)}, f32[3,96,192]{2,1,0:T(8,128)}, f32[3,96,192]{2,1,0:T(8,128)}, f32[3,96,192]{2,1,0:T(8,128)}, f32[192,96]{1,0:T(8,128)}, /*ind...) custom-call(s32[1]{0:T(128)} %bitcast.19.refs_0_, ...), custom_call_target="tpu_custom_call" | custom-call | tf_op jit(solution)/shard_map/adam/pallas_call | solution.py:650
  (278 shorter events, 94.8 us)
Async XLA Ops:
  22.6 18.3 %collective-permute-start.7 = (bf16[384,768]{1,0:T(8,128)(2,1)S(1)}, bf16[384,768]{1,0:T(8,128)(2,1)S(1)}, u32[]{:S(2)}, u32[]{:S(2)}) collective-permute-start(bf16[384,768]{1,0:T(8,128)(2,1)S(1)} %pad_maximum_fusion.6.qka_ref.voa_ref.att_ref), channel_id=1, source_target_pairs={{0,4},{4,0},{8,12},{12,8},{16,20},{20,16},{24,28},{28,24},{1,5},{5... | collective-permute-start | bytes 1769480 | tf_op jit(solution)/shard_map/ppermute | solution.py:31
  24.0 16.9 %collective-permute-start.8 = (bf16[384,768]{1,0:T(8,128)(2,1)S(1)}, bf16[384,768]{1,0:T(8,128)(2,1)S(1)}, u32[]{:S(2)}, u32[]{:S(2)}) collective-permute-start(bf16[384,768]{1,0:T(8,128)(2,1)S(1)} %pad_maximum_fusion.6.qka_ref.voa_ref.att_ref), channel_id=1, source_target_pairs={{0,2},{1,3},{2,0},{3,1},{4,6},{5,7},{6,4},{7,5},{8,10},{9,11},{10,... | collective-permute-start | bytes 1769480 | tf_op jit(solution)/shard_map/ppermute | solution.py:31
  25.6 15.2 %collective-permute-start.9 = (bf16[96,1280]{1,0:T(8,128)(2,1)S(1)}, bf16[96,1280]{1,0:T(8,128)(2,1)S(1)}, u32[]{:S(2)}, u32[]{:S(2)}) collective-permute-start(bf16[96,1280]{1,0:T(8,128)(2,1)S(1)} %pad_maximum_fusion.10), channel_id=1, source_target_pairs={{0,16},{4,20},{8,24},{12,28},{16,0},{20,4},{24,8},{28,12},{1,17},{... | collective-permute-start | bytes 737288 | tf_op jit(solution)/shard_map/ppermute | solution.py:31
  40.9 13.0 %collective-permute-start.13 = (bf16[192,1280]{1,0:T(8,128)(2,1)S(1)}, bf16[192,1280]{1,0:T(8,128)(2,1)S(1)}, u32[]{:S(2)}, u32[]{:S(2)}) collective-permute-start(bf16[192,1280]{1,0:T(8,128)(2,1)S(1)} %pad_maximum_fusion.7), channel_id=1, source_target_pairs={{0,8},{4,12},{8,0},{12,4},{16,24},{20,28},{24,16},{28,20},{1,9},{5... | collective-permute-start | bytes 1474568 | tf_op jit(solution)/shard_map/ppermute | solution.py:31
  41.7 12.3 %collective-permute-start.11 = (bf16[384,384]{1,0:T(8,128)(2,1)S(1)}, bf16[384,384]{1,0:T(8,128)(2,1)S(1)}, u32[]{:S(2)}, u32[]{:S(2)}) collective-permute-start(bf16[384,384]{1,0:T(8,128)(2,1)S(1)} %slice.146), channel_id=1, source_target_pairs={{0,2},{1,3},{2,0},{3,1},{4,6},{5,7},{6,4},{7,5},{8,10},{9,11},{10,... | collective-permute-start | bytes 884744 | tf_op jit(solution)/shard_map/ppermute | solution.py:31
  54.1 22.7 %collective-permute-start.15 = (bf16[384,1280]{1,0:T(8,128)(2,1)S(1)}, bf16[384,1280]{1,0:T(8,128)(2,1)S(1)}, u32[]{:S(2)}, u32[]{:S(2)}) collective-permute-start(bf16[384,1280]{1,0:T(8,128)(2,1)S(1)} %pad_maximum_fusion.4.own_ref.low_own_ref), channel_id=1, source_target_pairs={{0,4},{4,0},{8,12},{12,8},{16,20},{20,16},{24,28},{28,24},{1,5},{5... | collective-permute-start | bytes 2949128 | tf_op jit(solution)/shard_map/ppermute | solution.py:31
  55.4 22.3 %collective-permute-start.16 = (bf16[384,1280]{1,0:T(8,128)(2,1)S(1)}, bf16[384,1280]{1,0:T(8,128)(2,1)S(1)}, u32[]{:S(2)}, u32[]{:S(2)}) collective-permute-start(bf16[384,1280]{1,0:T(8,128)(2,1)S(1)} %pad_maximum_fusion.4.own_ref.low_own_ref), channel_id=1, source_target_pairs={{0,2},{1,3},{2,0},{3,1},{4,6},{5,7},{6,4},{7,5},{8,10},{9,11},{10,... | collective-permute-start | bytes 2949128 | tf_op jit(solution)/shard_map/ppermute | solution.py:31
  55.9 16.1 %collective-permute-start.17 = (bf16[4,1,96,256]{3,2,0,1:T(8,128)(2,1)S(1)}, bf16[4,1,96,256]{3,2,0,1:T(8,128)(2,1)S(1)}, u32[]{:S(2)}, u32[]{:S(2)}) collective-permute-start(bf16[4,1,96,256]{3,2,0,1:T(8,128)(2,1)S(1)} %maximum_bitcast_fusion), channel_id=1, source_target_pairs={{0,16},{4,20},{8,24},{12,28},{16,0},{20,4},{24,8},{28,12},{1,17},{... | collective-permute-start | bytes 589832 | tf_op jit(solution)/shard_map/ppermute | solution.py:31
  77.7 13.7 %collective-permute-start.19 = (bf16[512,768]{1,0:T(8,128)(2,1)}, bf16[512,768]{1,0:T(8,128)(2,1)}, u32[]{:S(2)}, u32[]{:S(2)}) collective-permute-start(bf16[512,768]{1,0:T(8,128)(2,1)} %get-tuple-element.198), channel_id=1, source_target_pairs={{0,1},{1,0},{2,3},{3,2},{4,5},{5,4},{6,7},{7,6},{8,9},{9,8},{10,11... | collective-permute-start | bytes 2359304 | tf_op jit(solution)/shard_map/ppermute | solution.py:31
  80.1 15.3 %collective-permute-start.22 = (bf16[384,768]{1,0:T(8,128)(2,1)}, bf16[384,768]{1,0:T(8,128)(2,1)}, u32[]{:S(2)}, u32[]{:S(2)}) collective-permute-start(bf16[384,768]{1,0:T(8,128)(2,1)} %slice.150), channel_id=1, source_target_pairs={{0,4},{4,0},{8,12},{12,8},{16,20},{20,16},{24,28},{28,24},{1,5},{5... | collective-permute-start | bytes 1769480 | tf_op jit(solution)/shard_map/ppermute | solution.py:31
  81.2 12.9 %collective-permute-start.21 = (bf16[384,512]{1,0:T(8,128)(2,1)S(1)}, bf16[384,512]{1,0:T(8,128)(2,1)S(1)}, u32[]{:S(2)}, u32[]{:S(2)}) collective-permute-start(bf16[384,512]{1,0:T(8,128)(2,1)S(1)} %slice.149), channel_id=1, source_target_pairs={{0,2},{1,3},{2,0},{3,1},{4,6},{5,7},{6,4},{7,5},{8,10},{9,11},{10,... | collective-permute-start | bytes 1179656 | tf_op jit(solution)/shard_map/ppermute | solution.py:31
  114.6 20.0 %collective-permute-start.26 = (bf16[768,512]{1,0:T(8,128)(2,1)S(1)}, bf16[768,512]{1,0:T(8,128)(2,1)S(1)}, u32[]{:S(2)}, u32[]{:S(2)}) collective-permute-start(bf16[768,512]{1,0:T(8,128)(2,1)S(1)} %convolution_convert_fusion.2), channel_id=1, source_target_pairs={{0,2},{1,3},{2,0},{3,1},{4,6},{5,7},{6,4},{7,5},{8,10},{9,11},{10,... | collective-permute-start | bytes 2359304 | tf_op jit(solution)/shard_map/ppermute | solution.py:31
  122.7 30.4 %collective-permute-start.28 = (bf16[384,1024]{1,0:T(8,128)(2,1)S(1)}, bf16[384,1024]{1,0:T(8,128)(2,1)S(1)}, u32[]{:S(2)}, u32[]{:S(2)}) collective-permute-start(bf16[384,1024]{1,0:T(8,128)(2,1)S(1)} %convolution_convert_fusion.6), channel_id=1, source_target_pairs={{0,4},{4,0},{8,12},{12,8},{16,20},{20,16},{24,28},{28,24},{1,5},{5... | collective-permute-start | bytes 2359304 | tf_op jit(solution)/shard_map/ppermute | solution.py:31
  131.4 29.0 %collective-permute-start.27 = (bf16[384,1024]{1,0:T(8,128)(2,1)S(1)}, bf16[384,1024]{1,0:T(8,128)(2,1)S(1)}, u32[]{:S(2)}, u32[]{:S(2)}) collective-permute-start(bf16[384,1024]{1,0:T(8,128)(2,1)S(1)} %convolution_convert_fusion.5), channel_id=1, source_target_pairs={{0,4},{4,0},{8,12},{12,8},{16,20},{20,16},{24,28},{28,24},{1,5},{5... | collective-permute-start | bytes 2359304 | tf_op jit(solution)/shard_map/ppermute | solution.py:31
  153.4 22.4 %collective-permute-start.29 = (bf16[384,512]{1,0:T(8,128)(2,1)S(1)}, bf16[384,512]{1,0:T(8,128)(2,1)S(1)}, u32[]{:S(2)}, u32[]{:S(2)}) collective-permute-start(bf16[384,512]{1,0:T(8,128)(2,1)S(1)} %slice.236), channel_id=1, source_target_pairs={{0,4},{4,0},{8,12},{12,8},{16,20},{20,16},{24,28},{28,24},{1,5},{5... | collective-permute-start | bytes 1179656 | tf_op jit(solution)/shard_map/ppermute | solution.py:31
  154.7 21.0 %collective-permute-start.31 = (bf16[384,512]{1,0:T(8,128)(2,1)S(1)}, bf16[384,512]{1,0:T(8,128)(2,1)S(1)}, u32[]{:S(2)}, u32[]{:S(2)}) collective-permute-start(bf16[384,512]{1,0:T(8,128)(2,1)S(1)} %slice.238), channel_id=1, source_target_pairs={{0,2},{1,3},{2,0},{3,1},{4,6},{5,7},{6,4},{7,5},{8,10},{9,11},{10,... | collective-permute-start | bytes 1179656 | tf_op jit(solution)/shard_map/ppermute | solution.py:31
  160.4 15.4 %collective-permute-start.30 = (bf16[384,384]{1,0:T(8,128)(2,1)}, bf16[384,384]{1,0:T(8,128)(2,1)S(1)}, u32[]{:S(2)}, u32[]{:S(2)}) collective-permute-start(bf16[384,384]{1,0:T(8,128)(2,1)} %get-tuple-element.254), channel_id=1, source_target_pairs={{0,4},{4,0},{8,12},{12,8},{16,20},{20,16},{24,28},{28,24},{1,5},{5... | collective-permute-start | bytes 884744 | tf_op jit(solution)/shard_map/ppermute | solution.py:31
  161.8 21.7 %collective-permute-start.35 = (bf16[384,512]{1,0:T(8,128)(2,1)S(1)}, bf16[384,512]{1,0:T(8,128)(2,1)S(1)}, u32[]{:S(2)}, u32[]{:S(2)}) collective-permute-start(bf16[384,512]{1,0:T(8,128)(2,1)S(1)} %slice.237), channel_id=1, source_target_pairs={{0,2},{1,3},{2,0},{3,1},{4,6},{5,7},{6,4},{7,5},{8,10},{9,11},{10,... | collective-permute-start | bytes 1179656 | tf_op jit(solution)/shard_map/ppermute | solution.py:31
  162.9 25.0 %collective-permute-start.34 = (bf16[768,384]{1,0:T(8,128)(2,1)S(1)}, bf16[768,384]{1,0:T(8,128)(2,1)S(1)}, u32[]{:S(2)}, u32[]{:S(2)}) collective-permute-start(bf16[768,384]{1,0:T(8,128)(2,1)S(1)} %copy-done.47), channel_id=1, source_target_pairs={{0,2},{1,3},{2,0},{3,1},{4,6},{5,7},{6,4},{7,5},{8,10},{9,11},{10,... | collective-permute-start | bytes 1769480 | tf_op jit(solution)/shard_map/ppermute | solution.py:31
  177.0 23.3 %collective-permute-start.33 = (bf16[384,384]{1,0:T(8,128)(2,1)S(1)}, bf16[384,384]{1,0:T(8,128)(2,1)S(1)}, u32[]{:S(2)}, u32[]{:S(2)}) collective-permute-start(bf16[384,384]{1,0:T(8,128)(2,1)S(1)} %add_convert_fusion), channel_id=1, source_target_pairs={{0,2},{1,3},{2,0},{3,1},{4,6},{5,7},{6,4},{7,5},{8,10},{9,11},{10,... | collective-permute-start | bytes 884744 | tf_op jit(solution)/shard_map/ppermute | solution.py:31
  182.2 18.1 %collective-permute-start.32 = (bf16[384,384]{1,0:T(8,128)(2,1)}, bf16[384,384]{1,0:T(8,128)(2,1)S(1)}, u32[]{:S(2)}, u32[]{:S(2)}) collective-permute-start(bf16[384,384]{1,0:T(8,128)(2,1)} %get-tuple-element.258), channel_id=1, source_target_pairs={{0,4},{4,0},{8,12},{12,8},{16,20},{20,16},{24,28},{28,24},{1,5},{5... | collective-permute-start | bytes 884744 | tf_op jit(solution)/shard_map/ppermute | solution.py:31
  201.3 14.0 %collective-permute-start.42 = (bf16[512,768]{1,0:T(8,128)(2,1)S(1)}, bf16[512,768]{1,0:T(8,128)(2,1)S(1)}, u32[]{:S(2)}, u32[]{:S(2)}) collective-permute-start(bf16[512,768]{1,0:T(8,128)(2,1)S(1)} %constant_dynamic-slice_fusion), channel_id=1, source_target_pairs={{0,1},{1,0},{2,3},{3,2},{4,5},{5,4},{6,7},{7,6},{8,9},{9,8},{10,11... | collective-permute-start | bytes 2359304 | tf_op jit(solution)/shard_map/ppermute | solution.py:31
  201.4 13.7 %collective-permute-start.40 = (bf16[192,768]{1,0:T(8,128)(2,1)S(1)}, bf16[192,768]{1,0:T(8,128)(2,1)S(1)}, u32[]{:S(2)}, u32[]{:S(2)}) collective-permute-start(bf16[192,768]{1,0:T(8,128)(2,1)S(1)} %slice.239), channel_id=1, source_target_pairs={{0,8},{4,12},{8,0},{12,4},{16,24},{20,28},{24,16},{28,20},{1,9},{5... | collective-permute-start | bytes 884744 | tf_op jit(solution)/shard_map/ppermute | solution.py:31
  202.2 21.5 %collective-permute-start.43 = (bf16[96,1024]{1,0:T(8,128)(2,1)S(1)}, bf16[96,1024]{1,0:T(8,128)(2,1)S(1)}, u32[]{:S(2)}, u32[]{:S(2)}) collective-permute-start(bf16[96,1024]{1,0:T(8,128)(2,1)S(1)} %slice.241), channel_id=1, source_target_pairs={{0,16},{4,20},{8,24},{12,28},{16,0},{20,4},{24,8},{28,12},{1,17},{... | collective-permute-start | bytes 589832 | tf_op jit(solution)/shard_map/ppermute | solution.py:31
  (74 other events, 850.6 us)
